TPU v7x, 256 devices: a whole 4x4x8 slice. The times are simulated.
256 devices in a mesh: px: 8 (over y, core), py: 32 (over x, z).
Axes of the slice: x: 4, y: 4, z: 8, core: 2. Of those that a mesh axis runs over, the one named last changes fastest.
Arguments:
- source: float32 [256, 512, 256], P('px', 'py'), may hold values from -3.5 to 3.7
- density: float32 [256, 512, 256], P('px', 'py'), may hold values from 0.25 to 4
Outputs:
- pressure: float32 [256, 512, 256], P('px', 'py')
All inputs are finite; a program needn't handle non-finite values.
Results may differ from a plain program's by a relative error of at most 0.0001.
Values sent between devices are 32-bit elements; how exact they have to be, the bound alone decides.
No kernel may reach another device: no remote copies, remote signals or barrier semaphores. Data moves between devices by JAX's collectives and lax.ppermute only.
A program may use at most 128 MiB of HBM per device.

v0:
```python
import jax
import jax.numpy as jnp
from jax import lax
from jax.sharding import PartitionSpec as P

LEVELS = 4
COARSE = 8


RELAXATION = 0.8


def padded_2(x, sides, width):
    edges = {}
    for axis, dim in sides:
        peers, length = (lax.axis_size(axis), x.shape[dim])
        up = [(i, (i + 1) % peers) for i in range(peers - 1)]
        last = lax.slice_in_dim(x, length - width, length, axis=dim)
        initial = lax.slice_in_dim(x, 0, width, axis=dim)
        edges[dim] = (
            lax.ppermute(last, axis, up),
            lax.ppermute(initial, axis, [(b, a) for a, b in up]),
        )
    done = []
    for _, dim in sides:
        low, high = edges[dim]
        around = [(width, width) if d in done else (0, 0) for d in range(x.ndim)]
        x = jnp.concatenate([jnp.pad(low, around), x, jnp.pad(high, around)], axis=dim)
        done.append(dim)
    return x


def extended(block, sides, width):
    for axis, dim in sides:
        count = lax.axis_size(axis)
        forward = [(i, i + 1) for i in range(count - 1)]
        backward = [(target, source) for source, target in forward]
        low = lax.ppermute(
            lax.slice_in_dim(block, block.shape[dim] - width, None, axis=dim), axis, forward
        )
        high = lax.ppermute(lax.slice_in_dim(block, 0, width, axis=dim), axis, backward)
        block = jnp.concatenate([low, block, high], axis=dim)
    return block


def neighbours(padded):
    return (
        padded[:-2, 1:-1, 1:-1],
        padded[2:, 1:-1, 1:-1],
        padded[1:-1, :-2, 1:-1],
        padded[1:-1, 2:, 1:-1],
        padded[1:-1, 1:-1, :-2],
        padded[1:-1, 1:-1, 2:],
    )


def centre(padded):
    return padded[1:-1, 1:-1, 1:-1]


def operate(field_pad, mobility_pad, factor):
    full_pad = jnp.pad(field_pad, ((0, 0), (0, 0), (1, 1)))
    centre_value = centre(full_pad)
    centre_mobility = centre(mobility_pad)
    summed = jnp.zeros(centre_value.shape, jnp.float32)
    for side_value, side_mobility in zip(neighbours(full_pad), neighbours(mobility_pad)):
        summed = summed + 0.5 * (centre_mobility + side_mobility) * (centre_value - side_value)
    return factor * summed


def diagonal(mobility_pad, factor):
    centre_mobility = centre(mobility_pad)
    summed = jnp.zeros(centre_mobility.shape, jnp.float32)
    for side_mobility in neighbours(mobility_pad):
        summed = summed + 0.5 * (centre_mobility + side_mobility)
    return factor * summed


def restrict(values):
    return jnp.mean(
        values.reshape(values.shape[0] // 2, 2, values.shape[1] // 2, 2, values.shape[2] // 2, 2),
        axis=(1, 3, 5),
    )


def prolong(values):
    expanded = jnp.broadcast_to(
        values[:, None, :, None, :, None],
        (values.shape[0], 2, values.shape[1], 2, values.shape[2], 2),
    )
    return expanded.reshape(values.shape[0] * 2, values.shape[1] * 2, values.shape[2] * 2)


def face_halo(values):
    return padded_2(values, (("px", 0), ("py", 1)), 1)


def rim_halo(values):
    return extended(values, (("px", 0), ("py", 1)), 2)


def trim_circle(values, layers):
    return values[layers : values.shape[0] - layers, layers : values.shape[1] - layers]


def fix_edges(padded, layers):
    at_start = lax.axis_index("px") == 0
    at_end = lax.axis_index("px") == lax.axis_size("px") - 1
    lower = jnp.where(
        at_start,
        jnp.broadcast_to(padded[layers : layers + 1], padded[:layers].shape),
        padded[:layers],
    )
    upper = jnp.where(
        at_end,
        jnp.broadcast_to(padded[-layers - 1 : -layers], padded[-layers:].shape),
        padded[-layers:],
    )
    padded = jnp.concatenate([lower, padded[layers:-layers], upper], 0)
    at_start = lax.axis_index("py") == 0
    at_end = lax.axis_index("py") == lax.axis_size("py") - 1
    lower = jnp.where(
        at_start,
        jnp.broadcast_to(padded[:, layers : layers + 1], padded[:, :layers].shape),
        padded[:, :layers],
    )
    upper = jnp.where(
        at_end,
        jnp.broadcast_to(padded[:, -layers - 1 : -layers], padded[:, -layers:].shape),
        padded[:, -layers:],
    )
    padded = jnp.concatenate([lower, padded[:, layers:-layers], upper], 1)
    return jnp.pad(padded, ((0, 0), (0, 0), (1, 1)), mode="edge")


def inside_mask(extent, layers):
    block_rows = extent[0] - 2 * layers
    block_cols = extent[1] - 2 * layers
    global_rows = lax.axis_index("px") * block_rows - layers + lax.iota(jnp.int32, extent[0])
    global_cols = lax.axis_index("py") * block_cols - layers + lax.iota(jnp.int32, extent[1])
    valid_rows = (global_rows >= 0) & (global_rows < block_rows * lax.axis_size("px"))
    valid_cols = (global_cols >= 0) & (global_cols < block_cols * lax.axis_size("py"))
    return valid_rows[:, None, None] & valid_cols[None, :, None]


def jacobi_sweep(values, rhs_value, mobility_pad, inverse, factor):
    return (
        values
        + RELAXATION * (rhs_value - operate(face_halo(values), mobility_pad, factor)) * inverse
    )


def per_device(source, density):
    mobilities = [1.0 / density]
    for level_index in range(1, LEVELS):
        mobilities.append(restrict(mobilities[-1]))
    factors = [0.25**level_index for level_index in range(LEVELS)]
    sources = []
    smoothed = []
    rhs_value = source
    pads = [
        fix_edges(extended(mobilities[level_index], (("px", 0), ("py", 1)), 3), 3)
        for level_index in range(LEVELS - 1)
    ]
    inverses = [
        1.0 / diagonal(padded, factors[level_index]) for level_index, padded in enumerate(pads)
    ]
    for level_index in range(LEVELS - 1):
        factor = factors[level_index]
        padded = pads[level_index]
        inverse = inverses[level_index]
        rhs_wide = rim_halo(rhs_value)
        first_pass = RELAXATION * rhs_wide * inverse
        second = trim_circle(first_pass, 1) + RELAXATION * (
            trim_circle(rhs_wide, 1) - operate(first_pass, trim_circle(padded, 1), factor)
        ) * trim_circle(inverse, 1)
        second = jnp.where(inside_mask(second.shape, 1), second, 0.0)
        residual = trim_circle(rhs_wide, 2) - operate(second, trim_circle(padded, 2), factor)
        sources.append(rhs_wide)
        smoothed.append(trim_circle(second, 1))
        rhs_value = restrict(residual)
    coarse_mobility = mobilities[LEVELS - 1]
    coarse_factor = factors[LEVELS - 1]
    coarse_pad = fix_edges(face_halo(coarse_mobility), 1)
    coarse_inverse = 1.0 / diagonal(coarse_pad, coarse_factor)
    values = RELAXATION * rhs_value * coarse_inverse
    for sweep_index in range(COARSE - 1):
        values = jacobi_sweep(values, rhs_value, coarse_pad, coarse_inverse, coarse_factor)
    for level_index in reversed(range(LEVELS - 1)):
        factor = factors[level_index]
        padded = pads[level_index]
        inverse = inverses[level_index]
        rhs_wide = sources[level_index]
        values = smoothed[level_index] + prolong(values)
        wide_values = rim_halo(values)
        first_pass = trim_circle(wide_values, 1) + RELAXATION * (
            trim_circle(rhs_wide, 1) - operate(wide_values, trim_circle(padded, 1), factor)
        ) * trim_circle(inverse, 1)
        first_pass = jnp.where(inside_mask(first_pass.shape, 1), first_pass, 0.0)
        values = trim_circle(first_pass, 1) + RELAXATION * (
            trim_circle(rhs_wide, 2) - operate(first_pass, trim_circle(padded, 2), factor)
        ) * trim_circle(inverse, 2)
    return values


def solution(mesh):
    in_specs = (P("px", "py", None), P("px", "py", None))
    out_specs = P("px", "py", None)
    return jax.shard_map(
        per_device, mesh=mesh, in_specs=in_specs, out_specs=out_specs, check_vma=False
    )
```

profile of v0, /device:TPU:10, one launch (start us, length us, event | category | flops | bytes accessed | tf_op | source)
XLA Modules:
  0.0 468.1 jit_solution(6154971809719221029)
XLA Ops:
  4.0 34.8 %reshape.171 = f32[16,2,8,2,128,2]{5,4,3,2,1,0:T(8,128)} reshape(f32[32,16,256]{2,1,0:T(8,128)S(1)} %copy.20) | data formatting | bytes 1048576 | tf_op jit(solution)/shard_map/reshape | solution.py:81
  38.9 12.2 %reduce_sum.55 = f32[16,8,128]{2,1,0:T(8,128)S(1)} reduce(f32[16,2,8,2,128,2]{5,4,3,2,1,0:T(8,128)} %reshape.171, f32[]{:T(128)} %constant.39.clone.1), dimensions={1,3,5}, to_apply=%region_1.0 | reduce | flops 114688 | bytes 589828 | tf_op jit(solution)/shard_map/reduce_sum | solution.py:80
  51.1 5.6 %div.62 = f32[8,2,4,2,64,2]{5,4,3,2,1,0:T(8,128)} reshape(f32[16,8,128]{2,1,0:T(8,128)S(1)} %broadcast_multiply_fusion) | data formatting | bytes 131072 | tf_op jit(solution)/shard_map/div | solution.py:80
  60.0 7.7 %collective-permute-start.27 = (f32[4,1,32]{2,0,1:T(4,128)S(1)}, f32[4,1,32]{2,0,1:T(4,128)S(1)}, u32[]{:S(2)}, u32[]{:S(2)}) collective-permute-start(f32[4,1,32]{2,0,1:T(4,128)S(1)} %get-tuple-element.140), channel_id=1, source_target_pairs={{1,0},{2,1},{3,2},{4,3},{5,4},{6,5},{7,6},{8,7},{9,8},{10,9},{11,1... | collective-permute-start | bytes 1544 | tf_op jit(solution)/shard_map/ppermute | solution.py:22
  92.9 5.8 %collective-permute-start.23 = (f32[14,3,64]{2,1,0:T(4,128)S(1)}, f32[14,3,64]{2,1,0:T(4,128)S(1)}, u32[]{:S(2)}, u32[]{:S(2)}) collective-permute-start(f32[14,3,64]{2,1,0:T(4,128)S(1)} %get-tuple-element.92), channel_id=1, source_target_pairs={{1,0},{2,1},{3,2},{4,3},{5,4},{6,5},{7,6},{8,7},{9,8},{10,9},{11,1... | collective-permute-start | bytes 32264 | tf_op jit(solution)/shard_map/ppermute | solution.py:41
  113.4 5.3 %collective-permute-start.3 = (f32[36,2,256]{2,0,1:T(8,128)S(1)}, f32[36,2,256]{2,0,1:T(8,128)S(1)}, u32[]{:S(2)}, u32[]{:S(2)}) collective-permute-start(f32[36,2,256]{2,0,1:T(8,128)S(1)} %get-tuple-element.50), channel_id=1, source_target_pairs={{1,0},{2,1},{3,2},{4,3},{5,4},{6,5},{7,6},{8,7},{9,8},{10,9},{11,1... | collective-permute-start | bytes 221192 | tf_op jit(solution)/shard_map/ppermute | solution.py:41
  121.0 6.0 %collective-permute-start.7 = (f32[38,3,256]{2,0,1:T(8,128)S(1)}, f32[38,3,256]{2,0,1:T(8,128)S(1)}, u32[]{:S(2)}, u32[]{:S(2)}) collective-permute-start(f32[38,3,256]{2,0,1:T(8,128)S(1)} %get-tuple-element.46), channel_id=1, source_target_pairs={{1,0},{2,1},{3,2},{4,3},{5,4},{6,5},{7,6},{8,7},{9,8},{10,9},{11,1... | collective-permute-start | bytes 350216 | tf_op jit(solution)/shard_map/ppermute | solution.py:41
  129.5 6.5 %collective-permute-done.6 = f32[38,3,256]{2,0,1:T(8,128)S(1)} collective-permute-done((f32[38,3,256]{2,0,1:T(8,128)S(1)}, f32[38,3,256]{2,0,1:T(8,128)S(1)}, u32[]{:S(2)}, u32[]{:S(2)}) %collective-permute-start.6) | collective-permute-done | bytes 116768 | tf_op jit(solution)/shard_map/ppermute | solution.py:38
  144.9 35.6 %reshape.170 = f32[16,2,8,2,128,2]{5,4,3,2,1,0:T(8,128)} reshape(f32[32,16,256]{2,1,0:T(8,128)} %copy.19) | data formatting | bytes 1048576 | tf_op jit(solution)/shard_map/reshape | solution.py:81
  180.5 12.8 %reduce_sum.54 = f32[16,8,128]{2,1,0:T(8,128)} reduce(f32[16,2,8,2,128,2]{5,4,3,2,1,0:T(8,128)} %reshape.170, f32[]{:T(128)} %constant.39.clone.1), dimensions={1,3,5}, to_apply=%region_0.0 | reduce | flops 114688 | bytes 589828 | tf_op jit(solution)/shard_map/reduce_sum | solution.py:80
  213.1 6.3 %reshape.172 = f32[8,2,4,2,64,2]{5,4,3,2,1,0:T(8,128)} reshape(f32[16,8,128]{2,1,0:T(8,128)} %get-tuple-element.21) | data formatting | bytes 131072 | tf_op jit(solution)/shard_map/reshape | solution.py:81
  259.9 4.0 collective-permute-start.35
  273.6 6.0 %collective-permute-start.39 = (f32[4,1,32]{2,0,1:T(4,128)S(1)}, f32[4,1,32]{2,0,1:T(4,128)S(1)}, u32[]{:S(2)}, u32[]{:S(2)}) collective-permute-start(f32[4,1,32]{2,0,1:T(4,128)S(1)} %get-tuple-element.128), channel_id=1, source_target_pairs={{1,0},{2,1},{3,2},{4,3},{5,4},{6,5},{7,6},{8,7},{9,8},{10,9},{11,1... | collective-permute-start | bytes 1544 | tf_op jit(solution)/shard_map/ppermute | solution.py:22
  289.5 6.0 %collective-permute-start.43 = (f32[4,1,32]{2,0,1:T(4,128)S(1)}, f32[4,1,32]{2,0,1:T(4,128)S(1)}, u32[]{:S(2)}, u32[]{:S(2)}) collective-permute-start(f32[4,1,32]{2,0,1:T(4,128)S(1)} %get-tuple-element.124), channel_id=1, source_target_pairs={{1,0},{2,1},{3,2},{4,3},{5,4},{6,5},{7,6},{8,7},{9,8},{10,9},{11,1... | collective-permute-start | bytes 1544 | tf_op jit(solution)/shard_map/ppermute | solution.py:22
  305.1 6.0 %collective-permute-start.47 = (f32[4,1,32]{2,0,1:T(4,128)S(1)}, f32[4,1,32]{2,0,1:T(4,128)S(1)}, u32[]{:S(2)}, u32[]{:S(2)}) collective-permute-start(f32[4,1,32]{2,0,1:T(4,128)S(1)} %get-tuple-element.120), channel_id=1, source_target_pairs={{1,0},{2,1},{3,2},{4,3},{5,4},{6,5},{7,6},{8,7},{9,8},{10,9},{11,1... | collective-permute-start | bytes 1544 | tf_op jit(solution)/shard_map/ppermute | solution.py:22
  320.8 6.0 %collective-permute-start.51 = (f32[4,1,32]{2,0,1:T(4,128)S(1)}, f32[4,1,32]{2,0,1:T(4,128)S(1)}, u32[]{:S(2)}, u32[]{:S(2)}) collective-permute-start(f32[4,1,32]{2,0,1:T(4,128)S(1)} %get-tuple-element.116), channel_id=1, source_target_pairs={{1,0},{2,1},{3,2},{4,3},{5,4},{6,5},{7,6},{8,7},{9,8},{10,9},{11,1... | collective-permute-start | bytes 1544 | tf_op jit(solution)/shard_map/ppermute | solution.py:22
  336.4 6.0 %collective-permute-start.55 = (f32[4,1,32]{2,0,1:T(4,128)S(1)}, f32[4,1,32]{2,0,1:T(4,128)S(1)}, u32[]{:S(2)}, u32[]{:S(2)}) collective-permute-start(f32[4,1,32]{2,0,1:T(4,128)S(1)} %get-tuple-element.112), channel_id=1, source_target_pairs={{1,0},{2,1},{3,2},{4,3},{5,4},{6,5},{7,6},{8,7},{9,8},{10,9},{11,1... | collective-permute-start | bytes 1544 | tf_op jit(solution)/shard_map/ppermute | solution.py:22
  362.6 6.0 %collective-permute-start.59 = (f32[12,2,64]{2,1,0:T(2,128)S(1)}, f32[12,2,64]{2,1,0:T(2,128)S(1)}, u32[]{:S(2)}, u32[]{:S(2)}) collective-permute-start(f32[12,2,64]{2,1,0:T(2,128)S(1)} %get-tuple-element.94), channel_id=1, source_target_pairs={{1,0},{2,1},{3,2},{4,3},{5,4},{6,5},{7,6},{8,7},{9,8},{10,9},{11,1... | collective-permute-start | bytes 18440 | tf_op jit(solution)/shard_map/ppermute | solution.py:41
  370.6 5.8 %collective-permute-done.58 = f32[12,2,64]{2,1,0:T(2,128)S(1)} collective-permute-done((f32[12,2,64]{2,1,0:T(2,128)S(1)}, f32[12,2,64]{2,1,0:T(2,128)S(1)}, u32[]{:S(2)}, u32[]{:S(2)}) %collective-permute-start.58) | collective-permute-done | bytes 6176 | tf_op jit(solution)/shard_map/ppermute | solution.py:38
  380.9 4.6 reshape.175
  405.8 11.4 %broadcast_in_dim.194 = f32[16,2,8,2,128,2]{5,4,3,2,1,0:T(8,128)} broadcast(f32[16,8,128]{2,1,0:T(8,128)S(1)} %fusion.169), dimensions={0,2,4} | broadcast | bytes 589824 | tf_op jit(solution)/shard_map/broadcast_in_dim | solution.py:87
  417.2 24.6 %reshape.176 = f32[32,16,256]{2,1,0:T(8,128)} reshape(f32[16,2,8,2,128,2]{5,4,3,2,1,0:T(8,128)} %broadcast_in_dim.194) | data formatting | bytes 1048576 | tf_op jit(solution)/shard_map/reshape | solution.py:91
  457.0 4.0 collective-permute-done.66
  461.2 4.0 fusion.32
  (445 shorter events, 232.2 us)
Async XLA Ops:
  1.5 109.2 %collective-permute-start.1 = (f32[2,16,256]{2,0,1:T(2,128)S(1)}, f32[2,16,256]{2,0,1:T(2,128)S(1)}, u32[]{:S(2)}, u32[]{:S(2)}) collective-permute-start(f32[2,16,256]{2,0,1:T(2,128)S(1)} %get-tuple-element.56), channel_id=1, source_target_pairs={{32,0},{64,32},{96,64},{128,96},{160,128},{192,160},{224,192},{33,... | collective-permute-start | bytes 98312 | tf_op jit(solution)/shard_map/ppermute | solution.py:41
  60.0 21.8 %collective-permute-start.27 = (f32[4,1,32]{2,0,1:T(4,128)S(1)}, f32[4,1,32]{2,0,1:T(4,128)S(1)}, u32[]{:S(2)}, u32[]{:S(2)}) collective-permute-start(f32[4,1,32]{2,0,1:T(4,128)S(1)} %get-tuple-element.140), channel_id=1, source_target_pairs={{1,0},{2,1},{3,2},{4,3},{5,4},{6,5},{7,6},{8,7},{9,8},{10,9},{11,1... | collective-permute-start | bytes 1544 | tf_op jit(solution)/shard_map/ppermute | solution.py:22
  67.7 16.2 %collective-permute-start.24 = (f32[4,1,32]{2,0,1:T(4,128)S(1)}, f32[4,1,32]{2,0,1:T(4,128)S(1)}, u32[]{:S(2)}, u32[]{:S(2)}) collective-permute-start(f32[4,1,32]{2,0,1:T(4,128)S(1)} %get-tuple-element.139), channel_id=1, source_target_pairs={{0,1},{1,2},{2,3},{3,4},{4,5},{5,6},{6,7},{7,8},{8,9},{9,10},{10,1... | collective-permute-start | bytes 1544 | tf_op jit(solution)/shard_map/ppermute | solution.py:21
  76.2 37.2 %collective-permute-start = (f32[2,16,256]{2,0,1:T(2,128)S(1)}, f32[2,16,256]{2,0,1:T(2,128)S(1)}, u32[]{:S(2)}, u32[]{:S(2)}) collective-permute-start(f32[2,16,256]{2,0,1:T(2,128)S(1)} %get-tuple-element.55), channel_id=1, source_target_pairs={{0,32},{32,64},{64,96},{96,128},{128,160},{160,192},{192,224},{1,3... | collective-permute-start | bytes 98312 | tf_op jit(solution)/shard_map/ppermute | solution.py:38
  79.5 41.5 %collective-permute-start.5 = (f32[3,16,256]{2,0,1:T(4,128)S(1)}, f32[3,16,256]{2,0,1:T(4,128)S(1)}, u32[]{:S(2)}, u32[]{:S(2)}) collective-permute-start(f32[3,16,256]{2,0,1:T(4,128)S(1)} %get-tuple-element.54), channel_id=1, source_target_pairs={{32,0},{64,32},{96,64},{128,96},{160,128},{192,160},{224,192},{33,... | collective-permute-start | bytes 147464 | tf_op jit(solution)/shard_map/ppermute | solution.py:41
  98.7 7.9 %collective-permute-start.22 = (f32[14,3,64]{2,1,0:T(4,128)S(1)}, f32[14,3,64]{2,1,0:T(4,128)S(1)}, u32[]{:S(2)}, u32[]{:S(2)}) collective-permute-start(f32[14,3,64]{2,1,0:T(4,128)S(1)} %get-tuple-element.91), channel_id=1, source_target_pairs={{0,1},{1,2},{2,3},{3,4},{4,5},{5,6},{6,7},{7,8},{8,9},{9,10},{10,1... | collective-permute-start | bytes 32264 | tf_op jit(solution)/shard_map/ppermute | solution.py:38
  100.7 20.3 %collective-permute-start.4 = (f32[3,16,256]{2,0,1:T(4,128)S(1)}, f32[3,16,256]{2,0,1:T(4,128)S(1)}, u32[]{:S(2)}, u32[]{:S(2)}) collective-permute-start(f32[3,16,256]{2,0,1:T(4,128)S(1)} %get-tuple-element.53), channel_id=1, source_target_pairs={{0,32},{32,64},{64,96},{96,128},{128,160},{160,192},{192,224},{1,3... | collective-permute-start | bytes 147464 | tf_op jit(solution)/shard_map/ppermute | solution.py:38
  106.6 12.2 %collective-permute-start.15 = (f32[22,3,128]{2,1,0:T(4,128)S(1)}, f32[22,3,128]{2,1,0:T(4,128)S(1)}, u32[]{:S(2)}, u32[]{:S(2)}) collective-permute-start(f32[22,3,128]{2,1,0:T(4,128)S(1)} %get-tuple-element.73), channel_id=1, source_target_pairs={{1,0},{2,1},{3,2},{4,3},{5,4},{6,5},{7,6},{8,7},{9,8},{10,9},{11,1... | collective-permute-start | bytes 101384 | tf_op jit(solution)/shard_map/ppermute | solution.py:41
  110.7 10.0 %collective-permute-start.14 = (f32[22,3,128]{2,1,0:T(4,128)S(1)}, f32[22,3,128]{2,1,0:T(4,128)S(1)}, u32[]{:S(2)}, u32[]{:S(2)}) collective-permute-start(f32[22,3,128]{2,1,0:T(4,128)S(1)} %get-tuple-element.72), channel_id=1, source_target_pairs={{0,1},{1,2},{2,3},{3,4},{4,5},{5,6},{6,7},{7,8},{8,9},{9,10},{10,1... | collective-permute-start | bytes 101384 | tf_op jit(solution)/shard_map/ppermute | solution.py:38
  113.4 23.9 %collective-permute-start.3 = (f32[36,2,256]{2,0,1:T(8,128)S(1)}, f32[36,2,256]{2,0,1:T(8,128)S(1)}, u32[]{:S(2)}, u32[]{:S(2)}) collective-permute-start(f32[36,2,256]{2,0,1:T(8,128)S(1)} %get-tuple-element.50), channel_id=1, source_target_pairs={{1,0},{2,1},{3,2},{4,3},{5,4},{6,5},{7,6},{8,7},{9,8},{10,9},{11,1... | collective-permute-start | bytes 221192 | tf_op jit(solution)/shard_map/ppermute | solution.py:41
  118.7 18.6 %collective-permute-start.2 = (f32[36,2,256]{2,0,1:T(8,128)S(1)}, f32[36,2,256]{2,0,1:T(8,128)S(1)}, u32[]{:S(2)}, u32[]{:S(2)}) collective-permute-start(f32[36,2,256]{2,0,1:T(8,128)S(1)} %get-tuple-element.49), channel_id=1, source_target_pairs={{0,1},{1,2},{2,3},{3,4},{4,5},{5,6},{6,7},{7,8},{8,9},{9,10},{10,1... | collective-permute-start | bytes 221192 | tf_op jit(solution)/shard_map/ppermute | solution.py:38
  121.0 8.5 %collective-permute-start.7 = (f32[38,3,256]{2,0,1:T(8,128)S(1)}, f32[38,3,256]{2,0,1:T(8,128)S(1)}, u32[]{:S(2)}, u32[]{:S(2)}) collective-permute-start(f32[38,3,256]{2,0,1:T(8,128)S(1)} %get-tuple-element.46), channel_id=1, source_target_pairs={{1,0},{2,1},{3,2},{4,3},{5,4},{6,5},{7,6},{8,7},{9,8},{10,9},{11,1... | collective-permute-start | bytes 350216 | tf_op jit(solution)/shard_map/ppermute | solution.py:41
  127.1 8.9 %collective-permute-start.6 = (f32[38,3,256]{2,0,1:T(8,128)S(1)}, f32[38,3,256]{2,0,1:T(8,128)S(1)}, u32[]{:S(2)}, u32[]{:S(2)}) collective-permute-start(f32[38,3,256]{2,0,1:T(8,128)S(1)} %get-tuple-element.45), channel_id=1, source_target_pairs={{0,1},{1,2},{2,3},{3,4},{4,5},{5,6},{6,7},{7,8},{8,9},{9,10},{10,1... | collective-permute-start | bytes 350216 | tf_op jit(solution)/shard_map/ppermute | solution.py:38
  203.0 7.8 %collective-permute-start.10 = (f32[20,2,128]{2,1,0:T(2,128)S(1)}, f32[20,2,128]{2,1,0:T(2,128)S(1)}, u32[]{:S(2)}, u32[]{:S(2)}) collective-permute-start(f32[20,2,128]{2,1,0:T(2,128)S(1)} %get-tuple-element.82), channel_id=1, source_target_pairs={{0,1},{1,2},{2,3},{3,4},{4,5},{5,6},{6,7},{7,8},{8,9},{9,10},{10,1... | collective-permute-start | bytes 61448 | tf_op jit(solution)/shard_map/ppermute | solution.py:38
  246.4 10.2 %collective-permute-start.31 = (f32[4,1,32]{2,0,1:T(4,128)S(1)}, f32[4,1,32]{2,0,1:T(4,128)S(1)}, u32[]{:S(2)}, u32[]{:S(2)}) collective-permute-start(f32[4,1,32]{2,0,1:T(4,128)S(1)} %get-tuple-element.136), channel_id=1, source_target_pairs={{1,0},{2,1},{3,2},{4,3},{5,4},{6,5},{7,6},{8,7},{9,8},{10,9},{11,1... | collective-permute-start | bytes 1544 | tf_op jit(solution)/shard_map/ppermute | solution.py:22
  248.3 8.3 %collective-permute-start.30 = (f32[4,1,32]{2,0,1:T(4,128)S(1)}, f32[4,1,32]{2,0,1:T(4,128)S(1)}, u32[]{:S(2)}, u32[]{:S(2)}) collective-permute-start(f32[4,1,32]{2,0,1:T(4,128)S(1)} %get-tuple-element.135), channel_id=1, source_target_pairs={{0,1},{1,2},{2,3},{3,4},{4,5},{5,6},{6,7},{7,8},{8,9},{9,10},{10,1... | collective-permute-start | bytes 1544 | tf_op jit(solution)/shard_map/ppermute | solution.py:21
  259.9 10.3 %collective-permute-start.35 = (f32[4,1,32]{2,0,1:T(4,128)S(1)}, f32[4,1,32]{2,0,1:T(4,128)S(1)}, u32[]{:S(2)}, u32[]{:S(2)}) collective-permute-start(f32[4,1,32]{2,0,1:T(4,128)S(1)} %get-tuple-element.132), channel_id=1, source_target_pairs={{1,0},{2,1},{3,2},{4,3},{5,4},{6,5},{7,6},{8,7},{9,8},{10,9},{11,1... | collective-permute-start | bytes 1544 | tf_op jit(solution)/shard_map/ppermute | solution.py:22
  273.6 12.5 %collective-permute-start.39 = (f32[4,1,32]{2,0,1:T(4,128)S(1)}, f32[4,1,32]{2,0,1:T(4,128)S(1)}, u32[]{:S(2)}, u32[]{:S(2)}) collective-permute-start(f32[4,1,32]{2,0,1:T(4,128)S(1)} %get-tuple-element.128), channel_id=1, source_target_pairs={{1,0},{2,1},{3,2},{4,3},{5,4},{6,5},{7,6},{8,7},{9,8},{10,9},{11,1... | collective-permute-start | bytes 1544 | tf_op jit(solution)/shard_map/ppermute | solution.py:22
  289.5 12.3 %collective-permute-start.43 = (f32[4,1,32]{2,0,1:T(4,128)S(1)}, f32[4,1,32]{2,0,1:T(4,128)S(1)}, u32[]{:S(2)}, u32[]{:S(2)}) collective-permute-start(f32[4,1,32]{2,0,1:T(4,128)S(1)} %get-tuple-element.124), channel_id=1, source_target_pairs={{1,0},{2,1},{3,2},{4,3},{5,4},{6,5},{7,6},{8,7},{9,8},{10,9},{11,1... | collective-permute-start | bytes 1544 | tf_op jit(solution)/shard_map/ppermute | solution.py:22
  305.1 12.3 %collective-permute-start.47 = (f32[4,1,32]{2,0,1:T(4,128)S(1)}, f32[4,1,32]{2,0,1:T(4,128)S(1)}, u32[]{:S(2)}, u32[]{:S(2)}) collective-permute-start(f32[4,1,32]{2,0,1:T(4,128)S(1)} %get-tuple-element.120), channel_id=1, source_target_pairs={{1,0},{2,1},{3,2},{4,3},{5,4},{6,5},{7,6},{8,7},{9,8},{10,9},{11,1... | collective-permute-start | bytes 1544 | tf_op jit(solution)/shard_map/ppermute | solution.py:22
  320.8 12.3 %collective-permute-start.51 = (f32[4,1,32]{2,0,1:T(4,128)S(1)}, f32[4,1,32]{2,0,1:T(4,128)S(1)}, u32[]{:S(2)}, u32[]{:S(2)}) collective-permute-start(f32[4,1,32]{2,0,1:T(4,128)S(1)} %get-tuple-element.116), channel_id=1, source_target_pairs={{1,0},{2,1},{3,2},{4,3},{5,4},{6,5},{7,6},{8,7},{9,8},{10,9},{11,1... | collective-permute-start | bytes 1544 | tf_op jit(solution)/shard_map/ppermute | solution.py:22
  336.4 12.3 %collective-permute-start.55 = (f32[4,1,32]{2,0,1:T(4,128)S(1)}, f32[4,1,32]{2,0,1:T(4,128)S(1)}, u32[]{:S(2)}, u32[]{:S(2)}) collective-permute-start(f32[4,1,32]{2,0,1:T(4,128)S(1)} %get-tuple-element.112), channel_id=1, source_target_pairs={{1,0},{2,1},{3,2},{4,3},{5,4},{6,5},{7,6},{8,7},{9,8},{10,9},{11,1... | collective-permute-start | bytes 1544 | tf_op jit(solution)/shard_map/ppermute | solution.py:22
  362.6 8.0 %collective-permute-start.59 = (f32[12,2,64]{2,1,0:T(2,128)S(1)}, f32[12,2,64]{2,1,0:T(2,128)S(1)}, u32[]{:S(2)}, u32[]{:S(2)}) collective-permute-start(f32[12,2,64]{2,1,0:T(2,128)S(1)} %get-tuple-element.94), channel_id=1, source_target_pairs={{1,0},{2,1},{3,2},{4,3},{5,4},{6,5},{7,6},{8,7},{9,8},{10,9},{11,1... | collective-permute-start | bytes 18440 | tf_op jit(solution)/shard_map/ppermute | solution.py:41
  452.6 8.4 %collective-permute-start.66 = (f32[36,2,256]{2,0,1:T(8,128)S(1)}, f32[36,2,256]{2,0,1:T(8,128)S(1)}, u32[]{:S(2)}, u32[]{:S(2)}) collective-permute-start(f32[36,2,256]{2,0,1:T(8,128)S(1)} %get-tuple-element.47), channel_id=1, source_target_pairs={{0,1},{1,2},{2,3},{3,4},{4,5},{5,6},{6,7},{7,8},{8,9},{9,10},{10,1... | collective-permute-start | bytes 221192 | tf_op jit(solution)/shard_map/ppermute | solution.py:38
  (124 other events, 1153.5 us)
where the time goes:
time: 472 us; the launch traced here: 468 us
  starting transfers between devices  198 us (42%)
  local copies, waits for them, and re-layouts  141 us (30%)
  other arithmetic  68 us (14%)
  waiting for transfers between devices  58.4 us (12%)
    reshape x4, local copies, waits for them, and re-layouts, restrict(): values.reshape(values.shape[0] // 2, 2, values.shape[1] // 2, 2, values.s...  78.8 us
    ppermute x16, starting transfers between devices, padded_2(): lax.ppermute(initial, axis, [(b, a) for a, b in up])  59.5 us
    ppermute x18, starting transfers between devices, extended(): lax.ppermute(lax.slice_in_dim(block, 0, width, axis=dim), axis, backward)  53.4 us
    ppermute x18, starting transfers between devices, extended(): lax.ppermute(lax.slice_in_dim(block, block.shape[dim] - width, None, axis...  49 us
    ppermute x18, waiting for transfers between devices, extended(): lax.ppermute(lax.slice_in_dim(block, block.shape[dim] - width, None, axis...  40.6 us
    ppermute x16, starting transfers between devices, padded_2(): lax.ppermute(last, axis, up)  36.6 us
    reduce_sum x6, other arithmetic, restrict(): jnp.mean(values.reshape(values.shape[0] // 2, 2, values.shape[1] // 2, 2,...  32.6 us
    reshape x3, local copies, waits for them, and re-layouts, prolong(): expanded.reshape(values.shape[0] * 2, values.shape[1] * 2, values.shape[2...  31.1 us
  transfers between devices with their start and end apart: 68, of which 27 were waited for; matrix products, arithmetic and copies ran while one was open for 14% of the time, Pallas kernels for 0%

commit v1 on v0

v1 whole, which is shorter than its diff:
```python
import jax
import jax.numpy as jnp
from jax import lax
from jax.experimental import pallas as pl
from jax.experimental.pallas import tpu as pltpu
from jax.sharding import PartitionSpec as P

F32 = jnp.float32
W = 24
HIGH = lax.Precision.HIGHEST


def iota(shape, dim):
    return lax.broadcasted_iota(jnp.int32, shape, dim)


def up(x):
    return pltpu.roll(x, 1, 0)


def down(x):
    return pltpu.roll(x, x.shape[0] - 1, 0)


def left(x):
    return pltpu.roll(x, 1, 1)


def right(x):
    return pltpu.roll(x, x.shape[1] - 1, 1)


def dot(a, b):
    return jnp.dot(a, b, precision=HIGH, preferred_element_type=F32)


def select_matrix(shape, where):
    return jnp.where(where(iota(shape, 0), iota(shape, 1)), 1.0, 0.0).astype(F32)


def wrap(x, n):
    return jnp.where(x < 0, x + n, jnp.where(x >= n, x - n, x))


class Level:
    def __init__(self, rows, halo, cols, right_cols, lanes, planes, nrows, ncols):
        self.rows, self.halo, self.cols, self.right_cols = rows, halo, cols, right_cols
        self.lanes, self.planes, self.nrows, self.ncols = lanes, planes, nrows, ncols
        self.total = rows + 2 * halo

    def masks(self):
        shape = (W, self.lanes)
        col = iota(shape, 0)
        col = jnp.where(col < self.cols + self.right_cols, col, col - W)
        col = wrap(col + lax.axis_index("py") * self.cols, self.ncols)
        lane = iota(shape, 1)
        return (
            lane < self.planes,
            col == 0,
            col == self.ncols - 1,
            lane == 0,
            lane == self.planes - 1,
            (lane > 0) & (lane < self.planes),
        )

    def global_row(self, i):
        return wrap(lax.axis_index("px") * self.rows - self.halo + i, self.nrows)


def prepare(level, mob, rhs, sx, sy, sz, coef, diag, out):
    inside, first_col, last_col, first_plane, last_plane, inner_plane = level.masks()

    def step(i, carry):
        m, above, below = mob[i], mob[i - 1], mob[i + 1]
        g = level.global_row(i)
        wx = m + above
        m_up, m_left = up(m), left(m)
        sx[i] = jnp.where(g == 0, 0.0, wx)
        sy[i] = jnp.where(first_col, 0.0, m + m_up)
        sz[i] = jnp.where(inner_plane, m + m_left, 0.0)
        d = 6.0 * m + jnp.where(g == 0, m, above) + jnp.where(g == level.nrows - 1, m, below)
        d = d + jnp.where(first_col, m, m_up) + jnp.where(last_col, m, down(m))
        d = d + jnp.where(first_plane, m, m_left) + jnp.where(last_plane, m, right(m))
        c = jnp.where(inside, 0.8 / d, 0.0)
        coef[i] = c
        diag[i] = d
        out[i] = c * rhs[i]
        return carry

    lax.fori_loop(1, level.total - 1, step, 0)
    last = level.total - 1
    sx[last] = jnp.where(level.global_row(last) == 0, 0.0, mob[last] + mob[last - 1])


def coupling(v, i, sx, sy, sz):
    c = v[i]
    total = sx[i] * v[i - 1] + sx[i + 1] * v[i + 1]
    wy = sy[i]
    total = total + wy * up(c) + down(wy * c)
    wz = sz[i]
    return c, total + wz * left(c) + right(wz * c)


def sweep(lo, hi, v, out, rhs, sx, sy, sz, coef):
    def step(i, carry):
        c, total = coupling(v, i, sx, sy, sz)
        out[i] = 0.2 * c + coef[i] * (rhs[i] + total)
        return carry

    lax.fori_loop(lo, hi, step, 0)


def paired_residual(pairs, lo, v, out, rhs, sx, sy, sz, diag):
    def row(i):
        c, total = coupling(v, i, sx, sy, sz)
        return rhs[i] - diag[i] * c + total

    def step(k, carry):
        i = lo + 2 * k
        out[k] = row(i) + row(i + 1)
        return carry

    lax.fori_loop(0, pairs, step, 0)


def pair_planes(lanes_in, offset=0, lanes_out=128):
    return select_matrix((lanes_in, lanes_out), lambda r, c: (r >> 1) + offset == c)


def spread_planes(lanes_out, offset=0, planes=128):
    return select_matrix((128, lanes_out), lambda r, c: ((c >> 1) + offset == r) & ((c >> 1) < planes))


def level0_kernel(lv, src, dens, lo, hi, from_left, from_right, packed, v, rhs, sx, sy, sz, coef,
                  mob, first, diag, pair, low):
    h = lv.halo
    tile = iota((8, lv.lanes), 0)

    def load(i, s, d):
        rhs[i, 0:16] = 2.0 * s
        mob[i, 0:16] = 1.0 / d
        a, b = from_right[i], from_left[i]
        rhs[i, 16:24] = 2.0 * jnp.where(tile < 4, a, b)
        mob[i, 16:24] = 1.0 / pltpu.roll(jnp.where(tile < 4, b, a), 4, 0)

    for i in range(h):
        load(i, lo[i], lo[h + i])
        load(lv.total - h + i, hi[i], hi[h + i])

    def body(i, carry):
        load(h + i, src[i], dens[i])
        return carry

    lax.fori_loop(0, lv.rows, body, 0)
    zero = jnp.zeros((W, lv.lanes), F32)
    for ref in (first, v):
        ref[0] = zero
        ref[lv.total - 1] = zero
    prepare(lv, mob, rhs, sx, sy, sz, coef, diag, first)
    sweep(1, lv.total - 1, first, v, rhs, sx, sy, sz, coef)
    half = lv.rows // 2
    z = pair_planes(lv.lanes)
    paired_residual(half, h, v, pair, rhs, sx, sy, sz, diag)

    def emit(place, scale):
        x = dot(pair[:, 0:16].reshape(half * 16, lv.lanes), z)
        low[...] = x
        y = low[pl.ds(0, half * 8, stride=2)] + low[pl.ds(1, half * 8, stride=2)]
        packed[:, place : place + 8] = (scale * y).reshape(half, 8, 128)

    emit(0, 0.5)

    def mobs(k, carry):
        pair[k] = mob[h + 2 * k] + mob[h + 2 * k + 1]
        return carry

    lax.fori_loop(0, half, mobs, 0)
    emit(8, 0.125)


def level1_kernel(lv, own, lo, hi, from_left, from_right, packed, v, rhs, sx, sy, sz, coef,
                  mob, first, diag, pair, low):
    h = lv.halo

    def load(i, block):
        rhs[i, 0:8] = block[0:8]
        mob[i, 0:8] = block[8:16]
        rhs[i, 8:16] = from_right[i, 0:8]
        mob[i, 8:16] = from_right[i, 8:16]
        rhs[i, 16:24] = from_left[i, 0:8]
        mob[i, 16:24] = from_left[i, 8:16]

    for i in range(h):
        load(i, lo[i])
        load(lv.total - h + i, hi[i])

    def body(i, carry):
        load(h + i, own[i])
        return carry

    lax.fori_loop(0, lv.rows, body, 0)
    zero = jnp.zeros((W, lv.lanes), F32)
    for ref in (first, v):
        ref[0] = zero
        ref[lv.total - 1] = zero
    prepare(lv, mob, rhs, sx, sy, sz, coef, diag, first)
    sweep(1, lv.total - 1, first, v, rhs, sx, sy, sz, coef)
    half = lv.rows // 2
    paired_residual(half, h, v, pair, rhs, sx, sy, sz, diag)
    x = 0.5 * dot(pair[...].reshape(half * W, lv.lanes), pair_planes(lv.lanes))

    def mobs(k, carry):
        pair[k] = mob[h + 2 * k] + mob[h + 2 * k + 1]
        return carry

    lax.fori_loop(0, half, mobs, 0)
    low[...] = x + 0.125 * dot(pair[...].reshape(half * W, lv.lanes), pair_planes(lv.lanes, 64))
    for k in range(half):
        a = k * W
        y = low[pl.ds(a, 8, stride=2)] + low[pl.ds(a + 1, 8, stride=2)]
        packed[k, 8:16] = y
        packed[k, 4:8] = y[0:4]
        packed[k, 0:4] = low[pl.ds(a + 16, 4, stride=2)] + low[pl.ds(a + 17, 4, stride=2)]


def level2_kernel(lv, own, lo, hi, from_left, from_right, packed, v, rhs, sx, sy, sz, coef,
                  mob, first, diag, pair, wide):
    h = lv.halo
    tile = iota((8, 128), 0)
    lane = iota((8, 128), 1) < lv.planes

    def load(i, block):
        r = pltpu.roll(from_right[i], 4, 0)
        parts = (jnp.where(tile < 4, block, r), r, from_left[i])
        for k, part in enumerate(parts):
            rhs[i, 8 * k : 8 * k + 8] = jnp.where(lane, part, 0.0)
            mob[i, 8 * k : 8 * k + 8] = jnp.where(lane, pltpu.roll(part, 64, 1), 1.0)

    for i in range(h):
        load(i, lo[i, 8:16])
        load(h + i, own[i, 8:16])
        load(2 * h + i, hi[i, 8:16])
    zero = jnp.zeros((W, lv.lanes), F32)
    for ref in (first, v):
        ref[0] = zero
        ref[lv.total - 1] = zero
    prepare(lv, mob, rhs, sx, sy, sz, coef, diag, first)
    sweep(1, lv.total - 1, first, v, rhs, sx, sy, sz, coef)
    paired_residual(8, 4, v, pair, rhs, sx, sy, sz, diag)
    for k in range(12):
        wide[k] = mob[2 * k] + mob[2 * k + 1]
    for k in range(12, 16):
        wide[k] = zero

    def column(ref, n, q):
        two = ref.reshape(n * W, 128)
        return two[pl.ds((2 * q) % W, n, stride=W)] + two[pl.ds((2 * q + 1) % W, n, stride=W)]

    f = jnp.zeros((8, 128), F32)
    m = jnp.zeros((16, 128), F32)
    for g in range(4):
        place = select_matrix((128, 128), lambda r, c: ((r >> 1) + 32 * g == c) & (r < 64))
        f = f + dot(column(pair, 8, g - 1), place)
        m = m + dot(column(wide, 16, g - 1), place)
    f, m = 0.5 * f, 0.125 * m
    p0 = select_matrix((128, 128), lambda r, c: ((r >> 1) + 96 == c) & (r < 64))
    p3 = select_matrix((128, 128), lambda r, c: ((r >> 1) == c) & (r < 64))
    beside = 0.125 * (dot(column(wide, 16, -2), p0) + dot(column(wide, 16, 3), p3))
    lanes = iota((16, 128), 1)
    nr, nc = lv.nrows // 2, lv.ncols // 2
    row = wrap(iota((16, 128), 0) - 4 + lax.axis_index("px") * 4, nr)
    col = wrap((lanes >> 5) - 1 + lax.axis_index("py") * 2, nc)
    prev = jnp.where(lanes < 32, pltpu.roll(beside, 32, 1), pltpu.roll(m, 32, 1))
    nxt = jnp.where(lanes >= 96, pltpu.roll(beside, 96, 1), pltpu.roll(m, 96, 1))
    d = 6.0 * m + jnp.where(row == 0, m, up(m)) + jnp.where(row == nr - 1, m, down(m))
    d = d + jnp.where(col == 0, m, prev) + jnp.where(col == nc - 1, m, nxt)
    plane = lanes & 31
    d = d + jnp.where(plane == 0, m, left(m)) + jnp.where(plane == 31, m, right(m))
    packed[0] = f
    packed[1] = m[2:10]
    packed[2] = (0.8 / d)[2:10]


def coarse_solve(groups, nr, nc, out):
    shape = (W, 128)
    lane = iota(shape, 1)
    row_ok = wrap(iota(shape, 0) - 10 + lax.axis_index("px") * 4, nr) > 0
    plane_ok = (lane & 31) > 0
    low, high = lane < 32, lane >= 96
    n = len(groups)
    f = [g[0] for g in groups]
    m = [g[1] for g in groups]
    c = [g[2] for g in groups]
    col_ok = [wrap((lane >> 5) - 9 + 4 * k + lax.axis_index("py") * 2, nc) > 0 for k in range(n)]
    zero = jnp.zeros(shape, F32)

    def before(x, k):
        a = pltpu.roll(x[k], 32, 1)
        b = pltpu.roll(x[k - 1], 32, 1) if k else zero
        return jnp.where(low, b, a)

    def after(x, k):
        a = pltpu.roll(x[k], 96, 1)
        b = pltpu.roll(x[k + 1], 96, 1) if k + 1 < n else zero
        return jnp.where(high, b, a)

    sx = [jnp.where(row_ok, a + up(a), 0.0) for a in m]
    sy = [jnp.where(col_ok[k], a + before(m, k), 0.0) for k, a in enumerate(m)]
    sz = [jnp.where(plane_ok, a + left(a), 0.0) for a in m]
    v = [a * b for a, b in zip(c, f)]
    for _ in range(7):
        wy = [a * b for a, b in zip(sy, v)]
        new = []
        for k in range(n):
            x = v[k]
            total = f[k] + sx[k] * up(x) + down(sx[k] * x)
            total = total + sy[k] * before(v, k) + after(wy, k)
            total = total + sz[k] * left(x) + right(sz[k] * x)
            new.append(0.2 * x + c[k] * total)
        v = new
    for k in range(n):
        out[k] = v[k]


def ascent_kernel(levels, g0, g1, g2, g3, g4, *refs):
    fields = [refs[6 * k : 6 * k + 6] for k in range(3)]
    result = refs[18]
    e3, p2, a2, b2, p1, q1, a1, b1, p0, q0, a0, b0 = refs[19:]
    lv0, lv1, lv2 = levels
    coarse_solve([g0, g1, g2, g3, g4], lv2.nrows // 2, lv2.ncols // 2, e3)

    p2[...] = jnp.zeros(p2.shape, F32)
    two = p2.reshape(8 * W, 128)
    for q in range(-2, 4):
        group, g = (q + 9) // 4, (q + 9) % 4
        spread = select_matrix((128, 128), lambda r, c: ((c >> 1) + 32 * g == r) & (c < 64))
        x = dot(e3[group, 8:16], spread)
        two[pl.ds((2 * q) % W, 8, stride=W)] = x
        two[pl.ds((2 * q + 1) % W, 8, stride=W)] = x
    v, rhs, sx, sy, sz, coef = fields[2]

    def add2(i, carry):
        a2[i] = v[i] + p2[i // 2 - 2]
        return carry

    lax.fori_loop(4, 20, add2, 0)
    sweep(5, 19, a2, b2, rhs, sx, sy, sz, coef)
    sweep(6, 18, b2, a2, rhs, sx, sy, sz, coef)

    for k in range(12):
        x = a2[k + 6]
        for s in range(2):
            p1[k, pl.ds(s, 8, stride=2)] = x[0:8]
            p1[k, pl.ds(16 + s, 4, stride=2)] = x[20:24]
    q1[...] = dot(p1[...].reshape(12 * W, 128), spread_planes(128, 0, 64)).reshape(12, W, 128)
    v1, rhs1, sx1, sy1, sz1, coef1 = fields[1]

    def add1(i, carry):
        a1[i] = v1[i] + q1[i // 2 - 1]
        return carry

    lax.fori_loop(3, 25, add1, 0)
    sweep(4, 24, a1, b1, rhs1, sx1, sy1, sz1, coef1)
    sweep(5, 23, b1, a1, rhs1, sx1, sy1, sz1, coef1)

    for k in range(18):
        x = a1[k + 5]
        for s in range(2):
            p0[k, pl.ds(s, 8, stride=2)] = x[0:8]
            p0[k, pl.ds(16 + s, 2, stride=2)] = x[8:10]
            p0[k, pl.ds(20 + s, 2, stride=2)] = x[22:24]
    q0[...] = dot(p0[...].reshape(18 * W, 128), spread_planes(256)).reshape(18, W, 256)
    v0, rhs0, sx0, sy0, sz0, coef0 = fields[0]

    def add0(i, carry):
        b0[i] = v0[i] + q0[i // 2 - 1]
        return carry

    lax.fori_loop(2, 38, add0, 0)
    sweep(3, 37, b0, a0, rhs0, sx0, sy0, sz0, coef0)

    def final(i, carry):
        c, total = coupling(a0, i, sx0, sy0, sz0)
        result[i - 4] = (0.2 * c + coef0[i] * (rhs0[i] + total))[0:16]
        return carry

    lax.fori_loop(4, 36, final, 0)


VMEM = pl.BlockSpec(memory_space=pltpu.VMEM)
LIMIT = 48 << 20


def descend(kernel, lv, inputs, packed, scratch):
    block = jax.ShapeDtypeStruct((lv.total, W, lv.lanes), F32)
    outs = pl.pallas_call(
        lambda *refs: kernel(lv, *refs),
        out_shape=[jax.ShapeDtypeStruct(packed, F32)] + [block] * 6,
        in_specs=[VMEM] * len(inputs),
        out_specs=[VMEM] * 7,
        scratch_shapes=[pltpu.VMEM(block.shape, F32)] * 3 + [pltpu.VMEM(s, F32) for s in scratch],
        compiler_params=pltpu.CompilerParams(vmem_limit_bytes=LIMIT),
        name="descent",
    )(*inputs)
    return outs[0], outs[1:]


def ring(x, axis, step):
    n = lax.axis_size(axis)
    return lax.ppermute(x, axis, [(i, (i + step) % n) for i in range(n)])


def per_device(source, density):
    npx, npy = lax.axis_size("px"), lax.axis_size("py")
    lv0 = Level(32, 4, 16, 4, 256, 256, 32 * npx, 16 * npy)
    lv1 = Level(16, 6, 8, 8, 128, 128, 16 * npx, 8 * npy)
    lv2 = Level(8, 8, 4, 8, 128, 64, 8 * npx, 4 * npy)

    h = lv0.halo
    lo = ring(jnp.concatenate([source[-h:], density[-h:]], 0), "px", 1)
    hi = ring(jnp.concatenate([source[:h], density[:h]], 0), "px", -1)
    es = lambda a, b: jnp.concatenate([lo[:h, a:b], source[:, a:b], hi[:h, a:b]], 0)
    ed = lambda a, b: jnp.concatenate([lo[h:, a:b], density[:, a:b], hi[h:, a:b]], 0)
    from_left = ring(jnp.concatenate([ed(12, 16), es(12, 16)], 1), "py", 1)
    from_right = ring(jnp.concatenate([es(0, 4), ed(0, 4)], 1), "py", -1)
    one, saved0 = descend(
        level0_kernel, lv0, (source, density, lo, hi, from_left, from_right), (16, 16, 128),
        [(16, W, 256), (256, 128)],
    )

    h = lv1.halo
    lo = ring(one[-h:], "px", 1)
    hi = ring(one[:h], "px", -1)
    wide = jnp.concatenate([lo, one, hi], 0)
    from_left = ring(wide, "py", 1)
    from_right = ring(wide, "py", -1)
    two, saved1 = descend(
        level1_kernel, lv1, (one, lo, hi, from_left, from_right), (8, 16, 128),
        [(8, W, 128), (8 * W, 128)],
    )

    lo = ring(two, "px", 1)
    hi = ring(two, "px", -1)
    from_left = ring(jnp.concatenate([lo[:, :8], two[:, :8], hi[:, :8]], 0), "py", 1)
    from_right = ring(jnp.concatenate([lo[:, 8:], two[:, 8:], hi[:, 8:]], 0), "py", -1)
    three, saved2 = descend(
        level2_kernel, lv2, (two, lo, hi, from_left, from_right), (3, 8, 128),
        [(8, W, 128), (16, W, 128)],
    )

    wide = jnp.concatenate([ring(three, "px", 2), three, ring(three, "px", -2)], 1)
    groups = [ring(wide, "py", 4), ring(wide, "py", 2), wide, ring(wide, "py", -2), ring(wide, "py", -4)]
    inputs = (*groups, *saved0, *saved1, *saved2)
    shapes = [(5, W, 128), (8, W, 128), (24, W, 128), (24, W, 128), (12, W, 128), (12, W, 128),
              (28, W, 128), (28, W, 128), (18, W, 128), (18, W, 256), (40, W, 256),
              (40, W, 256)]
    return pl.pallas_call(
        lambda *refs: ascent_kernel((lv0, lv1, lv2), *refs),
        out_shape=jax.ShapeDtypeStruct(source.shape, F32),
        in_specs=[VMEM] * len(inputs),
        out_specs=VMEM,
        scratch_shapes=[pltpu.VMEM(s, F32) for s in shapes],
        compiler_params=pltpu.CompilerParams(vmem_limit_bytes=LIMIT),
        name="ascent",
    )(*inputs)


def solution(mesh):
    spec = P("px", "py", None)
    return jax.shard_map(
        per_device, mesh=mesh, in_specs=(spec, spec), out_specs=spec, check_vma=False
    )
```

time: 472 us -> 121 us (0.26)
  the two profiles are of different devices: /device:TPU:10 before, /device:TPU:120 now
where the time goes in v1:
time: 121 us
  waiting for transfers between devices  45.9 us (38%)
  Pallas kernels  37.9 us (31%)
  starting transfers between devices  34.1 us (28%)
  local copies, waits for them, and re-layouts  3.17 us (3%)
    ppermute x18, waiting for transfers between devices, ring(): return lax.ppermute(x, axis, [(i, (i + step) % n) for i in range(n)])  45.9 us
    ppermute x18, starting transfers between devices, ring(): return lax.ppermute(x, axis, [(i, (i + step) % n) for i in range(n)])  34.1 us
    pallas_call x3, Pallas kernels, descend(): pl.pallas_call(lambda *refs: kernel(lv, *refs), out_shape=[jax.ShapeDtype...  21.1 us
    pallas_call x1, Pallas kernels, per_device(): pl.pallas_call(lambda *refs: ascent_kernel((lv0, lv1, lv2), *refs), out_s...  16.8 us
  transfers between devices with their start and end apart: 18, of which 13 were waited for; matrix products, arithmetic and copies ran while one was open for 0% of the time, Pallas kernels for 0%

profile of v1, /device:TPU:120, one launch (start us, length us, event | category | flops | bytes accessed | tf_op | source)
XLA Modules:
  0.0 121.3 jit_solution(7614489498450333240)
XLA Ops:
  1.1 1.7 %collective-permute-start.1 = (f32[8,16,256]{2,1,0:T(8,128)S(1)}, f32[8,16,256]{2,1,0:T(8,128)S(1)}, u32[]{:S(2)}, u32[]{:S(2)}) collective-permute-start(f32[8,16,256]{2,1,0:T(8,128)S(1)} %pad_maximum_fusion.1), channel_id=1, source_target_pairs={{0,224},{32,0},{64,32},{96,64},{128,96},{160,128},{192,160},{224,1... | collective-permute-start | bytes 393224 | tf_op jit(solution)/shard_map/ppermute | solution.py:410
  3.0 2.5 %collective-permute-done.refs_2_ = f32[8,16,256]{2,1,0:T(8,128)S(1)} collective-permute-done((f32[8,16,256]{2,1,0:T(8,128)S(1)}, f32[8,16,256]{2,1,0:T(8,128)S(1)}, u32[]{:S(2)}, u32[]{:S(2)}) %collective-permute-start) | collective-permute-done | bytes 131104 | tf_op jit(solution)/shard_map/ppermute | solution.py:410
  5.6 3.2 %collective-permute-start.2 = (f32[40,8,256]{2,1,0:T(8,128)S(1)}, f32[40,8,256]{2,1,0:T(8,128)S(1)}, u32[]{:S(2)}, u32[]{:S(2)}) collective-permute-start(f32[40,8,256]{2,1,0:T(8,128)S(1)} %maximum_maximum_fusion), channel_id=1, source_target_pairs={{0,1},{1,2},{2,3},{3,4},{4,5},{5,6},{6,7},{7,8},{8,9},{9,10},{10,1... | collective-permute-start | bytes 983048 | tf_op jit(solution)/shard_map/ppermute | solution.py:410
  9.0 7.4 %collective-permute-done.2.refs_4_ = f32[40,8,256]{2,1,0:T(8,128)S(1)} collective-permute-done((f32[40,8,256]{2,1,0:T(8,128)S(1)}, f32[40,8,256]{2,1,0:T(8,128)S(1)}, u32[]{:S(2)}, u32[]{:S(2)}) %collective-permute-start.2) | collective-permute-done | bytes 327712 | tf_op jit(solution)/shard_map/ppermute | solution.py:410
  16.3 4.1 %collective-permute-done.3.refs_5_ = f32[40,8,256]{2,1,0:T(8,128)S(1)} collective-permute-done((f32[40,8,256]{2,1,0:T(8,128)S(1)}, f32[40,8,256]{2,1,0:T(8,128)S(1)}, u32[]{:S(2)}, u32[]{:S(2)}) %collective-permute-start.3) | collective-permute-done | bytes 327712 | tf_op jit(solution)/shard_map/ppermute | solution.py:410
  20.5 10.7 %descent.3 = (f32[16,16,128]{2,1,0:T(8,128)S(1)}, f32[40,24,256]{2,1,0:T(8,128)S(1)}, f32[40,24,256]{2,1,0:T(8,128)S(1)}, f32[40,24,256]{2,1,0:T(8,128)S(1)}, f3...) custom-call(f32[32,16,256]{2,1,0:T(8,128)S(1)} %copy-done, f32[32,16,256]{2,1,0:T(8,128)S(1)} %copy-done.1, ...), custom_call_target="tpu_custom_call" | custom-call | tf_op jit(solution)/shard_map/descent/pallas_call | solution.py:396
  34.9 1.8 %collective-permute-done.4.refs_1_ = f32[6,16,128]{2,1,0:T(8,128)S(1)} collective-permute-done((f32[6,16,128]{2,1,0:T(8,128)S(1)}, f32[6,16,128]{2,1,0:T(8,128)S(1)}, u32[]{:S(2)}, u32[]{:S(2)}) %collective-permute-start.4) | collective-permute-done | bytes 49184 | tf_op jit(solution)/shard_map/ppermute | solution.py:410
  36.8 3.2 %collective-permute-start.6 = (f32[28,16,128]{2,1,0:T(8,128)S(1)}, f32[28,16,128]{2,1,0:T(8,128)S(1)}, u32[]{:S(2)}, u32[]{:S(2)}) collective-permute-start(f32[28,16,128]{2,1,0:T(8,128)S(1)} %constant_dynamic-update-slice_fusion), channel_id=1, source_target_pairs={{0,1},{1,2},{2,3},{3,4},{4,5},{5,6},{6,7},{7,8},{8,9},{9,10},{10,1... | collective-permute-start | bytes 688136 | tf_op jit(solution)/shard_map/ppermute | solution.py:410
  40.0 5.3 %collective-permute-done.7.refs_4_ = f32[28,16,128]{2,1,0:T(8,128)S(1)} collective-permute-done((f32[28,16,128]{2,1,0:T(8,128)S(1)}, f32[28,16,128]{2,1,0:T(8,128)S(1)}, u32[]{:S(2)}, u32[]{:S(2)}) %collective-permute-start.7) | collective-permute-done | bytes 229408 | tf_op jit(solution)/shard_map/ppermute | solution.py:410
  45.3 5.6 %descent.4 = (f32[8,16,128]{2,1,0:T(8,128)S(1)}, f32[28,24,128]{2,1,0:T(8,128)S(1)}, f32[28,24,128]{2,1,0:T(8,128)S(1)}, f32[28,24,128]{2,1,0:T(8,128)S(1)}, f32...) custom-call(f32[16,16,128]{2,1,0:T(8,128)S(1)} %get-tuple-element.26.refs_0_, ...), custom_call_target="tpu_custom_call" | custom-call | tf_op jit(solution)/shard_map/descent/pallas_call | solution.py:396
  50.9 1.6 %collective-permute-start.9 = (f32[8,16,128]{2,1,0:T(8,128)S(1)}, f32[8,16,128]{2,1,0:T(8,128)S(1)}, u32[]{:S(2)}, u32[]{:S(2)}) collective-permute-start(f32[8,16,128]{2,1,0:T(8,128)S(1)} %get-tuple-element.27.refs_0_), channel_id=1, source_target_pairs={{0,224},{32,0},{64,32},{96,64},{128,96},{160,128},{192,160},{224,1... | collective-permute-start | bytes 196616 | tf_op jit(solution)/shard_map/ppermute | solution.py:410
  52.5 1.9 %collective-permute-done.9.refs_2_ = f32[8,16,128]{2,1,0:T(8,128)S(1)} collective-permute-done((f32[8,16,128]{2,1,0:T(8,128)S(1)}, f32[8,16,128]{2,1,0:T(8,128)S(1)}, u32[]{:S(2)}, u32[]{:S(2)}) %collective-permute-start.9) | collective-permute-done | bytes 65568 | tf_op jit(solution)/shard_map/ppermute | solution.py:410
  54.4 1.8 %collective-permute-done.8.refs_1_ = f32[8,16,128]{2,1,0:T(8,128)S(1)} collective-permute-done((f32[8,16,128]{2,1,0:T(8,128)S(1)}, f32[8,16,128]{2,1,0:T(8,128)S(1)}, u32[]{:S(2)}, u32[]{:S(2)}) %collective-permute-start.8) | collective-permute-done | bytes 65568 | tf_op jit(solution)/shard_map/ppermute | solution.py:410
  56.2 3.2 %collective-permute-start.10 = (f32[24,8,128]{2,1,0:T(8,128)S(1)}, f32[24,8,128]{2,1,0:T(8,128)S(1)}, u32[]{:S(2)}, u32[]{:S(2)}) collective-permute-start(f32[24,8,128]{2,1,0:T(8,128)S(1)} %pad_maximum_fusion.2), channel_id=1, source_target_pairs={{0,1},{1,2},{2,3},{3,4},{4,5},{5,6},{6,7},{7,8},{8,9},{9,10},{10,1... | collective-permute-start | bytes 294920 | tf_op jit(solution)/shard_map/ppermute | solution.py:410
  59.6 2.8 %collective-permute-done.10.refs_3_ = f32[24,8,128]{2,1,0:T(8,128)S(1)} collective-permute-done((f32[24,8,128]{2,1,0:T(8,128)S(1)}, f32[24,8,128]{2,1,0:T(8,128)S(1)}, u32[]{:S(2)}, u32[]{:S(2)}) %collective-permute-start.10) | collective-permute-done | bytes 98336 | tf_op jit(solution)/shard_map/ppermute | solution.py:410
  62.4 3.5 %collective-permute-done.11.refs_4_ = f32[24,8,128]{2,1,0:T(8,128)S(1)} collective-permute-done((f32[24,8,128]{2,1,0:T(8,128)S(1)}, f32[24,8,128]{2,1,0:T(8,128)S(1)}, u32[]{:S(2)}, u32[]{:S(2)}) %collective-permute-start.11) | collective-permute-done | bytes 98336 | tf_op jit(solution)/shard_map/ppermute | solution.py:410
  65.9 4.8 %descent.5 = (f32[3,8,128]{2,1,0:T(8,128)S(1)}, f32[24,24,128]{2,1,0:T(8,128)S(1)}, f32[24,24,128]{2,1,0:T(8,128)S(1)}, f32[24,24,128]{2,1,0:T(8,128)S(1)}, f32[...) custom-call(f32[8,16,128]{2,1,0:T(8,128)S(1)} %get-tuple-element.27.refs_0_, ...), custom_call_target="tpu_custom_call" | custom-call | tf_op jit(solution)/shard_map/descent/pallas_call | solution.py:396
  70.7 3.1 %collective-permute-start.12 = (f32[3,8,128]{2,1,0:T(8,128)S(1)}, f32[3,8,128]{2,1,0:T(8,128)S(1)}, u32[]{:S(2)}, u32[]{:S(2)}) collective-permute-start(f32[3,8,128]{2,1,0:T(8,128)S(1)} %get-tuple-element.28), channel_id=1, source_target_pairs={{0,64},{32,96},{64,128},{96,160},{128,192},{160,224},{192,0},{224,... | collective-permute-start | bytes 36872 | tf_op jit(solution)/shard_map/ppermute | solution.py:410
  75.2 3.5 %collective-permute-done.13 = f32[3,8,128]{2,1,0:T(8,128)S(1)} collective-permute-done((f32[3,8,128]{2,1,0:T(8,128)S(1)}, f32[3,8,128]{2,1,0:T(8,128)S(1)}, u32[]{:S(2)}, u32[]{:S(2)}) %collective-permute-start.13) | collective-permute-done | bytes 12320 | tf_op jit(solution)/shard_map/ppermute | solution.py:410
  78.7 11.7 %collective-permute-start.17 = (f32[3,24,128]{2,1,0:T(8,128)S(1)}, f32[3,24,128]{2,1,0:T(8,128)S(1)}, u32[]{:S(2)}, u32[]{:S(2)}) collective-permute-start(f32[3,24,128]{2,1,0:T(8,128)S(1)} %constant_dynamic-update-slice_fusion.3.refs_2_), channel_id=1, source_target_pairs={{0,28},{1,29},{2,30},{3,31},{4,0},{5,1},{6,2},{7,3},{8,4},{9,5},{1... | collective-permute-start | bytes 110600 | tf_op jit(solution)/shard_map/ppermute | solution.py:410
  90.4 4.1 %collective-permute-start.15 = (f32[3,24,128]{2,1,0:T(8,128)S(1)}, f32[3,24,128]{2,1,0:T(8,128)S(1)}, u32[]{:S(2)}, u32[]{:S(2)}) collective-permute-start(f32[3,24,128]{2,1,0:T(8,128)S(1)} %constant_dynamic-update-slice_fusion.3.refs_2_), channel_id=1, source_target_pairs={{0,2},{1,3},{2,4},{3,5},{4,6},{5,7},{6,8},{7,9},{8,10},{9,11},{10,... | collective-permute-start | bytes 110600 | tf_op jit(solution)/shard_map/ppermute | solution.py:410
  94.6 2.2 %collective-permute-done.16.refs_3_ = f32[3,24,128]{2,1,0:T(8,128)S(1)} collective-permute-done((f32[3,24,128]{2,1,0:T(8,128)S(1)}, f32[3,24,128]{2,1,0:T(8,128)S(1)}, u32[]{:S(2)}, u32[]{:S(2)}) %collective-permute-start.16) | collective-permute-done | bytes 36896 | tf_op jit(solution)/shard_map/ppermute | solution.py:410
  96.7 7.8 %collective-permute-done.14.refs_0_ = f32[3,24,128]{2,1,0:T(8,128)S(1)} collective-permute-done((f32[3,24,128]{2,1,0:T(8,128)S(1)}, f32[3,24,128]{2,1,0:T(8,128)S(1)}, u32[]{:S(2)}, u32[]{:S(2)}) %collective-permute-start.14) | collective-permute-done | bytes 36896 | tf_op jit(solution)/shard_map/ppermute | solution.py:410
  104.5 16.8 %ascent.1 = f32[32,16,256]{2,1,0:T(8,128)} custom-call(f32[3,24,128]{2,1,0:T(8,128)S(1)} %collective-permute-done.14.refs_0_, f32[3,24,128]{2,1,0:T(8,128)S(1)} %collective-permute-done.15.refs_1_, f32[3,24,128]{2,1,0:T(8,128)S(1)} %constant_dynamic-update-slice_fusion.3.refs_2_, f32[3,24,128]{2,1,0:T(8,128)S(1)} %collective-permute-done.16.refs_3_, ...), custom_call_target="tpu_custom_call" | custom-call | tf_op jit(solution)/shard_map/ascent/pallas_call | solution.py:457
  (44 shorter events, 6.8 us)
Async XLA Ops:
  0.0 2.9 %copy-start.1 = (f32[32,16,256]{2,1,0:T(8,128)S(1)}, f32[32,16,256]{2,1,0:T(8,128)}, u32[]{:S(2)}) copy-start(f32[32,16,256]{2,1,0:T(8,128)} %refs_1_.1) | copy-start | bytes 1572868
  0.0 2.9 %copy-start = (f32[32,16,256]{2,1,0:T(8,128)S(1)}, f32[32,16,256]{2,1,0:T(8,128)}, u32[]{:S(2)}) copy-start(f32[32,16,256]{2,1,0:T(8,128)} %refs_0_.1) | copy-start | bytes 1572868
  1.1 4.4 %collective-permute-start = (f32[8,16,256]{2,1,0:T(8,128)S(1)}, f32[8,16,256]{2,1,0:T(8,128)S(1)}, u32[]{:S(2)}, u32[]{:S(2)}) collective-permute-start(f32[8,16,256]{2,1,0:T(8,128)S(1)} %pad_maximum_fusion), channel_id=1, source_target_pairs={{0,32},{32,64},{64,96},{96,128},{128,160},{160,192},{192,224},{224... | collective-permute-start | bytes 393224 | tf_op jit(solution)/shard_map/ppermute | solution.py:410
  1.1 4.4 %collective-permute-start.1 = (f32[8,16,256]{2,1,0:T(8,128)S(1)}, f32[8,16,256]{2,1,0:T(8,128)S(1)}, u32[]{:S(2)}, u32[]{:S(2)}) collective-permute-start(f32[8,16,256]{2,1,0:T(8,128)S(1)} %pad_maximum_fusion.1), channel_id=1, source_target_pairs={{0,224},{32,0},{64,32},{96,64},{128,96},{160,128},{192,160},{224,1... | collective-permute-start | bytes 393224 | tf_op jit(solution)/shard_map/ppermute | solution.py:410
  5.6 10.7 %collective-permute-start.2 = (f32[40,8,256]{2,1,0:T(8,128)S(1)}, f32[40,8,256]{2,1,0:T(8,128)S(1)}, u32[]{:S(2)}, u32[]{:S(2)}) collective-permute-start(f32[40,8,256]{2,1,0:T(8,128)S(1)} %maximum_maximum_fusion), channel_id=1, source_target_pairs={{0,1},{1,2},{2,3},{3,4},{4,5},{5,6},{6,7},{7,8},{8,9},{9,10},{10,1... | collective-permute-start | bytes 983048 | tf_op jit(solution)/shard_map/ppermute | solution.py:410
  8.9 11.6 %collective-permute-start.3 = (f32[40,8,256]{2,1,0:T(8,128)S(1)}, f32[40,8,256]{2,1,0:T(8,128)S(1)}, u32[]{:S(2)}, u32[]{:S(2)}) collective-permute-start(f32[40,8,256]{2,1,0:T(8,128)S(1)} %maximum_maximum_fusion.1), channel_id=1, source_target_pairs={{0,31},{1,0},{2,1},{3,2},{4,3},{5,4},{6,5},{7,6},{8,7},{9,8},{10,9... | collective-permute-start | bytes 983048 | tf_op jit(solution)/shard_map/ppermute | solution.py:410
  31.2 1.0 copy-start.2
  32.1 1.0 copy-start.3
  33.1 3.5 %collective-permute-start.4 = (f32[6,16,128]{2,1,0:T(8,128)S(1)}, f32[6,16,128]{2,1,0:T(8,128)S(1)}, u32[]{:S(2)}, u32[]{:S(2)}) collective-permute-start(f32[6,16,128]{2,1,0:T(8,128)S(1)} %get-tuple-element.56), channel_id=1, source_target_pairs={{0,32},{32,64},{64,96},{96,128},{128,160},{160,192},{192,224},{224... | collective-permute-start | bytes 147464 | tf_op jit(solution)/shard_map/ppermute | solution.py:410
  33.3 3.4 %collective-permute-start.5 = (f32[6,16,128]{2,1,0:T(8,128)S(1)}, f32[6,16,128]{2,1,0:T(8,128)S(1)}, u32[]{:S(2)}, u32[]{:S(2)}) collective-permute-start(f32[6,16,128]{2,1,0:T(8,128)S(1)} %get-tuple-element.55), channel_id=1, source_target_pairs={{0,224},{32,0},{64,32},{96,64},{128,96},{160,128},{192,160},{224,1... | collective-permute-start | bytes 147464 | tf_op jit(solution)/shard_map/ppermute | solution.py:410
  36.7 8.6 %collective-permute-start.7 = (f32[28,16,128]{2,1,0:T(8,128)S(1)}, f32[28,16,128]{2,1,0:T(8,128)S(1)}, u32[]{:S(2)}, u32[]{:S(2)}) collective-permute-start(f32[28,16,128]{2,1,0:T(8,128)S(1)} %constant_dynamic-update-slice_fusion), channel_id=1, source_target_pairs={{0,31},{1,0},{2,1},{3,2},{4,3},{5,4},{6,5},{7,6},{8,7},{9,8},{10,9... | collective-permute-start | bytes 688136 | tf_op jit(solution)/shard_map/ppermute | solution.py:410
  36.8 8.5 %collective-permute-start.6 = (f32[28,16,128]{2,1,0:T(8,128)S(1)}, f32[28,16,128]{2,1,0:T(8,128)S(1)}, u32[]{:S(2)}, u32[]{:S(2)}) collective-permute-start(f32[28,16,128]{2,1,0:T(8,128)S(1)} %constant_dynamic-update-slice_fusion), channel_id=1, source_target_pairs={{0,1},{1,2},{2,3},{3,4},{4,5},{5,6},{6,7},{7,8},{8,9},{9,10},{10,1... | collective-permute-start | bytes 688136 | tf_op jit(solution)/shard_map/ppermute | solution.py:410
  50.9 3.6 %collective-permute-start.9 = (f32[8,16,128]{2,1,0:T(8,128)S(1)}, f32[8,16,128]{2,1,0:T(8,128)S(1)}, u32[]{:S(2)}, u32[]{:S(2)}) collective-permute-start(f32[8,16,128]{2,1,0:T(8,128)S(1)} %get-tuple-element.27.refs_0_), channel_id=1, source_target_pairs={{0,224},{32,0},{64,32},{96,64},{128,96},{160,128},{192,160},{224,1... | collective-permute-start | bytes 196616 | tf_op jit(solution)/shard_map/ppermute | solution.py:410
  52.5 3.7 %collective-permute-start.8 = (f32[8,16,128]{2,1,0:T(8,128)S(1)}, f32[8,16,128]{2,1,0:T(8,128)S(1)}, u32[]{:S(2)}, u32[]{:S(2)}) collective-permute-start(f32[8,16,128]{2,1,0:T(8,128)S(1)} %get-tuple-element.27.refs_0_), channel_id=1, source_target_pairs={{0,32},{32,64},{64,96},{96,128},{128,160},{160,192},{192,224},{224... | collective-permute-start | bytes 196616 | tf_op jit(solution)/shard_map/ppermute | solution.py:410
  56.2 6.1 %collective-permute-start.10 = (f32[24,8,128]{2,1,0:T(8,128)S(1)}, f32[24,8,128]{2,1,0:T(8,128)S(1)}, u32[]{:S(2)}, u32[]{:S(2)}) collective-permute-start(f32[24,8,128]{2,1,0:T(8,128)S(1)} %pad_maximum_fusion.2), channel_id=1, source_target_pairs={{0,1},{1,2},{2,3},{3,4},{4,5},{5,6},{6,7},{7,8},{8,9},{9,10},{10,1... | collective-permute-start | bytes 294920 | tf_op jit(solution)/shard_map/ppermute | solution.py:410
  59.5 6.4 %collective-permute-start.11 = (f32[24,8,128]{2,1,0:T(8,128)S(1)}, f32[24,8,128]{2,1,0:T(8,128)S(1)}, u32[]{:S(2)}, u32[]{:S(2)}) collective-permute-start(f32[24,8,128]{2,1,0:T(8,128)S(1)} %pad_maximum_fusion.3), channel_id=1, source_target_pairs={{0,31},{1,0},{2,1},{3,2},{4,3},{5,4},{6,5},{7,6},{8,7},{9,8},{10,9... | collective-permute-start | bytes 294920 | tf_op jit(solution)/shard_map/ppermute | solution.py:410
  70.7 4.5 %collective-permute-start.12 = (f32[3,8,128]{2,1,0:T(8,128)S(1)}, f32[3,8,128]{2,1,0:T(8,128)S(1)}, u32[]{:S(2)}, u32[]{:S(2)}) collective-permute-start(f32[3,8,128]{2,1,0:T(8,128)S(1)} %get-tuple-element.28), channel_id=1, source_target_pairs={{0,64},{32,96},{64,128},{96,160},{128,192},{160,224},{192,0},{224,... | collective-permute-start | bytes 36872 | tf_op jit(solution)/shard_map/ppermute | solution.py:410
  73.8 4.9 %collective-permute-start.13 = (f32[3,8,128]{2,1,0:T(8,128)S(1)}, f32[3,8,128]{2,1,0:T(8,128)S(1)}, u32[]{:S(2)}, u32[]{:S(2)}) collective-permute-start(f32[3,8,128]{2,1,0:T(8,128)S(1)} %get-tuple-element.28), channel_id=1, source_target_pairs={{0,192},{32,224},{64,0},{96,32},{128,64},{160,96},{192,128},{224,1... | collective-permute-start | bytes 36872 | tf_op jit(solution)/shard_map/ppermute | solution.py:410
  78.7 15.9 %collective-permute-start.17 = (f32[3,24,128]{2,1,0:T(8,128)S(1)}, f32[3,24,128]{2,1,0:T(8,128)S(1)}, u32[]{:S(2)}, u32[]{:S(2)}) collective-permute-start(f32[3,24,128]{2,1,0:T(8,128)S(1)} %constant_dynamic-update-slice_fusion.3.refs_2_), channel_id=1, source_target_pairs={{0,28},{1,29},{2,30},{3,31},{4,0},{5,1},{6,2},{7,3},{8,4},{9,5},{1... | collective-permute-start | bytes 110600 | tf_op jit(solution)/shard_map/ppermute | solution.py:410
  90.4 6.3 %collective-permute-start.16 = (f32[3,24,128]{2,1,0:T(8,128)S(1)}, f32[3,24,128]{2,1,0:T(8,128)S(1)}, u32[]{:S(2)}, u32[]{:S(2)}) collective-permute-start(f32[3,24,128]{2,1,0:T(8,128)S(1)} %constant_dynamic-update-slice_fusion.3.refs_2_), channel_id=1, source_target_pairs={{0,30},{1,31},{2,0},{3,1},{4,2},{5,3},{6,4},{7,5},{8,6},{9,7},{10,... | collective-permute-start | bytes 110600 | tf_op jit(solution)/shard_map/ppermute | solution.py:410
  90.4 6.3 %collective-permute-start.15 = (f32[3,24,128]{2,1,0:T(8,128)S(1)}, f32[3,24,128]{2,1,0:T(8,128)S(1)}, u32[]{:S(2)}, u32[]{:S(2)}) collective-permute-start(f32[3,24,128]{2,1,0:T(8,128)S(1)} %constant_dynamic-update-slice_fusion.3.refs_2_), channel_id=1, source_target_pairs={{0,2},{1,3},{2,4},{3,5},{4,6},{5,7},{6,8},{7,9},{8,10},{9,11},{10,... | collective-permute-start | bytes 110600 | tf_op jit(solution)/shard_map/ppermute | solution.py:410
  94.6 10.0 %collective-permute-start.14 = (f32[3,24,128]{2,1,0:T(8,128)S(1)}, f32[3,24,128]{2,1,0:T(8,128)S(1)}, u32[]{:S(2)}, u32[]{:S(2)}) collective-permute-start(f32[3,24,128]{2,1,0:T(8,128)S(1)} %constant_dynamic-update-slice_fusion.3.refs_2_), channel_id=1, source_target_pairs={{0,4},{1,5},{2,6},{3,7},{4,8},{5,9},{6,10},{7,11},{8,12},{9,13},{1... | collective-permute-start | bytes 110600 | tf_op jit(solution)/shard_map/ppermute | solution.py:410

commit v2 on v1

--- a/solution.py
+++ b/solution.py
@@ -7,7 +7,8 @@
 
 F32 = jnp.float32
 W = 24
-HIGH = lax.Precision.HIGHEST
+BF16 = jnp.bfloat16
+UNROLL = 2
 
 
 def iota(shape, dim):
@@ -31,11 +32,15 @@
 
 
 def dot(a, b):
-    return jnp.dot(a, b, precision=HIGH, preferred_element_type=F32)
+    high = a.astype(BF16)
+    rest = a - high.astype(F32)
+    mid = rest.astype(BF16)
+    low = (rest - mid.astype(F32)).astype(BF16)
+    return sum(jnp.dot(x, b, preferred_element_type=F32) for x in (high, mid, low))
 
 
 def select_matrix(shape, where):
-    return jnp.where(where(iota(shape, 0), iota(shape, 1)), 1.0, 0.0).astype(F32)
+    return jnp.where(where(iota(shape, 0), iota(shape, 1)), 1.0, 0.0).astype(BF16)
 
 
 def wrap(x, n):
@@ -54,73 +59,93 @@
         col = jnp.where(col < self.cols + self.right_cols, col, col - W)
         col = wrap(col + lax.axis_index("py") * self.cols, self.ncols)
         lane = iota(shape, 1)
-        return (
-            lane < self.planes,
-            col == 0,
-            col == self.ncols - 1,
-            lane == 0,
-            lane == self.planes - 1,
-            (lane > 0) & (lane < self.planes),
-        )
+        edge = lambda hit: jnp.where(hit, 2.0, 0.0)
+        extra = edge(col == 0) + edge(col == self.ncols - 1)
+        extra = extra + edge(lane == 0) + edge(lane == self.planes - 1)
+        return lane < self.planes, col > 0, (lane > 0) & (lane < self.planes), extra
 
     def global_row(self, i):
         return wrap(lax.axis_index("px") * self.rows - self.halo + i, self.nrows)
 
 
 def prepare(level, mob, rhs, sx, sy, sz, coef, diag, out):
-    inside, first_col, last_col, first_plane, last_plane, inner_plane = level.masks()
+    inside, inner_col, inner_plane, extra = level.masks()
+
+    def face(i, a, b):
+        return (a + b) * jnp.where(level.global_row(i) == 0, 0.0, 1.0)
 
     def step(i, carry):
-        m, above, below = mob[i], mob[i - 1], mob[i + 1]
+        m, wx = carry
+        below = mob[i + 1]
         g = level.global_row(i)
-        wx = m + above
-        m_up, m_left = up(m), left(m)
-        sx[i] = jnp.where(g == 0, 0.0, wx)
-        sy[i] = jnp.where(first_col, 0.0, m + m_up)
-        sz[i] = jnp.where(inner_plane, m + m_left, 0.0)
-        d = 6.0 * m + jnp.where(g == 0, m, above) + jnp.where(g == level.nrows - 1, m, below)
-        d = d + jnp.where(first_col, m, m_up) + jnp.where(last_col, m, down(m))
-        d = d + jnp.where(first_plane, m, m_left) + jnp.where(last_plane, m, right(m))
-        c = jnp.where(inside, 0.8 / d, 0.0)
+        next_wx = face(i + 1, m, below)
+        wy = jnp.where(inner_col, m + up(m), 0.0)
+        wz = jnp.where(inner_plane, m + left(m), 0.0)
+        sx[i + 1] = next_wx
+        sy[i] = wy
+        sz[i] = wz
+        ends = jnp.where((g == 0) | (g == level.nrows - 1), 2.0, 0.0)
+        d = (wx + next_wx) + (wy + down(wy)) + (wz + right(wz)) + (extra + ends) * m
+        c = 0.8 / d
+        if level.planes < level.lanes:
+            c = jnp.where(inside, c, 0.0)
         coef[i] = c
         diag[i] = d
         out[i] = c * rhs[i]
-        return carry
-
-    lax.fori_loop(1, level.total - 1, step, 0)
-    last = level.total - 1
-    sx[last] = jnp.where(level.global_row(last) == 0, 0.0, mob[last] + mob[last - 1])
-
-
-def coupling(v, i, sx, sy, sz):
-    c = v[i]
-    total = sx[i] * v[i - 1] + sx[i + 1] * v[i + 1]
-    wy = sy[i]
-    total = total + wy * up(c) + down(wy * c)
-    wz = sz[i]
-    return c, total + wz * left(c) + right(wz * c)
-
-
-def sweep(lo, hi, v, out, rhs, sx, sy, sz, coef):
+        return below, next_wx
+
+    first = face(1, mob[0], mob[1])
+    sx[1] = first
+    lax.fori_loop(1, level.total - 1, step, (mob[1], first), unroll=UNROLL)
+
+
+def walk(lo, hi, load, emit, sx, sy, sz):
     def step(i, carry):
-        c, total = coupling(v, i, sx, sy, sz)
-        out[i] = 0.2 * c + coef[i] * (rhs[i] + total)
-        return carry
-
-    lax.fori_loop(lo, hi, step, 0)
-
-
-def paired_residual(pairs, lo, v, out, rhs, sx, sy, sz, diag):
-    def row(i):
-        c, total = coupling(v, i, sx, sy, sz)
-        return rhs[i] - diag[i] * c + total
-
+        above, c, wx = carry
+        below, next_wx = load(i + 1), sx[i + 1]
+        wy, wz = sy[i], sz[i]
+        total = (wx * above + next_wx * below) + (wy * up(c) + down(wy * c))
+        total = total + (wz * left(c) + right(wz * c))
+        emit(i, c, total)
+        return c, below, next_wx
+
+    lax.fori_loop(lo, hi, step, (load(lo - 1), load(lo), sx[lo]), unroll=UNROLL)
+
+
+def sweep(lo, hi, load, store, rhs, sx, sy, sz, coef):
+    def emit(i, c, total):
+        store(i, 0.2 * c + coef[i] * (rhs[i] + total))
+
+    walk(lo, hi, load, emit, sx, sy, sz)
+
+
+def reader(ref):
+    return lambda i: ref[i]
+
+
+def writer(ref):
+    def store(i, x):
+        ref[i] = x
+
+    return store
+
+
+def paired_residual(pairs, lo, cols, v, out, rhs, sx, sy, sz, diag):
     def step(k, carry):
-        i = lo + 2 * k
-        out[k] = row(i) + row(i + 1)
-        return carry
-
-    lax.fori_loop(0, pairs, step, 0)
+        above, c, wx = carry
+        done = []
+        for j in range(2):
+            i = lo + 2 * k + j
+            below, next_wx = v[i + 1], sx[i + 1]
+            wy, wz = sy[i], sz[i]
+            total = (wx * above + next_wx * below) + (wy * up(c) + down(wy * c))
+            total = total + (wz * left(c) + right(wz * c))
+            done.append((rhs[i] - diag[i] * c + total)[0:cols])
+            above, c, wx = c, below, next_wx
+        out[k] = done[0] + done[1]
+        return above, c, wx
+
+    lax.fori_loop(0, pairs, step, (v[lo - 1], v[lo], sx[lo]))
 
 
 def pair_planes(lanes_in, offset=0, lanes_out=128):
@@ -131,64 +156,75 @@
     return select_matrix((128, lanes_out), lambda r, c: ((c >> 1) + offset == r) & ((c >> 1) < planes))
 
 
-def level0_kernel(lv, src, dens, lo, hi, from_left, from_right, packed, v, rhs, sx, sy, sz, coef,
+def level0_kernel(lv, src, dens, lo, hi, from_left, from_right, corner_left, corner_right, packed, v, rhs, sx, sy, sz, coef,
                   mob, first, diag, pair, low):
     h = lv.halo
     tile = iota((8, lv.lanes), 0)
 
-    def load(i, s, d):
+    def load(i, s, d, a, b):
         rhs[i, 0:16] = 2.0 * s
         mob[i, 0:16] = 1.0 / d
-        a, b = from_right[i], from_left[i]
         rhs[i, 16:24] = 2.0 * jnp.where(tile < 4, a, b)
         mob[i, 16:24] = 1.0 / pltpu.roll(jnp.where(tile < 4, b, a), 4, 0)
 
     for i in range(h):
-        load(i, lo[i], lo[h + i])
-        load(lv.total - h + i, hi[i], hi[h + i])
+        load(i, lo[i], lo[h + i], corner_right[i], corner_left[i])
+        load(lv.total - h + i, hi[i], hi[h + i], corner_right[h + i], corner_left[h + i])
 
     def body(i, carry):
-        load(h + i, src[i], dens[i])
+        load(h + i, src[i], dens[i], from_right[i], from_left[i])
         return carry
 
-    lax.fori_loop(0, lv.rows, body, 0)
+    lax.fori_loop(0, lv.rows, body, 0, unroll=UNROLL)
     zero = jnp.zeros((W, lv.lanes), F32)
     for ref in (first, v):
         ref[0] = zero
         ref[lv.total - 1] = zero
     prepare(lv, mob, rhs, sx, sy, sz, coef, diag, first)
-    sweep(1, lv.total - 1, first, v, rhs, sx, sy, sz, coef)
+    sweep(1, lv.total - 1, reader(first), writer(v), rhs, sx, sy, sz, coef)
     half = lv.rows // 2
     z = pair_planes(lv.lanes)
-    paired_residual(half, h, v, pair, rhs, sx, sy, sz, diag)
-
-    def emit(place, scale):
-        x = dot(pair[:, 0:16].reshape(half * 16, lv.lanes), z)
-        low[...] = x
-        y = low[pl.ds(0, half * 8, stride=2)] + low[pl.ds(1, half * 8, stride=2)]
-        packed[:, place : place + 8] = (scale * y).reshape(half, 8, 128)
-
-    emit(0, 0.5)
+    paired_residual(half, h, 16, v, pair.at[:, 0:16], rhs, sx, sy, sz, diag)
+
+    low[0 : half * 16] = 0.5 * dot(pair[:, 0:16].reshape(half * 16, lv.lanes), z)
+    fine = low[pl.ds(0, half * 8, stride=2)] + low[pl.ds(1, half * 8, stride=2)]
 
     def mobs(k, carry):
         pair[k] = mob[h + 2 * k] + mob[h + 2 * k + 1]
         return carry
 
-    lax.fori_loop(0, half, mobs, 0)
-    emit(8, 0.125)
+    lax.fori_loop(0, half, mobs, 0, unroll=UNROLL)
+    low[...] = 0.125 * dot(pair[...].reshape(half * W, lv.lanes), z)
+    at = iota((8, 128), 0)
+    beside = jnp.zeros((4, 128), F32)
+    for k in range(half):
+        f = fine[8 * k : 8 * k + 8]
+        m = low[pl.ds(k * W, 8, stride=2)] + low[pl.ds(k * W + 1, 8, stride=2)]
+        e = low[pl.ds(k * W + 16, 4, stride=2)] + low[pl.ds(k * W + 17, 4, stride=2)]
+        e = pltpu.roll(jnp.concatenate([e, beside], 0), 2, 0)
+        shifted = pltpu.roll(m, 2, 0)
+        packed[k, 0:8] = jnp.where(at < 4, pltpu.roll(f, 4, 0), shifted)
+        packed[k, 8:16] = jnp.where(at < 4, f, shifted)
+        packed[k, 16:24] = jnp.where((at < 2) | (at >= 6), m, e)
 
 
 def level1_kernel(lv, own, lo, hi, from_left, from_right, packed, v, rhs, sx, sy, sz, coef,
                   mob, first, diag, pair, low):
     h = lv.halo
 
+    at = iota((8, lv.lanes), 0)
+
     def load(i, block):
-        rhs[i, 0:8] = block[0:8]
-        mob[i, 0:8] = block[8:16]
-        rhs[i, 8:16] = from_right[i, 0:8]
-        mob[i, 8:16] = from_right[i, 8:16]
-        rhs[i, 16:24] = from_left[i, 0:8]
-        mob[i, 16:24] = from_left[i, 8:16]
+        t0, t1, t2 = block[0:8], block[8:16], block[16:24]
+        a, b = from_right[i], from_left[i]
+        rhs[i, 0:8] = jnp.where(at < 4, t1, pltpu.roll(t0, 4, 0))
+        rhs[i, 8:16] = a
+        rhs[i, 16:24] = pltpu.roll(b, 4, 0)
+        mob[i, 0:8] = jnp.where((at < 2) | (at >= 6), t2, pltpu.roll(t0, 6, 0))
+        far = jnp.where(at < 6, pltpu.roll(a, 6, 0), 1.0)
+        mob[i, 8:16] = jnp.where(at < 2, pltpu.roll(t2, 6, 0), far)
+        far = jnp.where(at < 2, 1.0, pltpu.roll(b, 6, 0))
+        mob[i, 16:24] = jnp.where(at < 6, far, pltpu.roll(t2, 2, 0))
 
     for i in range(h):
         load(i, lo[i])
@@ -198,15 +234,15 @@
         load(h + i, own[i])
         return carry
 
-    lax.fori_loop(0, lv.rows, body, 0)
+    lax.fori_loop(0, lv.rows, body, 0, unroll=UNROLL)
     zero = jnp.zeros((W, lv.lanes), F32)
     for ref in (first, v):
         ref[0] = zero
         ref[lv.total - 1] = zero
     prepare(lv, mob, rhs, sx, sy, sz, coef, diag, first)
-    sweep(1, lv.total - 1, first, v, rhs, sx, sy, sz, coef)
+    sweep(1, lv.total - 1, reader(first), writer(v), rhs, sx, sy, sz, coef)
     half = lv.rows // 2
-    paired_residual(half, h, v, pair, rhs, sx, sy, sz, diag)
+    paired_residual(half, h, W, v, pair, rhs, sx, sy, sz, diag)
     x = 0.5 * dot(pair[...].reshape(half * W, lv.lanes), pair_planes(lv.lanes))
 
     def mobs(k, carry):
@@ -245,8 +281,8 @@
         ref[0] = zero
         ref[lv.total - 1] = zero
     prepare(lv, mob, rhs, sx, sy, sz, coef, diag, first)
-    sweep(1, lv.total - 1, first, v, rhs, sx, sy, sz, coef)
-    paired_residual(8, 4, v, pair, rhs, sx, sy, sz, diag)
+    sweep(1, lv.total - 1, reader(first), writer(v), rhs, sx, sy, sz, coef)
+    paired_residual(8, 4, W, v, pair, rhs, sx, sy, sz, diag)
     for k in range(12):
         wide[k] = mob[2 * k] + mob[2 * k + 1]
     for k in range(12, 16):
@@ -325,7 +361,7 @@
 def ascent_kernel(levels, g0, g1, g2, g3, g4, *refs):
     fields = [refs[6 * k : 6 * k + 6] for k in range(3)]
     result = refs[18]
-    e3, p2, a2, b2, p1, q1, a1, b1, p0, q0, a0, b0 = refs[19:]
+    e3, p2, a2, b2, p1, q1, a1, b1, p0, q0, a0 = refs[19:]
     lv0, lv1, lv2 = levels
     coarse_solve([g0, g1, g2, g3, g4], lv2.nrows // 2, lv2.ncols // 2, e3)
 
@@ -339,13 +375,9 @@
         two[pl.ds((2 * q + 1) % W, 8, stride=W)] = x
     v, rhs, sx, sy, sz, coef = fields[2]
 
-    def add2(i, carry):
-        a2[i] = v[i] + p2[i // 2 - 2]
-        return carry
-
-    lax.fori_loop(4, 20, add2, 0)
-    sweep(5, 19, a2, b2, rhs, sx, sy, sz, coef)
-    sweep(6, 18, b2, a2, rhs, sx, sy, sz, coef)
+    value2 = lambda i: v[i] + p2[i // 2 - 2]
+    sweep(5, 19, value2, writer(b2), rhs, sx, sy, sz, coef)
+    sweep(6, 18, reader(b2), writer(a2), rhs, sx, sy, sz, coef)
 
     for k in range(12):
         x = a2[k + 6]
@@ -355,13 +387,9 @@
     q1[...] = dot(p1[...].reshape(12 * W, 128), spread_planes(128, 0, 64)).reshape(12, W, 128)
     v1, rhs1, sx1, sy1, sz1, coef1 = fields[1]
 
-    def add1(i, carry):
-        a1[i] = v1[i] + q1[i // 2 - 1]
-        return carry
-
-    lax.fori_loop(3, 25, add1, 0)
-    sweep(4, 24, a1, b1, rhs1, sx1, sy1, sz1, coef1)
-    sweep(5, 23, b1, a1, rhs1, sx1, sy1, sz1, coef1)
+    value1 = lambda i: v1[i] + q1[i // 2 - 1]
+    sweep(4, 24, value1, writer(b1), rhs1, sx1, sy1, sz1, coef1)
+    sweep(5, 23, reader(b1), writer(a1), rhs1, sx1, sy1, sz1, coef1)
 
     for k in range(18):
         x = a1[k + 5]
@@ -372,23 +400,17 @@
     q0[...] = dot(p0[...].reshape(18 * W, 128), spread_planes(256)).reshape(18, W, 256)
     v0, rhs0, sx0, sy0, sz0, coef0 = fields[0]
 
-    def add0(i, carry):
-        b0[i] = v0[i] + q0[i // 2 - 1]
-        return carry
-
-    lax.fori_loop(2, 38, add0, 0)
-    sweep(3, 37, b0, a0, rhs0, sx0, sy0, sz0, coef0)
-
-    def final(i, carry):
-        c, total = coupling(a0, i, sx0, sy0, sz0)
-        result[i - 4] = (0.2 * c + coef0[i] * (rhs0[i] + total))[0:16]
-        return carry
-
-    lax.fori_loop(4, 36, final, 0)
+    value0 = lambda i: v0[i] + q0[i // 2 - 1]
+    sweep(3, 37, value0, writer(a0), rhs0, sx0, sy0, sz0, coef0)
+
+    def final(i, x):
+        result[i - 4] = x[0:16]
+
+    sweep(4, 36, reader(a0), final, rhs0, sx0, sy0, sz0, coef0)
 
 
 VMEM = pl.BlockSpec(memory_space=pltpu.VMEM)
-LIMIT = 48 << 20
+LIMIT = 14 << 20
 
 
 def descend(kernel, lv, inputs, packed, scratch):
@@ -419,21 +441,26 @@
     h = lv0.halo
     lo = ring(jnp.concatenate([source[-h:], density[-h:]], 0), "px", 1)
     hi = ring(jnp.concatenate([source[:h], density[:h]], 0), "px", -1)
-    es = lambda a, b: jnp.concatenate([lo[:h, a:b], source[:, a:b], hi[:h, a:b]], 0)
-    ed = lambda a, b: jnp.concatenate([lo[h:, a:b], density[:, a:b], hi[h:, a:b]], 0)
-    from_left = ring(jnp.concatenate([ed(12, 16), es(12, 16)], 1), "py", 1)
-    from_right = ring(jnp.concatenate([es(0, 4), ed(0, 4)], 1), "py", -1)
+    to_right = lambda s, d: jnp.concatenate([d[:, 12:16], s[:, 12:16]], 1)
+    to_left = lambda s, d: jnp.concatenate([s[:, 0:4], d[:, 0:4]], 1)
+    from_left = ring(to_right(source, density), "py", 1)
+    from_right = ring(to_left(source, density), "py", -1)
+    row_source = jnp.concatenate([lo[:h], hi[:h]], 0)
+    row_density = jnp.concatenate([lo[h:], hi[h:]], 0)
+    corner_left = ring(to_right(row_source, row_density), "py", 1)
+    corner_right = ring(to_left(row_source, row_density), "py", -1)
     one, saved0 = descend(
-        level0_kernel, lv0, (source, density, lo, hi, from_left, from_right), (16, 16, 128),
-        [(16, W, 256), (256, 128)],
+        level0_kernel, lv0, (source, density, lo, hi, from_left, from_right, corner_left, corner_right),
+        (16, W, 128),
+        [(16, W, 256), (16 * W, 128)],
     )
 
     h = lv1.halo
     lo = ring(one[-h:], "px", 1)
     hi = ring(one[:h], "px", -1)
-    wide = jnp.concatenate([lo, one, hi], 0)
-    from_left = ring(wide, "py", 1)
-    from_right = ring(wide, "py", -1)
+    wide = lambda a: jnp.concatenate([lo[:, a : a + 8], one[:, a : a + 8], hi[:, a : a + 8]], 0)
+    from_left = ring(wide(0), "py", 1)
+    from_right = ring(wide(8), "py", -1)
     two, saved1 = descend(
         level1_kernel, lv1, (one, lo, hi, from_left, from_right), (8, 16, 128),
         [(8, W, 128), (8 * W, 128)],
@@ -452,8 +479,7 @@
     groups = [ring(wide, "py", 4), ring(wide, "py", 2), wide, ring(wide, "py", -2), ring(wide, "py", -4)]
     inputs = (*groups, *saved0, *saved1, *saved2)
     shapes = [(5, W, 128), (8, W, 128), (24, W, 128), (24, W, 128), (12, W, 128), (12, W, 128),
-              (28, W, 128), (28, W, 128), (18, W, 128), (18, W, 256), (40, W, 256),
-              (40, W, 256)]
+              (28, W, 128), (28, W, 128), (18, W, 128), (18, W, 256), (40, W, 256)]
     return pl.pallas_call(
         lambda *refs: ascent_kernel((lv0, lv1, lv2), *refs),
         out_shape=jax.ShapeDtypeStruct(source.shape, F32),

time: 121 us -> 98.6 us (0.81)
  Pallas kernels: 37.9 us -> 24.2 us
  waiting for transfers between devices: 45.9 us -> 37.3 us
  local copies, waits for them, and re-layouts: 3.17 us -> 1.22 us
  starting transfers between devices: 34.1 us -> 35.4 us
    ppermute x18 -> x20, waiting for transfers between devices: 45.9 us -> 37.3 us  [ring(): return lax.ppermute(x, axis, [(i, (i + step) % n) for i in range(n)])]
    pallas_call x1, Pallas kernels: 16.8 us -> 8.51 us  [per_device(): pl.pallas_call(lambda *refs: ascent_kernel((lv0, lv1, lv2), *refs), out_s...]
    pallas_call x3, Pallas kernels: 21.1 us -> 15.7 us  [descend(): pl.pallas_call(lambda *refs: kernel(lv, *refs), out_shape=[jax.ShapeDtype...]
    unnamed x12 -> x6, local copies, waits for them, and re-layouts: 1.98 us -> 0.01 us
    ppermute x18 -> x20, starting transfers between devices: 34.1 us -> 35.4 us  [ring(): return lax.ppermute(x, axis, [(i, (i + step) % n) for i in range(n)])]
  transfers between devices with their start and end apart: 18 -> 20, of which waited for: 13 -> 13; matrix products, arithmetic and copies ran while one was open for 0% -> 0% of each run, Pallas kernels for 0% -> 0%
where the time goes in v2:
time: 98.6 us; the launch traced here: 98.5 us
  waiting for transfers between devices  37.3 us (38%)
  starting transfers between devices  35.4 us (36%)
  Pallas kernels  24.2 us (25%)
  local copies, waits for them, and re-layouts  1.22 us (1%)
    ppermute x20, waiting for transfers between devices, ring(): return lax.ppermute(x, axis, [(i, (i + step) % n) for i in range(n)])  37.3 us
    ppermute x20, starting transfers between devices, ring(): return lax.ppermute(x, axis, [(i, (i + step) % n) for i in range(n)])  35.4 us
    pallas_call x3, Pallas kernels, descend(): pl.pallas_call(lambda *refs: kernel(lv, *refs), out_shape=[jax.ShapeDtype...  15.7 us
    pallas_call x1, Pallas kernels, per_device(): pl.pallas_call(lambda *refs: ascent_kernel((lv0, lv1, lv2), *refs), out_s...  8.51 us
  transfers between devices with their start and end apart: 20, of which 13 were waited for; matrix products, arithmetic and copies ran while one was open for 0% of the time, Pallas kernels for 0%

profile of v2, /device:TPU:120, one launch (start us, length us, event | category | flops | bytes accessed | tf_op | source)
XLA Modules:
  0.0 98.5 jit_solution(5583236828416011755)
XLA Ops:
  1.1 1.7 %collective-permute-start.1 = (f32[8,16,256]{2,1,0:T(8,128)S(1)}, f32[8,16,256]{2,1,0:T(8,128)S(1)}, u32[]{:S(2)}, u32[]{:S(2)}) collective-permute-start(f32[8,16,256]{2,1,0:T(8,128)S(1)} %pad_maximum_fusion.3), channel_id=1, source_target_pairs={{0,224},{32,0},{64,32},{96,64},{128,96},{160,128},{192,160},{224,1... | collective-permute-start | bytes 393224 | tf_op jit(solution)/shard_map/ppermute | solution.py:432
  3.0 3.2 %collective-permute-start.2 = (f32[32,8,256]{2,1,0:T(8,128)S(1)}, f32[32,8,256]{2,1,0:T(8,128)S(1)}, u32[]{:S(2)}, u32[]{:S(2)}) collective-permute-start(f32[32,8,256]{2,1,0:T(8,128)S(1)} %pad_maximum_fusion), channel_id=1, source_target_pairs={{0,1},{1,2},{2,3},{3,4},{4,5},{5,6},{6,7},{7,8},{8,9},{9,10},{10,1... | collective-permute-start | bytes 786440 | tf_op jit(solution)/shard_map/ppermute | solution.py:432
  6.5 3.3 %collective-permute-start.4 = (f32[8,8,256]{2,1,0:T(8,128)S(1)}, f32[8,8,256]{2,1,0:T(8,128)S(1)}, u32[]{:S(2)}, u32[]{:S(2)}) collective-permute-start(f32[8,8,256]{2,1,0:T(8,128)S(1)} %get-tuple-element.56), channel_id=1, source_target_pairs={{0,1},{1,2},{2,3},{3,4},{4,5},{5,6},{6,7},{7,8},{8,9},{9,10},{10,1... | collective-permute-start | bytes 196616 | tf_op jit(solution)/shard_map/ppermute | solution.py:432
  9.8 5.8 %collective-permute-done.5.refs_7_ = f32[8,8,256]{2,1,0:T(8,128)S(1)} collective-permute-done((f32[8,8,256]{2,1,0:T(8,128)S(1)}, f32[8,8,256]{2,1,0:T(8,128)S(1)}, u32[]{:S(2)}, u32[]{:S(2)}) %collective-permute-start.5) | collective-permute-done | bytes 65568 | tf_op jit(solution)/shard_map/ppermute | solution.py:432
  15.7 7.6 %descent.3 = (f32[16,24,128]{2,1,0:T(8,128)S(1)}, f32[40,24,256]{2,1,0:T(8,128)S(1)}, f32[40,24,256]{2,1,0:T(8,128)S(1)}, f32[40,24,256]{2,1,0:T(8,128)S(1)}, f3...) custom-call(f32[32,16,256]{2,1,0:T(8,128)S(1)} %copy-done, ...), custom_call_target="tpu_custom_call" | custom-call | tf_op jit(solution)/shard_map/descent/pallas_call | solution.py:418
  23.8 1.5 %collective-permute-done.7.refs_2_ = f32[6,24,128]{2,1,0:T(8,128)S(1)} collective-permute-done((f32[6,24,128]{2,1,0:T(8,128)S(1)}, f32[6,24,128]{2,1,0:T(8,128)S(1)}, u32[]{:S(2)}, u32[]{:S(2)}) %collective-permute-start.7) | collective-permute-done | bytes 73760 | tf_op jit(solution)/shard_map/ppermute | solution.py:432
  25.3 1.8 %collective-permute-done.6.refs_1_ = f32[6,24,128]{2,1,0:T(8,128)S(1)} collective-permute-done((f32[6,24,128]{2,1,0:T(8,128)S(1)}, f32[6,24,128]{2,1,0:T(8,128)S(1)}, u32[]{:S(2)}, u32[]{:S(2)}) %collective-permute-start.6) | collective-permute-done | bytes 73760 | tf_op jit(solution)/shard_map/ppermute | solution.py:432
  27.4 1.9 %collective-permute-start.9 = (f32[28,8,128]{2,1,0:T(8,128)S(1)}, f32[28,8,128]{2,1,0:T(8,128)S(1)}, u32[]{:S(2)}, u32[]{:S(2)}) collective-permute-start(f32[28,8,128]{2,1,0:T(8,128)S(1)} %pad_maximum_fusion.5), channel_id=1, source_target_pairs={{0,31},{1,0},{2,1},{3,2},{4,3},{5,4},{6,5},{7,6},{8,7},{9,8},{10,9... | collective-permute-start | bytes 344072 | tf_op jit(solution)/shard_map/ppermute | solution.py:432
  29.3 2.7 %collective-permute-done.8.refs_3_ = f32[28,8,128]{2,1,0:T(8,128)S(1)} collective-permute-done((f32[28,8,128]{2,1,0:T(8,128)S(1)}, f32[28,8,128]{2,1,0:T(8,128)S(1)}, u32[]{:S(2)}, u32[]{:S(2)}) %collective-permute-start.8) | collective-permute-done | bytes 114720 | tf_op jit(solution)/shard_map/ppermute | solution.py:432
  32.0 2.4 %collective-permute-done.9.refs_4_ = f32[28,8,128]{2,1,0:T(8,128)S(1)} collective-permute-done((f32[28,8,128]{2,1,0:T(8,128)S(1)}, f32[28,8,128]{2,1,0:T(8,128)S(1)}, u32[]{:S(2)}, u32[]{:S(2)}) %collective-permute-start.9) | collective-permute-done | bytes 114720 | tf_op jit(solution)/shard_map/ppermute | solution.py:432
  34.5 4.4 %descent.4 = (f32[8,16,128]{2,1,0:T(8,128)S(1)}, f32[28,24,128]{2,1,0:T(8,128)S(1)}, f32[28,24,128]{2,1,0:T(8,128)S(1)}, f32[28,24,128]{2,1,0:T(8,128)S(1)}, f32...) custom-call(f32[16,24,128]{2,1,0:T(8,128)S(1)} %get-tuple-element.26.refs_0_, ...), custom_call_target="tpu_custom_call" | custom-call | tf_op jit(solution)/shard_map/descent/pallas_call | solution.py:418
  40.8 1.8 %collective-permute-done.10.refs_1_ = f32[8,16,128]{2,1,0:T(8,128)S(1)} collective-permute-done((f32[8,16,128]{2,1,0:T(8,128)S(1)}, f32[8,16,128]{2,1,0:T(8,128)S(1)}, u32[]{:S(2)}, u32[]{:S(2)}) %collective-permute-start.10) | collective-permute-done | bytes 65568 | tf_op jit(solution)/shard_map/ppermute | solution.py:432
  42.9 1.9 %collective-permute-start.13 = (f32[24,8,128]{2,1,0:T(8,128)S(1)}, f32[24,8,128]{2,1,0:T(8,128)S(1)}, u32[]{:S(2)}, u32[]{:S(2)}) collective-permute-start(f32[24,8,128]{2,1,0:T(8,128)S(1)} %pad_maximum_fusion.7), channel_id=1, source_target_pairs={{0,31},{1,0},{2,1},{3,2},{4,3},{5,4},{6,5},{7,6},{8,7},{9,8},{10,9... | collective-permute-start | bytes 294920 | tf_op jit(solution)/shard_map/ppermute | solution.py:432
  44.8 3.3 %collective-permute-done.12.refs_3_ = f32[24,8,128]{2,1,0:T(8,128)S(1)} collective-permute-done((f32[24,8,128]{2,1,0:T(8,128)S(1)}, f32[24,8,128]{2,1,0:T(8,128)S(1)}, u32[]{:S(2)}, u32[]{:S(2)}) %collective-permute-start.12) | collective-permute-done | bytes 98336 | tf_op jit(solution)/shard_map/ppermute | solution.py:432
  48.1 1.6 %collective-permute-done.13.refs_4_ = f32[24,8,128]{2,1,0:T(8,128)S(1)} collective-permute-done((f32[24,8,128]{2,1,0:T(8,128)S(1)}, f32[24,8,128]{2,1,0:T(8,128)S(1)}, u32[]{:S(2)}, u32[]{:S(2)}) %collective-permute-start.13) | collective-permute-done | bytes 98336 | tf_op jit(solution)/shard_map/ppermute | solution.py:432
  49.7 3.8 %descent.5 = (f32[3,8,128]{2,1,0:T(8,128)S(1)}, f32[24,24,128]{2,1,0:T(8,128)S(1)}, f32[24,24,128]{2,1,0:T(8,128)S(1)}, f32[24,24,128]{2,1,0:T(8,128)S(1)}, f32[...) custom-call(f32[8,16,128]{2,1,0:T(8,128)S(1)} %get-tuple-element.27.refs_0_, ...), custom_call_target="tpu_custom_call" | custom-call | tf_op jit(solution)/shard_map/descent/pallas_call | solution.py:418
  53.5 3.3 %collective-permute-start.14 = (f32[3,8,128]{2,1,0:T(8,128)S(1)}, f32[3,8,128]{2,1,0:T(8,128)S(1)}, u32[]{:S(2)}, u32[]{:S(2)}) collective-permute-start(f32[3,8,128]{2,1,0:T(8,128)S(1)} %get-tuple-element.28), channel_id=1, source_target_pairs={{0,64},{32,96},{64,128},{96,160},{128,192},{160,224},{192,0},{224,... | collective-permute-start | bytes 36872 | tf_op jit(solution)/shard_map/ppermute | solution.py:432
  56.8 1.4 %collective-permute-done.14 = f32[3,8,128]{2,1,0:T(8,128)S(1)} collective-permute-done((f32[3,8,128]{2,1,0:T(8,128)S(1)}, f32[3,8,128]{2,1,0:T(8,128)S(1)}, u32[]{:S(2)}, u32[]{:S(2)}) %collective-permute-start.14) | collective-permute-done | bytes 12320 | tf_op jit(solution)/shard_map/ppermute | solution.py:432
  58.2 3.5 %collective-permute-done.15 = f32[3,8,128]{2,1,0:T(8,128)S(1)} collective-permute-done((f32[3,8,128]{2,1,0:T(8,128)S(1)}, f32[3,8,128]{2,1,0:T(8,128)S(1)}, u32[]{:S(2)}, u32[]{:S(2)}) %collective-permute-start.15) | collective-permute-done | bytes 12320 | tf_op jit(solution)/shard_map/ppermute | solution.py:432
  61.7 14.2 %collective-permute-start.19 = (f32[3,24,128]{2,1,0:T(8,128)S(1)}, f32[3,24,128]{2,1,0:T(8,128)S(1)}, u32[]{:S(2)}, u32[]{:S(2)}) collective-permute-start(f32[3,24,128]{2,1,0:T(8,128)S(1)} %constant_dynamic-update-slice_fusion.refs_2_), channel_id=1, source_target_pairs={{0,28},{1,29},{2,30},{3,31},{4,0},{5,1},{6,2},{7,3},{8,4},{9,5},{1... | collective-permute-start | bytes 110600 | tf_op jit(solution)/shard_map/ppermute | solution.py:432
  75.9 4.1 %collective-permute-start.17 = (f32[3,24,128]{2,1,0:T(8,128)S(1)}, f32[3,24,128]{2,1,0:T(8,128)S(1)}, u32[]{:S(2)}, u32[]{:S(2)}) collective-permute-start(f32[3,24,128]{2,1,0:T(8,128)S(1)} %constant_dynamic-update-slice_fusion.refs_2_), channel_id=1, source_target_pairs={{0,2},{1,3},{2,4},{3,5},{4,6},{5,7},{6,8},{7,9},{8,10},{9,11},{10,... | collective-permute-start | bytes 110600 | tf_op jit(solution)/shard_map/ppermute | solution.py:432
  80.0 2.1 %collective-permute-done.18.refs_3_ = f32[3,24,128]{2,1,0:T(8,128)S(1)} collective-permute-done((f32[3,24,128]{2,1,0:T(8,128)S(1)}, f32[3,24,128]{2,1,0:T(8,128)S(1)}, u32[]{:S(2)}, u32[]{:S(2)}) %collective-permute-start.18) | collective-permute-done | bytes 36896 | tf_op jit(solution)/shard_map/ppermute | solution.py:432
  82.1 7.8 %collective-permute-done.16.refs_0_ = f32[3,24,128]{2,1,0:T(8,128)S(1)} collective-permute-done((f32[3,24,128]{2,1,0:T(8,128)S(1)}, f32[3,24,128]{2,1,0:T(8,128)S(1)}, u32[]{:S(2)}, u32[]{:S(2)}) %collective-permute-start.16) | collective-permute-done | bytes 36896 | tf_op jit(solution)/shard_map/ppermute | solution.py:432
  90.0 8.5 %ascent.1 = f32[32,16,256]{2,1,0:T(8,128)} custom-call(f32[3,24,128]{2,1,0:T(8,128)S(1)} %collective-permute-done.16.refs_0_, f32[3,24,128]{2,1,0:T(8,128)S(1)} %collective-permute-done.17.refs_1_, f32[3,24,128]{2,1,0:T(8,128)S(1)} %constant_dynamic-update-slice_fusion.refs_2_, f32[3,24,128]{2,1,0:T(8,128)S(1)} %collective-permute-done.18.refs_3_, ...), custom_call_target="tpu_custom_call" | custom-call | tf_op jit(solution)/shard_map/ascent/pallas_call | solution.py:483
  (47 shorter events, 4.6 us)
Async XLA Ops:
  0.0 2.9 %copy-start.1 = (f32[32,16,256]{2,1,0:T(8,128)S(1)}, f32[32,16,256]{2,1,0:T(8,128)}, u32[]{:S(2)}) copy-start(f32[32,16,256]{2,1,0:T(8,128)} %refs_1_.1) | copy-start | bytes 1572868
  0.0 2.9 %copy-start = (f32[32,16,256]{2,1,0:T(8,128)S(1)}, f32[32,16,256]{2,1,0:T(8,128)}, u32[]{:S(2)}) copy-start(f32[32,16,256]{2,1,0:T(8,128)} %refs_0_.1) | copy-start | bytes 1572868
  1.1 5.3 %collective-permute-start = (f32[8,16,256]{2,1,0:T(8,128)S(1)}, f32[8,16,256]{2,1,0:T(8,128)S(1)}, u32[]{:S(2)}, u32[]{:S(2)}) collective-permute-start(f32[8,16,256]{2,1,0:T(8,128)S(1)} %pad_maximum_fusion.2), channel_id=1, source_target_pairs={{0,32},{32,64},{64,96},{96,128},{128,160},{160,192},{192,224},{224... | collective-permute-start | bytes 393224 | tf_op jit(solution)/shard_map/ppermute | solution.py:432
  1.1 5.3 %collective-permute-start.1 = (f32[8,16,256]{2,1,0:T(8,128)S(1)}, f32[8,16,256]{2,1,0:T(8,128)S(1)}, u32[]{:S(2)}, u32[]{:S(2)}) collective-permute-start(f32[8,16,256]{2,1,0:T(8,128)S(1)} %pad_maximum_fusion.3), channel_id=1, source_target_pairs={{0,224},{32,0},{64,32},{96,64},{128,96},{160,128},{192,160},{224,1... | collective-permute-start | bytes 393224 | tf_op jit(solution)/shard_map/ppermute | solution.py:432
  3.0 12.7 %collective-permute-start.2 = (f32[32,8,256]{2,1,0:T(8,128)S(1)}, f32[32,8,256]{2,1,0:T(8,128)S(1)}, u32[]{:S(2)}, u32[]{:S(2)}) collective-permute-start(f32[32,8,256]{2,1,0:T(8,128)S(1)} %pad_maximum_fusion), channel_id=1, source_target_pairs={{0,1},{1,2},{2,3},{3,4},{4,5},{5,6},{6,7},{7,8},{8,9},{9,10},{10,1... | collective-permute-start | bytes 786440 | tf_op jit(solution)/shard_map/ppermute | solution.py:432
  6.3 9.4 %collective-permute-start.3 = (f32[32,8,256]{2,1,0:T(8,128)S(1)}, f32[32,8,256]{2,1,0:T(8,128)S(1)}, u32[]{:S(2)}, u32[]{:S(2)}) collective-permute-start(f32[32,8,256]{2,1,0:T(8,128)S(1)} %pad_maximum_fusion.1), channel_id=1, source_target_pairs={{0,31},{1,0},{2,1},{3,2},{4,3},{5,4},{6,5},{7,6},{8,7},{9,8},{10,9... | collective-permute-start | bytes 786440 | tf_op jit(solution)/shard_map/ppermute | solution.py:432
  6.5 9.2 %collective-permute-start.5 = (f32[8,8,256]{2,1,0:T(8,128)S(1)}, f32[8,8,256]{2,1,0:T(8,128)S(1)}, u32[]{:S(2)}, u32[]{:S(2)}) collective-permute-start(f32[8,8,256]{2,1,0:T(8,128)S(1)} %get-tuple-element.55), channel_id=1, source_target_pairs={{0,31},{1,0},{2,1},{3,2},{4,3},{5,4},{6,5},{7,6},{8,7},{9,8},{10,9... | collective-permute-start | bytes 196616 | tf_op jit(solution)/shard_map/ppermute | solution.py:432
  6.5 9.1 %collective-permute-start.4 = (f32[8,8,256]{2,1,0:T(8,128)S(1)}, f32[8,8,256]{2,1,0:T(8,128)S(1)}, u32[]{:S(2)}, u32[]{:S(2)}) collective-permute-start(f32[8,8,256]{2,1,0:T(8,128)S(1)} %get-tuple-element.56), channel_id=1, source_target_pairs={{0,1},{1,2},{2,3},{3,4},{4,5},{5,6},{6,7},{7,8},{8,9},{9,10},{10,1... | collective-permute-start | bytes 196616 | tf_op jit(solution)/shard_map/ppermute | solution.py:432
  23.3 2.0 %collective-permute-start.7 = (f32[6,24,128]{2,1,0:T(8,128)S(1)}, f32[6,24,128]{2,1,0:T(8,128)S(1)}, u32[]{:S(2)}, u32[]{:S(2)}) collective-permute-start(f32[6,24,128]{2,1,0:T(8,128)S(1)} %get-tuple-element.59), channel_id=1, source_target_pairs={{0,224},{32,0},{64,32},{96,64},{128,96},{160,128},{192,160},{224,1... | collective-permute-start | bytes 221192 | tf_op jit(solution)/shard_map/ppermute | solution.py:432
  23.3 3.8 %collective-permute-start.6 = (f32[6,24,128]{2,1,0:T(8,128)S(1)}, f32[6,24,128]{2,1,0:T(8,128)S(1)}, u32[]{:S(2)}, u32[]{:S(2)}) collective-permute-start(f32[6,24,128]{2,1,0:T(8,128)S(1)} %get-tuple-element.60), channel_id=1, source_target_pairs={{0,32},{32,64},{64,96},{96,128},{128,160},{160,192},{192,224},{224... | collective-permute-start | bytes 221192 | tf_op jit(solution)/shard_map/ppermute | solution.py:432
  27.1 4.9 %collective-permute-start.8 = (f32[28,8,128]{2,1,0:T(8,128)S(1)}, f32[28,8,128]{2,1,0:T(8,128)S(1)}, u32[]{:S(2)}, u32[]{:S(2)}) collective-permute-start(f32[28,8,128]{2,1,0:T(8,128)S(1)} %pad_maximum_fusion.4), channel_id=1, source_target_pairs={{0,1},{1,2},{2,3},{3,4},{4,5},{5,6},{6,7},{7,8},{8,9},{9,10},{10,1... | collective-permute-start | bytes 344072 | tf_op jit(solution)/shard_map/ppermute | solution.py:432
  27.4 7.0 %collective-permute-start.9 = (f32[28,8,128]{2,1,0:T(8,128)S(1)}, f32[28,8,128]{2,1,0:T(8,128)S(1)}, u32[]{:S(2)}, u32[]{:S(2)}) collective-permute-start(f32[28,8,128]{2,1,0:T(8,128)S(1)} %pad_maximum_fusion.5), channel_id=1, source_target_pairs={{0,31},{1,0},{2,1},{3,2},{4,3},{5,4},{6,5},{7,6},{8,7},{9,8},{10,9... | collective-permute-start | bytes 344072 | tf_op jit(solution)/shard_map/ppermute | solution.py:432
  38.8 1.9 %collective-permute-start.11 = (f32[8,16,128]{2,1,0:T(8,128)S(1)}, f32[8,16,128]{2,1,0:T(8,128)S(1)}, u32[]{:S(2)}, u32[]{:S(2)}) collective-permute-start(f32[8,16,128]{2,1,0:T(8,128)S(1)} %get-tuple-element.27.refs_0_), channel_id=1, source_target_pairs={{0,224},{32,0},{64,32},{96,64},{128,96},{160,128},{192,160},{224,1... | collective-permute-start | bytes 196616 | tf_op jit(solution)/shard_map/ppermute | solution.py:432
  38.9 3.7 %collective-permute-start.10 = (f32[8,16,128]{2,1,0:T(8,128)S(1)}, f32[8,16,128]{2,1,0:T(8,128)S(1)}, u32[]{:S(2)}, u32[]{:S(2)}) collective-permute-start(f32[8,16,128]{2,1,0:T(8,128)S(1)} %get-tuple-element.27.refs_0_), channel_id=1, source_target_pairs={{0,32},{32,64},{64,96},{96,128},{128,160},{160,192},{192,224},{224... | collective-permute-start | bytes 196616 | tf_op jit(solution)/shard_map/ppermute | solution.py:432
  42.6 5.5 %collective-permute-start.12 = (f32[24,8,128]{2,1,0:T(8,128)S(1)}, f32[24,8,128]{2,1,0:T(8,128)S(1)}, u32[]{:S(2)}, u32[]{:S(2)}) collective-permute-start(f32[24,8,128]{2,1,0:T(8,128)S(1)} %pad_maximum_fusion.6), channel_id=1, source_target_pairs={{0,1},{1,2},{2,3},{3,4},{4,5},{5,6},{6,7},{7,8},{8,9},{9,10},{10,1... | collective-permute-start | bytes 294920 | tf_op jit(solution)/shard_map/ppermute | solution.py:432
  42.9 6.8 %collective-permute-start.13 = (f32[24,8,128]{2,1,0:T(8,128)S(1)}, f32[24,8,128]{2,1,0:T(8,128)S(1)}, u32[]{:S(2)}, u32[]{:S(2)}) collective-permute-start(f32[24,8,128]{2,1,0:T(8,128)S(1)} %pad_maximum_fusion.7), channel_id=1, source_target_pairs={{0,31},{1,0},{2,1},{3,2},{4,3},{5,4},{6,5},{7,6},{8,7},{9,8},{10,9... | collective-permute-start | bytes 294920 | tf_op jit(solution)/shard_map/ppermute | solution.py:432
  53.5 4.7 %collective-permute-start.14 = (f32[3,8,128]{2,1,0:T(8,128)S(1)}, f32[3,8,128]{2,1,0:T(8,128)S(1)}, u32[]{:S(2)}, u32[]{:S(2)}) collective-permute-start(f32[3,8,128]{2,1,0:T(8,128)S(1)} %get-tuple-element.28), channel_id=1, source_target_pairs={{0,64},{32,96},{64,128},{96,160},{128,192},{160,224},{192,0},{224,... | collective-permute-start | bytes 36872 | tf_op jit(solution)/shard_map/ppermute | solution.py:432
  56.8 4.9 %collective-permute-start.15 = (f32[3,8,128]{2,1,0:T(8,128)S(1)}, f32[3,8,128]{2,1,0:T(8,128)S(1)}, u32[]{:S(2)}, u32[]{:S(2)}) collective-permute-start(f32[3,8,128]{2,1,0:T(8,128)S(1)} %get-tuple-element.28), channel_id=1, source_target_pairs={{0,192},{32,224},{64,0},{96,32},{128,64},{160,96},{192,128},{224,1... | collective-permute-start | bytes 36872 | tf_op jit(solution)/shard_map/ppermute | solution.py:432
  61.7 18.3 %collective-permute-start.19 = (f32[3,24,128]{2,1,0:T(8,128)S(1)}, f32[3,24,128]{2,1,0:T(8,128)S(1)}, u32[]{:S(2)}, u32[]{:S(2)}) collective-permute-start(f32[3,24,128]{2,1,0:T(8,128)S(1)} %constant_dynamic-update-slice_fusion.refs_2_), channel_id=1, source_target_pairs={{0,28},{1,29},{2,30},{3,31},{4,0},{5,1},{6,2},{7,3},{8,4},{9,5},{1... | collective-permute-start | bytes 110600 | tf_op jit(solution)/shard_map/ppermute | solution.py:432
  75.9 6.3 %collective-permute-start.18 = (f32[3,24,128]{2,1,0:T(8,128)S(1)}, f32[3,24,128]{2,1,0:T(8,128)S(1)}, u32[]{:S(2)}, u32[]{:S(2)}) collective-permute-start(f32[3,24,128]{2,1,0:T(8,128)S(1)} %constant_dynamic-update-slice_fusion.refs_2_), channel_id=1, source_target_pairs={{0,30},{1,31},{2,0},{3,1},{4,2},{5,3},{6,4},{7,5},{8,6},{9,7},{10,... | collective-permute-start | bytes 110600 | tf_op jit(solution)/shard_map/ppermute | solution.py:432
  75.9 6.3 %collective-permute-start.17 = (f32[3,24,128]{2,1,0:T(8,128)S(1)}, f32[3,24,128]{2,1,0:T(8,128)S(1)}, u32[]{:S(2)}, u32[]{:S(2)}) collective-permute-start(f32[3,24,128]{2,1,0:T(8,128)S(1)} %constant_dynamic-update-slice_fusion.refs_2_), channel_id=1, source_target_pairs={{0,2},{1,3},{2,4},{3,5},{4,6},{5,7},{6,8},{7,9},{8,10},{9,11},{10,... | collective-permute-start | bytes 110600 | tf_op jit(solution)/shard_map/ppermute | solution.py:432
  80.0 10.0 %collective-permute-start.16 = (f32[3,24,128]{2,1,0:T(8,128)S(1)}, f32[3,24,128]{2,1,0:T(8,128)S(1)}, u32[]{:S(2)}, u32[]{:S(2)}) collective-permute-start(f32[3,24,128]{2,1,0:T(8,128)S(1)} %constant_dynamic-update-slice_fusion.refs_2_), channel_id=1, source_target_pairs={{0,4},{1,5},{2,6},{3,7},{4,8},{5,9},{6,10},{7,11},{8,12},{9,13},{1... | collective-permute-start | bytes 110600 | tf_op jit(solution)/shard_map/ppermute | solution.py:432

commit v3 on v2

--- a/solution.py
+++ b/solution.py
@@ -156,10 +156,23 @@
     return select_matrix((128, lanes_out), lambda r, c: ((c >> 1) + offset == r) & ((c >> 1) < planes))
 
 
-def level0_kernel(lv, src, dens, lo, hi, from_left, from_right, corner_left, corner_right, packed, v, rhs, sx, sy, sz, coef,
+def chooser(axis, step=1):
+    odd = is_odd(axis, step)
+    return lambda a, b: (jnp.where(odd, a, b), jnp.where(odd, b, a))
+
+
+def halo_readers(rows0, rows1):
+    choose = chooser("px")
+    lo = lambda i: choose(rows0[i], rows1[i])[0]
+    hi = lambda i: choose(rows0[i], rows1[i])[1]
+    return lo, hi, chooser("py")
+
+
+def level0_kernel(lv, src, dens, rows0, rows1, sides0, sides1, corners0, corners1, packed, v, rhs, sx, sy, sz, coef,
                   mob, first, diag, pair, low):
     h = lv.halo
     tile = iota((8, lv.lanes), 0)
+    lo, hi, choose = halo_readers(rows0, rows1)
 
     def load(i, s, d, a, b):
         rhs[i, 0:16] = 2.0 * s
@@ -168,11 +181,14 @@
         mob[i, 16:24] = 1.0 / pltpu.roll(jnp.where(tile < 4, b, a), 4, 0)
 
     for i in range(h):
-        load(i, lo[i], lo[h + i], corner_right[i], corner_left[i])
-        load(lv.total - h + i, hi[i], hi[h + i], corner_right[h + i], corner_left[h + i])
+        left_side, right_side = choose(corners0[i], corners1[i])
+        load(i, lo(i), lo(h + i), right_side, left_side)
+        left_side, right_side = choose(corners0[h + i], corners1[h + i])
+        load(lv.total - h + i, hi(i), hi(h + i), right_side, left_side)
 
     def body(i, carry):
-        load(h + i, src[i], dens[i], from_right[i], from_left[i])
+        left_side, right_side = choose(sides0[i], sides1[i])
+        load(h + i, src[i], dens[i], right_side, left_side)
         return carry
 
     lax.fori_loop(0, lv.rows, body, 0, unroll=UNROLL)
@@ -208,15 +224,16 @@
         packed[k, 16:24] = jnp.where((at < 2) | (at >= 6), m, e)
 
 
-def level1_kernel(lv, own, lo, hi, from_left, from_right, packed, v, rhs, sx, sy, sz, coef,
+def level1_kernel(lv, own, rows0, rows1, sides0, sides1, packed, v, rhs, sx, sy, sz, coef,
                   mob, first, diag, pair, low):
     h = lv.halo
 
     at = iota((8, lv.lanes), 0)
+    lo, hi, choose = halo_readers(rows0, rows1)
 
     def load(i, block):
         t0, t1, t2 = block[0:8], block[8:16], block[16:24]
-        a, b = from_right[i], from_left[i]
+        b, a = choose(sides0[i], sides1[i])
         rhs[i, 0:8] = jnp.where(at < 4, t1, pltpu.roll(t0, 4, 0))
         rhs[i, 8:16] = a
         rhs[i, 16:24] = pltpu.roll(b, 4, 0)
@@ -227,8 +244,8 @@
         mob[i, 16:24] = jnp.where(at < 6, far, pltpu.roll(t2, 2, 0))
 
     for i in range(h):
-        load(i, lo[i])
-        load(lv.total - h + i, hi[i])
+        load(i, lo(i))
+        load(lv.total - h + i, hi(i))
 
     def body(i, carry):
         load(h + i, own[i])
@@ -259,23 +276,25 @@
         packed[k, 0:4] = low[pl.ds(a + 16, 4, stride=2)] + low[pl.ds(a + 17, 4, stride=2)]
 
 
-def level2_kernel(lv, own, lo, hi, from_left, from_right, packed, v, rhs, sx, sy, sz, coef,
+def level2_kernel(lv, own, rows0, rows1, sides0, sides1, packed, v, rhs, sx, sy, sz, coef,
                   mob, first, diag, pair, wide):
     h = lv.halo
     tile = iota((8, 128), 0)
     lane = iota((8, 128), 1) < lv.planes
+    lo, hi, choose = halo_readers(rows0, rows1)
 
     def load(i, block):
-        r = pltpu.roll(from_right[i], 4, 0)
-        parts = (jnp.where(tile < 4, block, r), r, from_left[i])
+        l, r = choose(sides0[i], sides1[i])
+        r = pltpu.roll(r, 4, 0)
+        parts = (jnp.where(tile < 4, block, r), r, l)
         for k, part in enumerate(parts):
             rhs[i, 8 * k : 8 * k + 8] = jnp.where(lane, part, 0.0)
             mob[i, 8 * k : 8 * k + 8] = jnp.where(lane, pltpu.roll(part, 64, 1), 1.0)
 
     for i in range(h):
-        load(i, lo[i, 8:16])
+        load(i, lo(i)[8:16])
         load(h + i, own[i, 8:16])
-        load(2 * h + i, hi[i, 8:16])
+        load(2 * h + i, hi(i)[8:16])
     zero = jnp.zeros((W, lv.lanes), F32)
     for ref in (first, v):
         ref[0] = zero
@@ -358,12 +377,22 @@
         out[k] = v[k]
 
 
-def ascent_kernel(levels, g0, g1, g2, g3, g4, *refs):
+def ascent_kernel(levels, own, near0, near1, far0, far1, *refs):
     fields = [refs[6 * k : 6 * k + 6] for k in range(3)]
     result = refs[18]
     e3, p2, a2, b2, p1, q1, a1, b1, p0, q0, a0 = refs[19:]
     lv0, lv1, lv2 = levels
-    coarse_solve([g0, g1, g2, g3, g4], lv2.nrows // 2, lv2.ncols // 2, e3)
+    position, count = lax.axis_index("py"), lax.axis_size("py")
+
+    def outer(pair, step):
+        prev, nxt = chooser("py", step)(pair[0][...], pair[1][...])
+        turn = lambda t: pltpu.roll(t, 64, 2)
+        prev = jnp.where(position < step, turn(prev), prev)
+        return prev, jnp.where(position >= count - step, turn(nxt), nxt)
+
+    before, after = outer((near0, near1), 2)
+    first, last = outer((far0, far1), 4)
+    coarse_solve([first, before, own[...], after, last], lv2.nrows // 2, lv2.ncols // 2, e3)
 
     p2[...] = jnp.zeros(p2.shape, F32)
     two = p2.reshape(8 * W, 128)
@@ -427,9 +456,41 @@
     return outs[0], outs[1:]
 
 
-def ring(x, axis, step):
-    n = lax.axis_size(axis)
-    return lax.ppermute(x, axis, [(i, (i + step) % n) for i in range(n)])
+def is_odd(axis, step):
+    return (lax.axis_index(axis) // step) % 2 == 1
+
+
+def swap_partners(n, step, parity):
+    partner = list(range(n))
+    for i in range(n - step):
+        if (i // step) % 2 == parity:
+            partner[i], partner[i + step] = i + step, i
+    alone = [i for i in range(n) if partner[i] == i]
+    for group in (alone[:step], alone[step:]):
+        for i, j in zip(group, reversed(group)):
+            partner[i] = j
+    return partner
+
+
+def exchange(to_prev, to_next, odd, axis, step=1):
+    n, other = lax.axis_size(axis), "py" if axis == "px" else "px"
+    got = []
+    for parity in range(2):
+        partner = swap_partners(n, step, parity)
+        pairs = []
+        for i in range(n):
+            for j in range(lax.axis_size(other)):
+                a, b = (i, j), (partner[i], j if partner[i] != i else j ^ 1)
+                if axis == "py":
+                    a, b = a[::-1], b[::-1]
+                pairs.append(tuple(p * lax.axis_size("py") + q for p, q in (a, b)))
+        out = to_next if to_prev is to_next else jnp.where(odd == (parity == 0), to_prev, to_next)
+        got.append(lax.ppermute(out, ("px", "py"), pairs))
+    return got
+
+
+def pick(got, odd):
+    return jnp.where(odd, got[0], got[1]), jnp.where(odd, got[1], got[0])
 
 
 def per_device(source, density):
@@ -438,45 +499,56 @@
     lv1 = Level(16, 6, 8, 8, 128, 128, 16 * npx, 8 * npy)
     lv2 = Level(8, 8, 4, 8, 128, 64, 8 * npx, 4 * npy)
 
+    x, step_rows = lax.axis_index("px"), 2
+    flags = (
+        is_odd("px", 1), is_odd("py", 1), is_odd("px", step_rows),
+        x < step_rows, x >= npx - step_rows,
+    )
+    source, density, (odd_x, odd_y, odd_2, first_x, last_x) = lax.optimization_barrier(
+        (source, density, flags)
+    )
+
     h = lv0.halo
-    lo = ring(jnp.concatenate([source[-h:], density[-h:]], 0), "px", 1)
-    hi = ring(jnp.concatenate([source[:h], density[:h]], 0), "px", -1)
+    rows = exchange(
+        jnp.concatenate([source[:h], density[:h]], 0),
+        jnp.concatenate([source[-h:], density[-h:]], 0), odd_x, "px",
+    )
+    lo, hi = pick(rows, odd_x)
     to_right = lambda s, d: jnp.concatenate([d[:, 12:16], s[:, 12:16]], 1)
     to_left = lambda s, d: jnp.concatenate([s[:, 0:4], d[:, 0:4]], 1)
-    from_left = ring(to_right(source, density), "py", 1)
-    from_right = ring(to_left(source, density), "py", -1)
+    sides = exchange(to_left(source, density), to_right(source, density), odd_y, "py")
     row_source = jnp.concatenate([lo[:h], hi[:h]], 0)
     row_density = jnp.concatenate([lo[h:], hi[h:]], 0)
-    corner_left = ring(to_right(row_source, row_density), "py", 1)
-    corner_right = ring(to_left(row_source, row_density), "py", -1)
+    corners = exchange(
+        to_left(row_source, row_density), to_right(row_source, row_density), odd_y, "py"
+    )
     one, saved0 = descend(
-        level0_kernel, lv0, (source, density, lo, hi, from_left, from_right, corner_left, corner_right),
-        (16, W, 128),
-        [(16, W, 256), (16 * W, 128)],
+        level0_kernel, lv0, (source, density, *rows, *sides, *corners),
+        (16, W, 128), [(16, W, 256), (16 * W, 128)],
     )
 
     h = lv1.halo
-    lo = ring(one[-h:], "px", 1)
-    hi = ring(one[:h], "px", -1)
+    rows = exchange(one[:h], one[-h:], odd_x, "px")
+    lo, hi = pick(rows, odd_x)
     wide = lambda a: jnp.concatenate([lo[:, a : a + 8], one[:, a : a + 8], hi[:, a : a + 8]], 0)
-    from_left = ring(wide(0), "py", 1)
-    from_right = ring(wide(8), "py", -1)
+    sides = exchange(wide(8), wide(0), odd_y, "py")
     two, saved1 = descend(
-        level1_kernel, lv1, (one, lo, hi, from_left, from_right), (8, 16, 128),
-        [(8, W, 128), (8 * W, 128)],
-    )
-
-    lo = ring(two, "px", 1)
-    hi = ring(two, "px", -1)
-    from_left = ring(jnp.concatenate([lo[:, :8], two[:, :8], hi[:, :8]], 0), "py", 1)
-    from_right = ring(jnp.concatenate([lo[:, 8:], two[:, 8:], hi[:, 8:]], 0), "py", -1)
+        level1_kernel, lv1, (one, *rows, *sides), (8, 16, 128), [(8, W, 128), (8 * W, 128)],
+    )
+
+    rows = exchange(two, two, odd_x, "px")
+    lo, hi = pick(rows, odd_x)
+    wide = lambda a: jnp.concatenate([lo[:, a : a + 8], two[:, a : a + 8], hi[:, a : a + 8]], 0)
+    sides = exchange(wide(8), wide(0), odd_y, "py")
     three, saved2 = descend(
-        level2_kernel, lv2, (two, lo, hi, from_left, from_right), (3, 8, 128),
-        [(8, W, 128), (16, W, 128)],
-    )
-
-    wide = jnp.concatenate([ring(three, "px", 2), three, ring(three, "px", -2)], 1)
-    groups = [ring(wide, "py", 4), ring(wide, "py", 2), wide, ring(wide, "py", -2), ring(wide, "py", -4)]
+        level2_kernel, lv2, (two, *rows, *sides), (3, 8, 128), [(8, W, 128), (16, W, 128)],
+    )
+
+    lo, hi = pick(exchange(three, three, odd_2, "px", step_rows), odd_2)
+    turn = lambda t: jnp.concatenate([t[:, 4:], t[:, :4]], 1)
+    lo, hi = jnp.where(first_x, turn(lo), lo), jnp.where(last_x, turn(hi), hi)
+    wide = jnp.concatenate([lo, three, hi], 1)
+    groups = (wide, *exchange(wide, wide, None, "py", 2), *exchange(wide, wide, None, "py", 4))
     inputs = (*groups, *saved0, *saved1, *saved2)
     shapes = [(5, W, 128), (8, W, 128), (24, W, 128), (24, W, 128), (12, W, 128), (12, W, 128),
               (28, W, 128), (28, W, 128), (18, W, 128), (18, W, 256), (40, W, 256)]

time: 98.6 us -> 84.6 us (0.86)
  the two profiles are of different devices: /device:TPU:120 before, /device:TPU:10 now
where the time goes in v3:
time: 84.6 us; the launch traced here: 84.5 us
  waiting for transfers between devices  28.9 us (34%)
  starting transfers between devices  28.7 us (34%)
  Pallas kernels  24.3 us (29%)
  local copies, waits for them, and re-layouts  2 us (2%)
    ppermute x20, waiting for transfers between devices, exchange(): got.append(lax.ppermute(out, ('px', 'py'), pairs))  28.9 us
    ppermute x20, starting transfers between devices, exchange(): got.append(lax.ppermute(out, ('px', 'py'), pairs))  28.7 us
    pallas_call x3, Pallas kernels, descend(): pl.pallas_call(lambda *refs: kernel(lv, *refs), out_shape=[jax.ShapeDtype...  15.7 us
    pallas_call x1, Pallas kernels, per_device(): pl.pallas_call(lambda *refs: ascent_kernel((lv0, lv1, lv2), *refs), out_s...  8.59 us
  transfers between devices with their start and end apart: 20, of which 12 were waited for; matrix products, arithmetic and copies ran while one was open for 0% of the time, Pallas kernels for 0%

profile of v3, /device:TPU:10, one launch (start us, length us, event | category | flops | bytes accessed | tf_op | source)
XLA Modules:
  0.0 84.5 jit_solution(9561742200971441418)
XLA Ops:
  2.0 1.7 %collective-permute-start = (f32[8,16,256]{2,1,0:T(8,128)S(1)}, f32[8,16,256]{2,1,0:T(8,128)S(1)}, u32[]{:S(2)}, u32[]{:S(2)}) collective-permute-start(f32[8,16,256]{2,1,0:T(8,128)S(1)} %get-tuple-element.77), channel_id=1, source_target_pairs={{0,32},{1,33},{2,34},{3,35},{4,36},{5,37},{6,38},{7,39},{8,40},{9,... | collective-permute-start | bytes 393224 | tf_op jit(solution)/shard_map/ppermute | solution.py:488
  3.9 5.9 %collective-permute-start.3 = (f32[32,8,256]{2,1,0:T(8,128)S(1)}, f32[32,8,256]{2,1,0:T(8,128)S(1)}, u32[]{:S(2)}, u32[]{:S(2)}) collective-permute-start(f32[32,8,256]{2,1,0:T(8,128)S(1)} %get-tuple-element.64), channel_id=1, source_target_pairs={{0,32},{32,0},{64,96},{96,64},{128,160},{160,128},{192,224},{224,1... | collective-permute-start | bytes 786440 | tf_op jit(solution)/shard_map/ppermute | solution.py:488
  10.0 2.1 %collective-permute-start.4 = (f32[8,8,256]{2,1,0:T(8,128)S(1)}, f32[8,8,256]{2,1,0:T(8,128)S(1)}, u32[]{:S(2)}, u32[]{:S(2)}) collective-permute-start(f32[8,8,256]{2,1,0:T(8,128)S(1)} %broadcast_select_fusion.7), channel_id=1, source_target_pairs={{0,1},{32,33},{64,65},{96,97},{128,129},{160,161},{192,193},{224,2... | collective-permute-start | bytes 196616 | tf_op jit(solution)/shard_map/ppermute | solution.py:488
  12.1 1.3 %collective-permute-start.5 = (f32[8,8,256]{2,1,0:T(8,128)S(1)}, f32[8,8,256]{2,1,0:T(8,128)S(1)}, u32[]{:S(2)}, u32[]{:S(2)}) collective-permute-start(f32[8,8,256]{2,1,0:T(8,128)S(1)} %get-tuple-element.61), channel_id=1, source_target_pairs={{0,32},{32,0},{64,96},{96,64},{128,160},{160,128},{192,224},{224,1... | collective-permute-start | bytes 196616 | tf_op jit(solution)/shard_map/ppermute | solution.py:488
  13.4 5.8 %collective-permute-done.4.refs_6_ = f32[8,8,256]{2,1,0:T(8,128)S(1)} collective-permute-done((f32[8,8,256]{2,1,0:T(8,128)S(1)}, f32[8,8,256]{2,1,0:T(8,128)S(1)}, u32[]{:S(2)}, u32[]{:S(2)}) %collective-permute-start.4) | collective-permute-done | bytes 65568 | tf_op jit(solution)/shard_map/ppermute | solution.py:488
  19.2 7.6 %descent.3 = (f32[16,24,128]{2,1,0:T(8,128)S(1)}, f32[40,24,256]{2,1,0:T(8,128)S(1)}, f32[40,24,256]{2,1,0:T(8,128)S(1)}, f32[40,24,256]{2,1,0:T(8,128)S(1)}, f3...) custom-call(f32[32,16,256]{2,1,0:T(8,128)S(1)} %copy-done, ...), custom_call_target="tpu_custom_call" | custom-call | tf_op jit(solution)/shard_map/descent/pallas_call | solution.py:447
  26.9 1.4 %collective-permute-start.6 = (f32[6,24,128]{2,1,0:T(8,128)S(1)}, f32[6,24,128]{2,1,0:T(8,128)S(1)}, u32[]{:S(2)}, u32[]{:S(2)}) collective-permute-start(f32[6,24,128]{2,1,0:T(8,128)S(1)} %get-tuple-element.85), channel_id=1, source_target_pairs={{0,32},{1,33},{2,34},{3,35},{4,36},{5,37},{6,38},{7,39},{8,40},{9,... | collective-permute-start | bytes 221192 | tf_op jit(solution)/shard_map/ppermute | solution.py:488
  28.3 2.4 %collective-permute-done.7.refs_2_ = f32[6,24,128]{2,1,0:T(8,128)S(1)} collective-permute-done((f32[6,24,128]{2,1,0:T(8,128)S(1)}, f32[6,24,128]{2,1,0:T(8,128)S(1)}, u32[]{:S(2)}, u32[]{:S(2)}) %collective-permute-start.7) | collective-permute-done | bytes 73760 | tf_op jit(solution)/shard_map/ppermute | solution.py:488
  30.7 2.5 %collective-permute-start.9 = (f32[28,8,128]{2,1,0:T(8,128)S(1)}, f32[28,8,128]{2,1,0:T(8,128)S(1)}, u32[]{:S(2)}, u32[]{:S(2)}) collective-permute-start(f32[28,8,128]{2,1,0:T(8,128)S(1)} %get-tuple-element.78), channel_id=1, source_target_pairs={{0,32},{32,0},{64,96},{96,64},{128,160},{160,128},{192,224},{224,1... | collective-permute-start | bytes 344072 | tf_op jit(solution)/shard_map/ppermute | solution.py:488
  33.2 4.7 %collective-permute-done.9.refs_4_ = f32[28,8,128]{2,1,0:T(8,128)S(1)} collective-permute-done((f32[28,8,128]{2,1,0:T(8,128)S(1)}, f32[28,8,128]{2,1,0:T(8,128)S(1)}, u32[]{:S(2)}, u32[]{:S(2)}) %collective-permute-start.9) | collective-permute-done | bytes 114720 | tf_op jit(solution)/shard_map/ppermute | solution.py:488
  38.0 4.3 %descent.4 = (f32[8,16,128]{2,1,0:T(8,128)S(1)}, f32[28,24,128]{2,1,0:T(8,128)S(1)}, f32[28,24,128]{2,1,0:T(8,128)S(1)}, f32[28,24,128]{2,1,0:T(8,128)S(1)}, f32...) custom-call(f32[16,24,128]{2,1,0:T(8,128)S(1)} %get-tuple-element.39.refs_0_, ...), custom_call_target="tpu_custom_call" | custom-call | tf_op jit(solution)/shard_map/descent/pallas_call | solution.py:447
  42.4 1.4 %collective-permute-start.10 = (f32[8,16,128]{2,1,0:T(8,128)S(1)}, f32[8,16,128]{2,1,0:T(8,128)S(1)}, u32[]{:S(2)}, u32[]{:S(2)}) collective-permute-start(f32[8,16,128]{2,1,0:T(8,128)S(1)} %get-tuple-element.40.refs_0_), channel_id=1, source_target_pairs={{0,32},{1,33},{2,34},{3,35},{4,36},{5,37},{6,38},{7,39},{8,40},{9,... | collective-permute-start | bytes 196616 | tf_op jit(solution)/shard_map/ppermute | solution.py:488
  43.8 2.3 %collective-permute-done.11.refs_2_ = f32[8,16,128]{2,1,0:T(8,128)S(1)} collective-permute-done((f32[8,16,128]{2,1,0:T(8,128)S(1)}, f32[8,16,128]{2,1,0:T(8,128)S(1)}, u32[]{:S(2)}, u32[]{:S(2)}) %collective-permute-start.11) | collective-permute-done | bytes 65568 | tf_op jit(solution)/shard_map/ppermute | solution.py:488
  46.2 2.4 %collective-permute-start.13 = (f32[24,8,128]{2,1,0:T(8,128)S(1)}, f32[24,8,128]{2,1,0:T(8,128)S(1)}, u32[]{:S(2)}, u32[]{:S(2)}) collective-permute-start(f32[24,8,128]{2,1,0:T(8,128)S(1)} %get-tuple-element.80), channel_id=1, source_target_pairs={{0,32},{32,0},{64,96},{96,64},{128,160},{160,128},{192,224},{224,1... | collective-permute-start | bytes 294920 | tf_op jit(solution)/shard_map/ppermute | solution.py:488
  48.6 4.4 %collective-permute-done.13.refs_4_ = f32[24,8,128]{2,1,0:T(8,128)S(1)} collective-permute-done((f32[24,8,128]{2,1,0:T(8,128)S(1)}, f32[24,8,128]{2,1,0:T(8,128)S(1)}, u32[]{:S(2)}, u32[]{:S(2)}) %collective-permute-start.13) | collective-permute-done | bytes 98336 | tf_op jit(solution)/shard_map/ppermute | solution.py:488
  53.2 3.8 %descent.5 = (f32[3,8,128]{2,1,0:T(8,128)S(1)}, f32[24,24,128]{2,1,0:T(8,128)S(1)}, f32[24,24,128]{2,1,0:T(8,128)S(1)}, f32[24,24,128]{2,1,0:T(8,128)S(1)}, f32[...) custom-call(f32[8,16,128]{2,1,0:T(8,128)S(1)} %get-tuple-element.40.refs_0_, ...), custom_call_target="tpu_custom_call" | custom-call | tf_op jit(solution)/shard_map/descent/pallas_call | solution.py:447
  57.0 1.2 %collective-permute-start.15 = (f32[3,8,128]{2,1,0:T(8,128)S(1)}, f32[3,8,128]{2,1,0:T(8,128)S(1)}, u32[]{:S(2)}, u32[]{:S(2)}) collective-permute-start(f32[3,8,128]{2,1,0:T(8,128)S(1)} %get-tuple-element.41), channel_id=1, source_target_pairs={{0,32},{1,33},{2,34},{3,35},{4,36},{5,37},{6,38},{7,39},{8,40},{9,... | collective-permute-start | bytes 36872 | tf_op jit(solution)/shard_map/ppermute | solution.py:488
  58.6 2.2 %collective-permute-done.15 = f32[3,8,128]{2,1,0:T(8,128)S(1)} collective-permute-done((f32[3,8,128]{2,1,0:T(8,128)S(1)}, f32[3,8,128]{2,1,0:T(8,128)S(1)}, u32[]{:S(2)}, u32[]{:S(2)}) %collective-permute-start.15) | collective-permute-done | bytes 12320 | tf_op jit(solution)/shard_map/ppermute | solution.py:488
  60.8 1.1 %collective-permute-done.14 = f32[3,8,128]{2,1,0:T(8,128)S(1)} collective-permute-done((f32[3,8,128]{2,1,0:T(8,128)S(1)}, f32[3,8,128]{2,1,0:T(8,128)S(1)}, u32[]{:S(2)}, u32[]{:S(2)}) %collective-permute-start.14) | collective-permute-done | bytes 12320 | tf_op jit(solution)/shard_map/ppermute | solution.py:488
  61.9 1.6 %collective-permute-start.19 = (f32[3,24,128]{2,1,0:T(8,128)S(1)}, f32[3,24,128]{2,1,0:T(8,128)S(1)}, u32[]{:S(2)}, u32[]{:S(2)}) collective-permute-start(f32[3,24,128]{2,1,0:T(8,128)S(1)} %pad_maximum_fusion.10.refs_0_), channel_id=1, source_target_pairs={{0,3},{32,35},{64,67},{96,99},{128,131},{160,163},{192,195},{224,2... | collective-permute-start | bytes 110600 | tf_op jit(solution)/shard_map/ppermute | solution.py:488
  63.6 5.3 %collective-permute-start.18 = (f32[3,24,128]{2,1,0:T(8,128)S(1)}, f32[3,24,128]{2,1,0:T(8,128)S(1)}, u32[]{:S(2)}, u32[]{:S(2)}) collective-permute-start(f32[3,24,128]{2,1,0:T(8,128)S(1)} %pad_maximum_fusion.10.refs_0_), channel_id=1, source_target_pairs={{0,4},{32,36},{64,68},{96,100},{128,132},{160,164},{192,196},{224,... | collective-permute-start | bytes 110600 | tf_op jit(solution)/shard_map/ppermute | solution.py:488
  68.9 1.2 %collective-permute-start.16 = (f32[3,24,128]{2,1,0:T(8,128)S(1)}, f32[3,24,128]{2,1,0:T(8,128)S(1)}, u32[]{:S(2)}, u32[]{:S(2)}) collective-permute-start(f32[3,24,128]{2,1,0:T(8,128)S(1)} %pad_maximum_fusion.10.refs_0_), channel_id=1, source_target_pairs={{0,2},{32,34},{64,66},{96,98},{128,130},{160,162},{192,194},{224,2... | collective-permute-start | bytes 110600 | tf_op jit(solution)/shard_map/ppermute | solution.py:488
  71.8 4.1 %collective-permute-done.17.refs_2_ = f32[3,24,128]{2,1,0:T(8,128)S(1)} collective-permute-done((f32[3,24,128]{2,1,0:T(8,128)S(1)}, f32[3,24,128]{2,1,0:T(8,128)S(1)}, u32[]{:S(2)}, u32[]{:S(2)}) %collective-permute-start.17) | collective-permute-done | bytes 36896 | tf_op jit(solution)/shard_map/ppermute | solution.py:488
  75.9 8.6 %ascent.1 = f32[32,16,256]{2,1,0:T(8,128)} custom-call(f32[3,24,128]{2,1,0:T(8,128)S(1)} %pad_maximum_fusion.10.refs_0_, f32[3,24,128]{2,1,0:T(8,128)S(1)} %collective-permute-done.16.refs_1_, f32[3,24,128]{2,1,0:T(8,128)S(1)} %collective-permute-done.17.refs_2_, f32[3,24,128]{2,1,0:T(8,128)S(1)} %collective-permute-done.18.refs_3_, ...), custom_call_target="tpu_custom_call" | custom-call | tf_op jit(solution)/shard_map/ascent/pallas_call | solution.py:555
  (51 shorter events, 5.0 us)
Async XLA Ops:
  0.0 3.7 %copy-start = (f32[32,16,256]{2,1,0:T(8,128)S(1)}, f32[32,16,256]{2,1,0:T(8,128)}, u32[]{:S(2)}) copy-start(f32[32,16,256]{2,1,0:T(8,128)} %refs_0_) | copy-start | bytes 1572868
  1.8 1.9 %copy-start.1 = (f32[32,16,256]{2,1,0:T(8,128)S(1)}, f32[32,16,256]{2,1,0:T(8,128)}, u32[]{:S(2)}) copy-start(f32[32,16,256]{2,1,0:T(8,128)} %refs_1_) | copy-start | bytes 1572868
  1.9 7.9 %collective-permute-start.1 = (f32[8,16,256]{2,1,0:T(8,128)S(1)}, f32[8,16,256]{2,1,0:T(8,128)S(1)}, u32[]{:S(2)}, u32[]{:S(2)}) collective-permute-start(f32[8,16,256]{2,1,0:T(8,128)S(1)} %get-tuple-element.76), channel_id=1, source_target_pairs={{0,1},{1,0},{2,3},{3,2},{4,5},{5,4},{6,7},{7,6},{8,9},{9,8},{10,11... | collective-permute-start | bytes 393224 | tf_op jit(solution)/shard_map/ppermute | solution.py:488
  2.0 7.8 %collective-permute-start = (f32[8,16,256]{2,1,0:T(8,128)S(1)}, f32[8,16,256]{2,1,0:T(8,128)S(1)}, u32[]{:S(2)}, u32[]{:S(2)}) collective-permute-start(f32[8,16,256]{2,1,0:T(8,128)S(1)} %get-tuple-element.77), channel_id=1, source_target_pairs={{0,32},{1,33},{2,34},{3,35},{4,36},{5,37},{6,38},{7,39},{8,40},{9,... | collective-permute-start | bytes 393224 | tf_op jit(solution)/shard_map/ppermute | solution.py:488
  3.9 15.3 %collective-permute-start.3 = (f32[32,8,256]{2,1,0:T(8,128)S(1)}, f32[32,8,256]{2,1,0:T(8,128)S(1)}, u32[]{:S(2)}, u32[]{:S(2)}) collective-permute-start(f32[32,8,256]{2,1,0:T(8,128)S(1)} %get-tuple-element.64), channel_id=1, source_target_pairs={{0,32},{32,0},{64,96},{96,64},{128,160},{160,128},{192,224},{224,1... | collective-permute-start | bytes 786440 | tf_op jit(solution)/shard_map/ppermute | solution.py:488
  9.8 9.3 %collective-permute-start.2 = (f32[32,8,256]{2,1,0:T(8,128)S(1)}, f32[32,8,256]{2,1,0:T(8,128)S(1)}, u32[]{:S(2)}, u32[]{:S(2)}) collective-permute-start(f32[32,8,256]{2,1,0:T(8,128)S(1)} %get-tuple-element.65), channel_id=1, source_target_pairs={{0,1},{32,33},{64,65},{96,97},{128,129},{160,161},{192,193},{224,2... | collective-permute-start | bytes 786440 | tf_op jit(solution)/shard_map/ppermute | solution.py:488
  10.0 9.2 %collective-permute-start.4 = (f32[8,8,256]{2,1,0:T(8,128)S(1)}, f32[8,8,256]{2,1,0:T(8,128)S(1)}, u32[]{:S(2)}, u32[]{:S(2)}) collective-permute-start(f32[8,8,256]{2,1,0:T(8,128)S(1)} %broadcast_select_fusion.7), channel_id=1, source_target_pairs={{0,1},{32,33},{64,65},{96,97},{128,129},{160,161},{192,193},{224,2... | collective-permute-start | bytes 196616 | tf_op jit(solution)/shard_map/ppermute | solution.py:488
  12.1 7.1 %collective-permute-start.5 = (f32[8,8,256]{2,1,0:T(8,128)S(1)}, f32[8,8,256]{2,1,0:T(8,128)S(1)}, u32[]{:S(2)}, u32[]{:S(2)}) collective-permute-start(f32[8,8,256]{2,1,0:T(8,128)S(1)} %get-tuple-element.61), channel_id=1, source_target_pairs={{0,32},{32,0},{64,96},{96,64},{128,160},{160,128},{192,224},{224,1... | collective-permute-start | bytes 196616 | tf_op jit(solution)/shard_map/ppermute | solution.py:488
  26.8 3.9 %collective-permute-start.7 = (f32[6,24,128]{2,1,0:T(8,128)S(1)}, f32[6,24,128]{2,1,0:T(8,128)S(1)}, u32[]{:S(2)}, u32[]{:S(2)}) collective-permute-start(f32[6,24,128]{2,1,0:T(8,128)S(1)} %get-tuple-element.84), channel_id=1, source_target_pairs={{0,1},{1,0},{2,3},{3,2},{4,5},{5,4},{6,7},{7,6},{8,9},{9,8},{10,11... | collective-permute-start | bytes 221192 | tf_op jit(solution)/shard_map/ppermute | solution.py:488
  26.9 3.8 %collective-permute-start.6 = (f32[6,24,128]{2,1,0:T(8,128)S(1)}, f32[6,24,128]{2,1,0:T(8,128)S(1)}, u32[]{:S(2)}, u32[]{:S(2)}) collective-permute-start(f32[6,24,128]{2,1,0:T(8,128)S(1)} %get-tuple-element.85), channel_id=1, source_target_pairs={{0,32},{1,33},{2,34},{3,35},{4,36},{5,37},{6,38},{7,39},{8,40},{9,... | collective-permute-start | bytes 221192 | tf_op jit(solution)/shard_map/ppermute | solution.py:488
  30.7 7.2 %collective-permute-start.9 = (f32[28,8,128]{2,1,0:T(8,128)S(1)}, f32[28,8,128]{2,1,0:T(8,128)S(1)}, u32[]{:S(2)}, u32[]{:S(2)}) collective-permute-start(f32[28,8,128]{2,1,0:T(8,128)S(1)} %get-tuple-element.78), channel_id=1, source_target_pairs={{0,32},{32,0},{64,96},{96,64},{128,160},{160,128},{192,224},{224,1... | collective-permute-start | bytes 344072 | tf_op jit(solution)/shard_map/ppermute | solution.py:488
  33.2 4.8 %collective-permute-start.8 = (f32[28,8,128]{2,1,0:T(8,128)S(1)}, f32[28,8,128]{2,1,0:T(8,128)S(1)}, u32[]{:S(2)}, u32[]{:S(2)}) collective-permute-start(f32[28,8,128]{2,1,0:T(8,128)S(1)} %get-tuple-element.79), channel_id=1, source_target_pairs={{0,1},{32,33},{64,65},{96,97},{128,129},{160,161},{192,193},{224,2... | collective-permute-start | bytes 344072 | tf_op jit(solution)/shard_map/ppermute | solution.py:488
  42.3 3.8 %collective-permute-start.11 = (f32[8,16,128]{2,1,0:T(8,128)S(1)}, f32[8,16,128]{2,1,0:T(8,128)S(1)}, u32[]{:S(2)}, u32[]{:S(2)}) collective-permute-start(f32[8,16,128]{2,1,0:T(8,128)S(1)} %get-tuple-element.40.refs_0_), channel_id=1, source_target_pairs={{0,1},{1,0},{2,3},{3,2},{4,5},{5,4},{6,7},{7,6},{8,9},{9,8},{10,11... | collective-permute-start | bytes 196616 | tf_op jit(solution)/shard_map/ppermute | solution.py:488
  42.4 3.7 %collective-permute-start.10 = (f32[8,16,128]{2,1,0:T(8,128)S(1)}, f32[8,16,128]{2,1,0:T(8,128)S(1)}, u32[]{:S(2)}, u32[]{:S(2)}) collective-permute-start(f32[8,16,128]{2,1,0:T(8,128)S(1)} %get-tuple-element.40.refs_0_), channel_id=1, source_target_pairs={{0,32},{1,33},{2,34},{3,35},{4,36},{5,37},{6,38},{7,39},{8,40},{9,... | collective-permute-start | bytes 196616 | tf_op jit(solution)/shard_map/ppermute | solution.py:488
  46.2 6.8 %collective-permute-start.13 = (f32[24,8,128]{2,1,0:T(8,128)S(1)}, f32[24,8,128]{2,1,0:T(8,128)S(1)}, u32[]{:S(2)}, u32[]{:S(2)}) collective-permute-start(f32[24,8,128]{2,1,0:T(8,128)S(1)} %get-tuple-element.80), channel_id=1, source_target_pairs={{0,32},{32,0},{64,96},{96,64},{128,160},{160,128},{192,224},{224,1... | collective-permute-start | bytes 294920 | tf_op jit(solution)/shard_map/ppermute | solution.py:488
  48.6 4.6 %collective-permute-start.12 = (f32[24,8,128]{2,1,0:T(8,128)S(1)}, f32[24,8,128]{2,1,0:T(8,128)S(1)}, u32[]{:S(2)}, u32[]{:S(2)}) collective-permute-start(f32[24,8,128]{2,1,0:T(8,128)S(1)} %get-tuple-element.81), channel_id=1, source_target_pairs={{0,1},{32,33},{64,65},{96,97},{128,129},{160,161},{192,193},{224,2... | collective-permute-start | bytes 294920 | tf_op jit(solution)/shard_map/ppermute | solution.py:488
  57.0 3.8 %collective-permute-start.15 = (f32[3,8,128]{2,1,0:T(8,128)S(1)}, f32[3,8,128]{2,1,0:T(8,128)S(1)}, u32[]{:S(2)}, u32[]{:S(2)}) collective-permute-start(f32[3,8,128]{2,1,0:T(8,128)S(1)} %get-tuple-element.41), channel_id=1, source_target_pairs={{0,32},{1,33},{2,34},{3,35},{4,36},{5,37},{6,38},{7,39},{8,40},{9,... | collective-permute-start | bytes 36872 | tf_op jit(solution)/shard_map/ppermute | solution.py:488
  58.2 3.7 %collective-permute-start.14 = (f32[3,8,128]{2,1,0:T(8,128)S(1)}, f32[3,8,128]{2,1,0:T(8,128)S(1)}, u32[]{:S(2)}, u32[]{:S(2)}) collective-permute-start(f32[3,8,128]{2,1,0:T(8,128)S(1)} %get-tuple-element.41), channel_id=1, source_target_pairs={{0,64},{1,65},{2,66},{3,67},{4,68},{5,69},{6,70},{7,71},{8,72},{9,... | collective-permute-start | bytes 36872 | tf_op jit(solution)/shard_map/ppermute | solution.py:488
  61.9 8.9 %collective-permute-start.19 = (f32[3,24,128]{2,1,0:T(8,128)S(1)}, f32[3,24,128]{2,1,0:T(8,128)S(1)}, u32[]{:S(2)}, u32[]{:S(2)}) collective-permute-start(f32[3,24,128]{2,1,0:T(8,128)S(1)} %pad_maximum_fusion.10.refs_0_), channel_id=1, source_target_pairs={{0,3},{32,35},{64,67},{96,99},{128,131},{160,163},{192,195},{224,2... | collective-permute-start | bytes 110600 | tf_op jit(solution)/shard_map/ppermute | solution.py:488
  63.6 8.2 %collective-permute-start.18 = (f32[3,24,128]{2,1,0:T(8,128)S(1)}, f32[3,24,128]{2,1,0:T(8,128)S(1)}, u32[]{:S(2)}, u32[]{:S(2)}) collective-permute-start(f32[3,24,128]{2,1,0:T(8,128)S(1)} %pad_maximum_fusion.10.refs_0_), channel_id=1, source_target_pairs={{0,4},{32,36},{64,68},{96,100},{128,132},{160,164},{192,196},{224,... | collective-permute-start | bytes 110600 | tf_op jit(solution)/shard_map/ppermute | solution.py:488
  68.9 7.0 %collective-permute-start.17 = (f32[3,24,128]{2,1,0:T(8,128)S(1)}, f32[3,24,128]{2,1,0:T(8,128)S(1)}, u32[]{:S(2)}, u32[]{:S(2)}) collective-permute-start(f32[3,24,128]{2,1,0:T(8,128)S(1)} %pad_maximum_fusion.10.refs_0_), channel_id=1, source_target_pairs={{0,1},{32,33},{64,65},{96,97},{128,129},{160,161},{192,193},{224,2... | collective-permute-start | bytes 110600 | tf_op jit(solution)/shard_map/ppermute | solution.py:488
  68.9 7.0 %collective-permute-start.16 = (f32[3,24,128]{2,1,0:T(8,128)S(1)}, f32[3,24,128]{2,1,0:T(8,128)S(1)}, u32[]{:S(2)}, u32[]{:S(2)}) collective-permute-start(f32[3,24,128]{2,1,0:T(8,128)S(1)} %pad_maximum_fusion.10.refs_0_), channel_id=1, source_target_pairs={{0,2},{32,34},{64,66},{96,98},{128,130},{160,162},{192,194},{224,2... | collective-permute-start | bytes 110600 | tf_op jit(solution)/shard_map/ppermute | solution.py:488

commit v4 on v3

--- a/solution.py
+++ b/solution.py
@@ -8,7 +8,7 @@
 F32 = jnp.float32
 W = 24
 BF16 = jnp.bfloat16
-UNROLL = 2
+UNROLL = 4
 
 
 def iota(shape, dim):
@@ -96,7 +96,7 @@
 
     first = face(1, mob[0], mob[1])
     sx[1] = first
-    lax.fori_loop(1, level.total - 1, step, (mob[1], first), unroll=UNROLL)
+    lax.fori_loop(1, level.total - 1, step, (mob[1], first), unroll=UNROLL if level.planes < 128 else 2 * UNROLL)
 
 
 def walk(lo, hi, load, emit, sx, sy, sz):
@@ -109,7 +109,8 @@
         emit(i, c, total)
         return c, below, next_wx
 
-    lax.fori_loop(lo, hi, step, (load(lo - 1), load(lo), sx[lo]), unroll=UNROLL)
+    unroll = UNROLL if hi - lo == 38 else 2 * UNROLL
+    lax.fori_loop(lo, hi, step, (load(lo - 1), load(lo), sx[lo]), unroll=unroll)
 
 
 def sweep(lo, hi, load, store, rhs, sx, sy, sz, coef):
@@ -145,7 +146,7 @@
         out[k] = done[0] + done[1]
         return above, c, wx
 
-    lax.fori_loop(0, pairs, step, (v[lo - 1], v[lo], sx[lo]))
+    lax.fori_loop(0, pairs, step, (v[lo - 1], v[lo], sx[lo]), unroll=UNROLL)
 
 
 def pair_planes(lanes_in, offset=0, lanes_out=128):
@@ -457,7 +458,7 @@
 
 
 def is_odd(axis, step):
-    return (lax.axis_index(axis) // step) % 2 == 1
+    return (lax.axis_index(axis) & step) != 0
 
 
 def swap_partners(n, step, parity):
@@ -484,7 +485,12 @@
                 if axis == "py":
                     a, b = a[::-1], b[::-1]
                 pairs.append(tuple(p * lax.axis_size("py") + q for p, q in (a, b)))
-        out = to_next if to_prev is to_next else jnp.where(odd == (parity == 0), to_prev, to_next)
+        if to_prev is None:
+            out = to_next[parity]
+        elif to_prev is to_next:
+            out = to_next
+        else:
+            out = jnp.where(odd == (parity == 0), to_prev, to_next)
         got.append(lax.ppermute(out, ("px", "py"), pairs))
     return got
 
@@ -503,16 +509,18 @@
     flags = (
         is_odd("px", 1), is_odd("py", 1), is_odd("px", step_rows),
         x < step_rows, x >= npx - step_rows,
-    )
-    source, density, (odd_x, odd_y, odd_2, first_x, last_x) = lax.optimization_barrier(
+        ((1 - (x & 1)) * (lv0.rows - lv0.halo), (x & 1) * (lv0.rows - lv0.halo)),
+    )
+    source, density, (odd_x, odd_y, odd_2, first_x, last_x, starts) = lax.optimization_barrier(
         (source, density, flags)
     )
 
     h = lv0.halo
-    rows = exchange(
-        jnp.concatenate([source[:h], density[:h]], 0),
-        jnp.concatenate([source[-h:], density[-h:]], 0), odd_x, "px",
-    )
+    edge_rows = [
+        jnp.concatenate([lax.dynamic_slice_in_dim(a, at, h, 0) for a in (source, density)], 0)
+        for at in starts
+    ]
+    rows = exchange(None, edge_rows, odd_x, "px")
     lo, hi = pick(rows, odd_x)
     to_right = lambda s, d: jnp.concatenate([d[:, 12:16], s[:, 12:16]], 1)
     to_left = lambda s, d: jnp.concatenate([s[:, 0:4], d[:, 0:4]], 1)

time: 84.6 us -> 76.9 us (0.909)
  Pallas kernels: 24.3 us -> 16 us
    pallas_call x3, Pallas kernels: 15.7 us -> 9.72 us  [descend(): pl.pallas_call(lambda *refs: kernel(lv, *refs), out_shape=[jax.ShapeDtype...]
    pallas_call x1, Pallas kernels: 8.59 us -> 6.28 us  [per_device(): pl.pallas_call(lambda *refs: ascent_kernel((lv0, lv1, lv2), *refs), out_s...]
    dynamic_slice x0 -> x2, local copies, waits for them, and re-layouts: none -> 1.83 us  [per_device(): lax.dynamic_slice_in_dim(a, at, h, 0)]
    slice x2 -> x0, local copies, waits for them, and re-layouts: 1.82 us -> none  [the longest x1 0.94 us: per_device(): source[:h]]
  transfers between devices with their start and end apart: 20 -> 20, of which waited for: 12 -> 11; matrix products, arithmetic and copies ran while one was open for 0% -> 0% of each run, Pallas kernels for 0% -> 0%
where the time goes in v4:
time: 76.9 us; the launch traced here: 76.8 us
  waiting for transfers between devices  29.7 us (39%)
  starting transfers between devices  28.4 us (37%)
  Pallas kernels  16 us (21%)
  local copies, waits for them, and re-layouts  2.21 us (3%)
    ppermute x20, waiting for transfers between devices, exchange(): got.append(lax.ppermute(out, ('px', 'py'), pairs))  29.7 us
    ppermute x20, starting transfers between devices, exchange(): got.append(lax.ppermute(out, ('px', 'py'), pairs))  28.4 us
    pallas_call x3, Pallas kernels, descend(): pl.pallas_call(lambda *refs: kernel(lv, *refs), out_shape=[jax.ShapeDtype...  9.72 us
    pallas_call x1, Pallas kernels, per_device(): pl.pallas_call(lambda *refs: ascent_kernel((lv0, lv1, lv2), *refs), out_s...  6.28 us
    dynamic_slice x2, local copies, waits for them, and re-layouts, per_device(): lax.dynamic_slice_in_dim(a, at, h, 0)  1.83 us
  transfers between devices with their start and end apart: 20, of which 11 were waited for; matrix products, arithmetic and copies ran while one was open for 0% of the time, Pallas kernels for 0%

profile of v4, /device:TPU:10, one launch (start us, length us, event | category | flops | bytes accessed | tf_op | source)
XLA Modules:
  0.0 76.8 jit_solution(16100393238526324167)
XLA Ops:
  0.0 0.9 %constant_dynamic-slice_fusion.1 = (f32[4,16,256]{2,1,0:T(8,128)S(1)}, f32[4,16,256]{2,1,0:T(8,128)S(1)}) fusion(f32[32,16,256]{2,1,0:T(8,128)} %refs_0_, s32[]{:T(128)S(6)} %select_n.137, s32[]{:T(128)S(6)} %select_n.136), kind=kLoop, calls=%fused_computation.38 | loop fusion | bytes 262152 | tf_op jit(solution)/shard_map/dynamic_slice | solution.py:520
  3.1 5.9 %collective-permute-start.3 = (f32[32,8,256]{2,1,0:T(8,128)S(1)}, f32[32,8,256]{2,1,0:T(8,128)S(1)}, u32[]{:S(2)}, u32[]{:S(2)}) collective-permute-start(f32[32,8,256]{2,1,0:T(8,128)S(1)} %get-tuple-element.68), channel_id=1, source_target_pairs={{0,32},{32,0},{64,96},{96,64},{128,160},{160,128},{192,224},{224,1... | collective-permute-start | bytes 786440 | tf_op jit(solution)/shard_map/ppermute | solution.py:494
  9.1 2.1 %collective-permute-start.4 = (f32[8,8,256]{2,1,0:T(8,128)S(1)}, f32[8,8,256]{2,1,0:T(8,128)S(1)}, u32[]{:S(2)}, u32[]{:S(2)}) collective-permute-start(f32[8,8,256]{2,1,0:T(8,128)S(1)} %broadcast_select_fusion.7), channel_id=1, source_target_pairs={{0,1},{32,33},{64,65},{96,97},{128,129},{160,161},{192,193},{224,2... | collective-permute-start | bytes 196616 | tf_op jit(solution)/shard_map/ppermute | solution.py:494
  11.2 2.3 %collective-permute-start.5 = (f32[8,8,256]{2,1,0:T(8,128)S(1)}, f32[8,8,256]{2,1,0:T(8,128)S(1)}, u32[]{:S(2)}, u32[]{:S(2)}) collective-permute-start(f32[8,8,256]{2,1,0:T(8,128)S(1)} %get-tuple-element.65), channel_id=1, source_target_pairs={{0,32},{32,0},{64,96},{96,64},{128,160},{160,128},{192,224},{224,1... | collective-permute-start | bytes 196616 | tf_op jit(solution)/shard_map/ppermute | solution.py:494
  13.5 5.8 %collective-permute-done.4.refs_6_ = f32[8,8,256]{2,1,0:T(8,128)S(1)} collective-permute-done((f32[8,8,256]{2,1,0:T(8,128)S(1)}, f32[8,8,256]{2,1,0:T(8,128)S(1)}, u32[]{:S(2)}, u32[]{:S(2)}) %collective-permute-start.4) | collective-permute-done | bytes 65568 | tf_op jit(solution)/shard_map/ppermute | solution.py:494
  19.3 5.0 %descent.3 = (f32[16,24,128]{2,1,0:T(8,128)S(1)}, f32[40,24,256]{2,1,0:T(8,128)S(1)}, f32[40,24,256]{2,1,0:T(8,128)S(1)}, f32[40,24,256]{2,1,0:T(8,128)S(1)}, f3...) custom-call(f32[32,16,256]{2,1,0:T(8,128)S(1)} %copy-done, ...), custom_call_target="tpu_custom_call" | custom-call | tf_op jit(solution)/shard_map/descent/pallas_call | solution.py:448
  24.4 1.4 %collective-permute-start.6 = (f32[6,24,128]{2,1,0:T(8,128)S(1)}, f32[6,24,128]{2,1,0:T(8,128)S(1)}, u32[]{:S(2)}, u32[]{:S(2)}) collective-permute-start(f32[6,24,128]{2,1,0:T(8,128)S(1)} %get-tuple-element.87), channel_id=1, source_target_pairs={{0,32},{1,33},{2,34},{3,35},{4,36},{5,37},{6,38},{7,39},{8,40},{9,... | collective-permute-start | bytes 221192 | tf_op jit(solution)/shard_map/ppermute | solution.py:494
  25.8 2.4 %collective-permute-done.7.refs_2_ = f32[6,24,128]{2,1,0:T(8,128)S(1)} collective-permute-done((f32[6,24,128]{2,1,0:T(8,128)S(1)}, f32[6,24,128]{2,1,0:T(8,128)S(1)}, u32[]{:S(2)}, u32[]{:S(2)}) %collective-permute-start.7) | collective-permute-done | bytes 73760 | tf_op jit(solution)/shard_map/ppermute | solution.py:494
  28.2 2.5 %collective-permute-start.9 = (f32[28,8,128]{2,1,0:T(8,128)S(1)}, f32[28,8,128]{2,1,0:T(8,128)S(1)}, u32[]{:S(2)}, u32[]{:S(2)}) collective-permute-start(f32[28,8,128]{2,1,0:T(8,128)S(1)} %get-tuple-element.80), channel_id=1, source_target_pairs={{0,32},{32,0},{64,96},{96,64},{128,160},{160,128},{192,224},{224,1... | collective-permute-start | bytes 344072 | tf_op jit(solution)/shard_map/ppermute | solution.py:494
  30.7 4.9 %collective-permute-done.9.refs_4_ = f32[28,8,128]{2,1,0:T(8,128)S(1)} collective-permute-done((f32[28,8,128]{2,1,0:T(8,128)S(1)}, f32[28,8,128]{2,1,0:T(8,128)S(1)}, u32[]{:S(2)}, u32[]{:S(2)}) %collective-permute-start.9) | collective-permute-done | bytes 114720 | tf_op jit(solution)/shard_map/ppermute | solution.py:494
  35.6 2.2 %descent.4 = (f32[8,16,128]{2,1,0:T(8,128)S(1)}, f32[28,24,128]{2,1,0:T(8,128)S(1)}, f32[28,24,128]{2,1,0:T(8,128)S(1)}, f32[28,24,128]{2,1,0:T(8,128)S(1)}, f32...) custom-call(f32[16,24,128]{2,1,0:T(8,128)S(1)} %get-tuple-element.43.refs_0_, ...), custom_call_target="tpu_custom_call" | custom-call | tf_op jit(solution)/shard_map/descent/pallas_call | solution.py:448
  37.8 1.4 %collective-permute-start.10 = (f32[8,16,128]{2,1,0:T(8,128)S(1)}, f32[8,16,128]{2,1,0:T(8,128)S(1)}, u32[]{:S(2)}, u32[]{:S(2)}) collective-permute-start(f32[8,16,128]{2,1,0:T(8,128)S(1)} %get-tuple-element.44.refs_0_), channel_id=1, source_target_pairs={{0,32},{1,33},{2,34},{3,35},{4,36},{5,37},{6,38},{7,39},{8,40},{9,... | collective-permute-start | bytes 196616 | tf_op jit(solution)/shard_map/ppermute | solution.py:494
  39.2 2.3 %collective-permute-done.11.refs_2_ = f32[8,16,128]{2,1,0:T(8,128)S(1)} collective-permute-done((f32[8,16,128]{2,1,0:T(8,128)S(1)}, f32[8,16,128]{2,1,0:T(8,128)S(1)}, u32[]{:S(2)}, u32[]{:S(2)}) %collective-permute-start.11) | collective-permute-done | bytes 65568 | tf_op jit(solution)/shard_map/ppermute | solution.py:494
  41.6 2.5 %collective-permute-start.13 = (f32[24,8,128]{2,1,0:T(8,128)S(1)}, f32[24,8,128]{2,1,0:T(8,128)S(1)}, u32[]{:S(2)}, u32[]{:S(2)}) collective-permute-start(f32[24,8,128]{2,1,0:T(8,128)S(1)} %get-tuple-element.82), channel_id=1, source_target_pairs={{0,32},{32,0},{64,96},{96,64},{128,160},{160,128},{192,224},{224,1... | collective-permute-start | bytes 294920 | tf_op jit(solution)/shard_map/ppermute | solution.py:494
  44.1 4.4 %collective-permute-done.13.refs_4_ = f32[24,8,128]{2,1,0:T(8,128)S(1)} collective-permute-done((f32[24,8,128]{2,1,0:T(8,128)S(1)}, f32[24,8,128]{2,1,0:T(8,128)S(1)}, u32[]{:S(2)}, u32[]{:S(2)}) %collective-permute-start.13) | collective-permute-done | bytes 98336 | tf_op jit(solution)/shard_map/ppermute | solution.py:494
  48.7 2.6 %descent.5 = (f32[3,8,128]{2,1,0:T(8,128)S(1)}, f32[24,24,128]{2,1,0:T(8,128)S(1)}, f32[24,24,128]{2,1,0:T(8,128)S(1)}, f32[24,24,128]{2,1,0:T(8,128)S(1)}, f32[...) custom-call(f32[8,16,128]{2,1,0:T(8,128)S(1)} %get-tuple-element.44.refs_0_, ...), custom_call_target="tpu_custom_call" | custom-call | tf_op jit(solution)/shard_map/descent/pallas_call | solution.py:448
  51.3 1.4 %collective-permute-start.15 = (f32[3,8,128]{2,1,0:T(8,128)S(1)}, f32[3,8,128]{2,1,0:T(8,128)S(1)}, u32[]{:S(2)}, u32[]{:S(2)}) collective-permute-start(f32[3,8,128]{2,1,0:T(8,128)S(1)} %get-tuple-element.45), channel_id=1, source_target_pairs={{0,32},{1,33},{2,34},{3,35},{4,36},{5,37},{6,38},{7,39},{8,40},{9,... | collective-permute-start | bytes 36872 | tf_op jit(solution)/shard_map/ppermute | solution.py:494
  52.7 2.4 %collective-permute-done.15 = f32[3,8,128]{2,1,0:T(8,128)S(1)} collective-permute-done((f32[3,8,128]{2,1,0:T(8,128)S(1)}, f32[3,8,128]{2,1,0:T(8,128)S(1)}, u32[]{:S(2)}, u32[]{:S(2)}) %collective-permute-start.15) | collective-permute-done | bytes 12320 | tf_op jit(solution)/shard_map/ppermute | solution.py:494
  55.1 1.3 %collective-permute-done.14 = f32[3,8,128]{2,1,0:T(8,128)S(1)} collective-permute-done((f32[3,8,128]{2,1,0:T(8,128)S(1)}, f32[3,8,128]{2,1,0:T(8,128)S(1)}, u32[]{:S(2)}, u32[]{:S(2)}) %collective-permute-start.14) | collective-permute-done | bytes 12320 | tf_op jit(solution)/shard_map/ppermute | solution.py:494
  56.4 1.6 %collective-permute-start.19 = (f32[3,24,128]{2,1,0:T(8,128)S(1)}, f32[3,24,128]{2,1,0:T(8,128)S(1)}, u32[]{:S(2)}, u32[]{:S(2)}) collective-permute-start(f32[3,24,128]{2,1,0:T(8,128)S(1)} %pad_maximum_fusion.10.refs_0_), channel_id=1, source_target_pairs={{0,3},{32,35},{64,67},{96,99},{128,131},{160,163},{192,195},{224,2... | collective-permute-start | bytes 110600 | tf_op jit(solution)/shard_map/ppermute | solution.py:494
  57.9 5.6 %collective-permute-start.18 = (f32[3,24,128]{2,1,0:T(8,128)S(1)}, f32[3,24,128]{2,1,0:T(8,128)S(1)}, u32[]{:S(2)}, u32[]{:S(2)}) collective-permute-start(f32[3,24,128]{2,1,0:T(8,128)S(1)} %pad_maximum_fusion.10.refs_0_), channel_id=1, source_target_pairs={{0,4},{32,36},{64,68},{96,100},{128,132},{160,164},{192,196},{224,... | collective-permute-start | bytes 110600 | tf_op jit(solution)/shard_map/ppermute | solution.py:494
  64.4 1.0 %collective-permute-done.19.refs_4_ = f32[3,24,128]{2,1,0:T(8,128)S(1)} collective-permute-done((f32[3,24,128]{2,1,0:T(8,128)S(1)}, f32[3,24,128]{2,1,0:T(8,128)S(1)}, u32[]{:S(2)}, u32[]{:S(2)}) %collective-permute-start.19) | collective-permute-done | bytes 36896 | tf_op jit(solution)/shard_map/ppermute | solution.py:494
  66.1 4.4 %collective-permute-done.17.refs_2_ = f32[3,24,128]{2,1,0:T(8,128)S(1)} collective-permute-done((f32[3,24,128]{2,1,0:T(8,128)S(1)}, f32[3,24,128]{2,1,0:T(8,128)S(1)}, u32[]{:S(2)}, u32[]{:S(2)}) %collective-permute-start.17) | collective-permute-done | bytes 36896 | tf_op jit(solution)/shard_map/ppermute | solution.py:494
  70.5 6.3 %ascent.1 = f32[32,16,256]{2,1,0:T(8,128)} custom-call(f32[3,24,128]{2,1,0:T(8,128)S(1)} %pad_maximum_fusion.10.refs_0_, f32[3,24,128]{2,1,0:T(8,128)S(1)} %collective-permute-done.16.refs_1_, f32[3,24,128]{2,1,0:T(8,128)S(1)} %collective-permute-done.17.refs_2_, f32[3,24,128]{2,1,0:T(8,128)S(1)} %collective-permute-done.18.refs_3_, ...), custom_call_target="tpu_custom_call" | custom-call | tf_op jit(solution)/shard_map/ascent/pallas_call | solution.py:563
  (52 shorter events, 4.4 us)
Async XLA Ops:
  0.0 2.6 %copy-start = (f32[32,16,256]{2,1,0:T(8,128)S(1)}, f32[32,16,256]{2,1,0:T(8,128)}, u32[]{:S(2)}) copy-start(f32[32,16,256]{2,1,0:T(8,128)} %refs_0_) | copy-start | bytes 1572868
  1.8 1.0 %copy-start.1 = (f32[32,16,256]{2,1,0:T(8,128)S(1)}, f32[32,16,256]{2,1,0:T(8,128)}, u32[]{:S(2)}) copy-start(f32[32,16,256]{2,1,0:T(8,128)} %refs_1_) | copy-start | bytes 1572868
  1.9 7.1 %collective-permute-start = (f32[8,16,256]{2,1,0:T(8,128)S(1)}, f32[8,16,256]{2,1,0:T(8,128)S(1)}, u32[]{:S(2)}, u32[]{:S(2)}) collective-permute-start(f32[8,16,256]{2,1,0:T(8,128)S(1)} %pad_maximum_fusion.2), channel_id=1, source_target_pairs={{0,32},{1,33},{2,34},{3,35},{4,36},{5,37},{6,38},{7,39},{8,40},{9,... | collective-permute-start | bytes 393224 | tf_op jit(solution)/shard_map/ppermute | solution.py:494
  2.0 7.0 %collective-permute-start.1 = (f32[8,16,256]{2,1,0:T(8,128)S(1)}, f32[8,16,256]{2,1,0:T(8,128)S(1)}, u32[]{:S(2)}, u32[]{:S(2)}) collective-permute-start(f32[8,16,256]{2,1,0:T(8,128)S(1)} %pad_maximum_fusion.3), channel_id=1, source_target_pairs={{0,1},{1,0},{2,3},{3,2},{4,5},{5,4},{6,7},{7,6},{8,9},{9,8},{10,11... | collective-permute-start | bytes 393224 | tf_op jit(solution)/shard_map/ppermute | solution.py:494
  3.1 16.2 %collective-permute-start.3 = (f32[32,8,256]{2,1,0:T(8,128)S(1)}, f32[32,8,256]{2,1,0:T(8,128)S(1)}, u32[]{:S(2)}, u32[]{:S(2)}) collective-permute-start(f32[32,8,256]{2,1,0:T(8,128)S(1)} %get-tuple-element.68), channel_id=1, source_target_pairs={{0,32},{32,0},{64,96},{96,64},{128,160},{160,128},{192,224},{224,1... | collective-permute-start | bytes 786440 | tf_op jit(solution)/shard_map/ppermute | solution.py:494
  9.0 10.3 %collective-permute-start.2 = (f32[32,8,256]{2,1,0:T(8,128)S(1)}, f32[32,8,256]{2,1,0:T(8,128)S(1)}, u32[]{:S(2)}, u32[]{:S(2)}) collective-permute-start(f32[32,8,256]{2,1,0:T(8,128)S(1)} %get-tuple-element.69), channel_id=1, source_target_pairs={{0,1},{32,33},{64,65},{96,97},{128,129},{160,161},{192,193},{224,2... | collective-permute-start | bytes 786440 | tf_op jit(solution)/shard_map/ppermute | solution.py:494
  9.1 10.2 %collective-permute-start.4 = (f32[8,8,256]{2,1,0:T(8,128)S(1)}, f32[8,8,256]{2,1,0:T(8,128)S(1)}, u32[]{:S(2)}, u32[]{:S(2)}) collective-permute-start(f32[8,8,256]{2,1,0:T(8,128)S(1)} %broadcast_select_fusion.7), channel_id=1, source_target_pairs={{0,1},{32,33},{64,65},{96,97},{128,129},{160,161},{192,193},{224,2... | collective-permute-start | bytes 196616 | tf_op jit(solution)/shard_map/ppermute | solution.py:494
  11.2 8.1 %collective-permute-start.5 = (f32[8,8,256]{2,1,0:T(8,128)S(1)}, f32[8,8,256]{2,1,0:T(8,128)S(1)}, u32[]{:S(2)}, u32[]{:S(2)}) collective-permute-start(f32[8,8,256]{2,1,0:T(8,128)S(1)} %get-tuple-element.65), channel_id=1, source_target_pairs={{0,32},{32,0},{64,96},{96,64},{128,160},{160,128},{192,224},{224,1... | collective-permute-start | bytes 196616 | tf_op jit(solution)/shard_map/ppermute | solution.py:494
  24.3 3.9 %collective-permute-start.7 = (f32[6,24,128]{2,1,0:T(8,128)S(1)}, f32[6,24,128]{2,1,0:T(8,128)S(1)}, u32[]{:S(2)}, u32[]{:S(2)}) collective-permute-start(f32[6,24,128]{2,1,0:T(8,128)S(1)} %get-tuple-element.86), channel_id=1, source_target_pairs={{0,1},{1,0},{2,3},{3,2},{4,5},{5,4},{6,7},{7,6},{8,9},{9,8},{10,11... | collective-permute-start | bytes 221192 | tf_op jit(solution)/shard_map/ppermute | solution.py:494
  24.4 3.8 %collective-permute-start.6 = (f32[6,24,128]{2,1,0:T(8,128)S(1)}, f32[6,24,128]{2,1,0:T(8,128)S(1)}, u32[]{:S(2)}, u32[]{:S(2)}) collective-permute-start(f32[6,24,128]{2,1,0:T(8,128)S(1)} %get-tuple-element.87), channel_id=1, source_target_pairs={{0,32},{1,33},{2,34},{3,35},{4,36},{5,37},{6,38},{7,39},{8,40},{9,... | collective-permute-start | bytes 221192 | tf_op jit(solution)/shard_map/ppermute | solution.py:494
  28.2 7.4 %collective-permute-start.9 = (f32[28,8,128]{2,1,0:T(8,128)S(1)}, f32[28,8,128]{2,1,0:T(8,128)S(1)}, u32[]{:S(2)}, u32[]{:S(2)}) collective-permute-start(f32[28,8,128]{2,1,0:T(8,128)S(1)} %get-tuple-element.80), channel_id=1, source_target_pairs={{0,32},{32,0},{64,96},{96,64},{128,160},{160,128},{192,224},{224,1... | collective-permute-start | bytes 344072 | tf_op jit(solution)/shard_map/ppermute | solution.py:494
  30.7 4.9 %collective-permute-start.8 = (f32[28,8,128]{2,1,0:T(8,128)S(1)}, f32[28,8,128]{2,1,0:T(8,128)S(1)}, u32[]{:S(2)}, u32[]{:S(2)}) collective-permute-start(f32[28,8,128]{2,1,0:T(8,128)S(1)} %get-tuple-element.81), channel_id=1, source_target_pairs={{0,1},{32,33},{64,65},{96,97},{128,129},{160,161},{192,193},{224,2... | collective-permute-start | bytes 344072 | tf_op jit(solution)/shard_map/ppermute | solution.py:494
  37.7 3.8 %collective-permute-start.11 = (f32[8,16,128]{2,1,0:T(8,128)S(1)}, f32[8,16,128]{2,1,0:T(8,128)S(1)}, u32[]{:S(2)}, u32[]{:S(2)}) collective-permute-start(f32[8,16,128]{2,1,0:T(8,128)S(1)} %get-tuple-element.44.refs_0_), channel_id=1, source_target_pairs={{0,1},{1,0},{2,3},{3,2},{4,5},{5,4},{6,7},{7,6},{8,9},{9,8},{10,11... | collective-permute-start | bytes 196616 | tf_op jit(solution)/shard_map/ppermute | solution.py:494
  37.8 3.7 %collective-permute-start.10 = (f32[8,16,128]{2,1,0:T(8,128)S(1)}, f32[8,16,128]{2,1,0:T(8,128)S(1)}, u32[]{:S(2)}, u32[]{:S(2)}) collective-permute-start(f32[8,16,128]{2,1,0:T(8,128)S(1)} %get-tuple-element.44.refs_0_), channel_id=1, source_target_pairs={{0,32},{1,33},{2,34},{3,35},{4,36},{5,37},{6,38},{7,39},{8,40},{9,... | collective-permute-start | bytes 196616 | tf_op jit(solution)/shard_map/ppermute | solution.py:494
  41.6 6.8 %collective-permute-start.13 = (f32[24,8,128]{2,1,0:T(8,128)S(1)}, f32[24,8,128]{2,1,0:T(8,128)S(1)}, u32[]{:S(2)}, u32[]{:S(2)}) collective-permute-start(f32[24,8,128]{2,1,0:T(8,128)S(1)} %get-tuple-element.82), channel_id=1, source_target_pairs={{0,32},{32,0},{64,96},{96,64},{128,160},{160,128},{192,224},{224,1... | collective-permute-start | bytes 294920 | tf_op jit(solution)/shard_map/ppermute | solution.py:494
  44.1 4.6 %collective-permute-start.12 = (f32[24,8,128]{2,1,0:T(8,128)S(1)}, f32[24,8,128]{2,1,0:T(8,128)S(1)}, u32[]{:S(2)}, u32[]{:S(2)}) collective-permute-start(f32[24,8,128]{2,1,0:T(8,128)S(1)} %get-tuple-element.83), channel_id=1, source_target_pairs={{0,1},{32,33},{64,65},{96,97},{128,129},{160,161},{192,193},{224,2... | collective-permute-start | bytes 294920 | tf_op jit(solution)/shard_map/ppermute | solution.py:494
  51.3 3.8 %collective-permute-start.15 = (f32[3,8,128]{2,1,0:T(8,128)S(1)}, f32[3,8,128]{2,1,0:T(8,128)S(1)}, u32[]{:S(2)}, u32[]{:S(2)}) collective-permute-start(f32[3,8,128]{2,1,0:T(8,128)S(1)} %get-tuple-element.45), channel_id=1, source_target_pairs={{0,32},{1,33},{2,34},{3,35},{4,36},{5,37},{6,38},{7,39},{8,40},{9,... | collective-permute-start | bytes 36872 | tf_op jit(solution)/shard_map/ppermute | solution.py:494
  52.6 3.7 %collective-permute-start.14 = (f32[3,8,128]{2,1,0:T(8,128)S(1)}, f32[3,8,128]{2,1,0:T(8,128)S(1)}, u32[]{:S(2)}, u32[]{:S(2)}) collective-permute-start(f32[3,8,128]{2,1,0:T(8,128)S(1)} %get-tuple-element.45), channel_id=1, source_target_pairs={{0,64},{1,65},{2,66},{3,67},{4,68},{5,69},{6,70},{7,71},{8,72},{9,... | collective-permute-start | bytes 36872 | tf_op jit(solution)/shard_map/ppermute | solution.py:494
  56.4 9.1 %collective-permute-start.19 = (f32[3,24,128]{2,1,0:T(8,128)S(1)}, f32[3,24,128]{2,1,0:T(8,128)S(1)}, u32[]{:S(2)}, u32[]{:S(2)}) collective-permute-start(f32[3,24,128]{2,1,0:T(8,128)S(1)} %pad_maximum_fusion.10.refs_0_), channel_id=1, source_target_pairs={{0,3},{32,35},{64,67},{96,99},{128,131},{160,163},{192,195},{224,2... | collective-permute-start | bytes 110600 | tf_op jit(solution)/shard_map/ppermute | solution.py:494
  57.9 8.2 %collective-permute-start.18 = (f32[3,24,128]{2,1,0:T(8,128)S(1)}, f32[3,24,128]{2,1,0:T(8,128)S(1)}, u32[]{:S(2)}, u32[]{:S(2)}) collective-permute-start(f32[3,24,128]{2,1,0:T(8,128)S(1)} %pad_maximum_fusion.10.refs_0_), channel_id=1, source_target_pairs={{0,4},{32,36},{64,68},{96,100},{128,132},{160,164},{192,196},{224,... | collective-permute-start | bytes 110600 | tf_op jit(solution)/shard_map/ppermute | solution.py:494
  63.5 7.0 %collective-permute-start.17 = (f32[3,24,128]{2,1,0:T(8,128)S(1)}, f32[3,24,128]{2,1,0:T(8,128)S(1)}, u32[]{:S(2)}, u32[]{:S(2)}) collective-permute-start(f32[3,24,128]{2,1,0:T(8,128)S(1)} %pad_maximum_fusion.10.refs_0_), channel_id=1, source_target_pairs={{0,1},{32,33},{64,65},{96,97},{128,129},{160,161},{192,193},{224,2... | collective-permute-start | bytes 110600 | tf_op jit(solution)/shard_map/ppermute | solution.py:494
  63.5 7.0 %collective-permute-start.16 = (f32[3,24,128]{2,1,0:T(8,128)S(1)}, f32[3,24,128]{2,1,0:T(8,128)S(1)}, u32[]{:S(2)}, u32[]{:S(2)}) collective-permute-start(f32[3,24,128]{2,1,0:T(8,128)S(1)} %pad_maximum_fusion.10.refs_0_), channel_id=1, source_target_pairs={{0,2},{32,34},{64,66},{96,98},{128,130},{160,162},{192,194},{224,2... | collective-permute-start | bytes 110600 | tf_op jit(solution)/shard_map/ppermute | solution.py:494

commit v5 on v4

--- a/solution.py
+++ b/solution.py
@@ -96,7 +96,7 @@
 
     first = face(1, mob[0], mob[1])
     sx[1] = first
-    lax.fori_loop(1, level.total - 1, step, (mob[1], first), unroll=UNROLL if level.planes < 128 else 2 * UNROLL)
+    lax.fori_loop(1, level.total - 1, step, (mob[1], first), unroll=level.total - 2)
 
 
 def walk(lo, hi, load, emit, sx, sy, sz):
@@ -109,7 +109,7 @@
         emit(i, c, total)
         return c, below, next_wx
 
-    unroll = UNROLL if hi - lo == 38 else 2 * UNROLL
+    unroll = hi - lo
     lax.fori_loop(lo, hi, step, (load(lo - 1), load(lo), sx[lo]), unroll=unroll)
 
 
@@ -146,7 +146,7 @@
         out[k] = done[0] + done[1]
         return above, c, wx
 
-    lax.fori_loop(0, pairs, step, (v[lo - 1], v[lo], sx[lo]), unroll=UNROLL)
+    lax.fori_loop(0, pairs, step, (v[lo - 1], v[lo], sx[lo]), unroll=pairs)
 
 
 def pair_planes(lanes_in, offset=0, lanes_out=128):
@@ -192,7 +192,7 @@
         load(h + i, src[i], dens[i], right_side, left_side)
         return carry
 
-    lax.fori_loop(0, lv.rows, body, 0, unroll=UNROLL)
+    lax.fori_loop(0, lv.rows, body, 0, unroll=lv.rows)
     zero = jnp.zeros((W, lv.lanes), F32)
     for ref in (first, v):
         ref[0] = zero
@@ -210,7 +210,7 @@
         pair[k] = mob[h + 2 * k] + mob[h + 2 * k + 1]
         return carry
 
-    lax.fori_loop(0, half, mobs, 0, unroll=UNROLL)
+    lax.fori_loop(0, half, mobs, 0, unroll=8)
     low[...] = 0.125 * dot(pair[...].reshape(half * W, lv.lanes), z)
     at = iota((8, 128), 0)
     beside = jnp.zeros((4, 128), F32)
@@ -252,7 +252,7 @@
         load(h + i, own[i])
         return carry
 
-    lax.fori_loop(0, lv.rows, body, 0, unroll=UNROLL)
+    lax.fori_loop(0, lv.rows, body, 0, unroll=lv.rows)
     zero = jnp.zeros((W, lv.lanes), F32)
     for ref in (first, v):
         ref[0] = zero
@@ -267,7 +267,7 @@
         pair[k] = mob[h + 2 * k] + mob[h + 2 * k + 1]
         return carry
 
-    lax.fori_loop(0, half, mobs, 0)
+    lax.fori_loop(0, half, mobs, 0, unroll=8)
     low[...] = x + 0.125 * dot(pair[...].reshape(half * W, lv.lanes), pair_planes(lv.lanes, 64))
     for k in range(half):
         a = k * W

time: 76.9 us -> 71.4 us (0.928)
  Pallas kernels: 16 us -> 10.7 us
    pallas_call x3, Pallas kernels: 9.72 us -> 6.47 us  [descend(): pl.pallas_call(lambda *refs: kernel(lv, *refs), out_shape=[jax.ShapeDtype...]
    pallas_call x1, Pallas kernels: 6.28 us -> 4.2 us  [per_device(): pl.pallas_call(lambda *refs: ascent_kernel((lv0, lv1, lv2), *refs), out_s...]
where the time goes in v5:
time: 71.4 us; the launch traced here: 71.3 us
  waiting for transfers between devices  29.6 us (41%)
  starting transfers between devices  28.2 us (39%)
  Pallas kernels  10.7 us (15%)
  local copies, waits for them, and re-layouts  2.21 us (3%)
    ppermute x20, waiting for transfers between devices, exchange(): got.append(lax.ppermute(out, ('px', 'py'), pairs))  29.6 us
    ppermute x20, starting transfers between devices, exchange(): got.append(lax.ppermute(out, ('px', 'py'), pairs))  28.2 us
    pallas_call x3, Pallas kernels, descend(): pl.pallas_call(lambda *refs: kernel(lv, *refs), out_shape=[jax.ShapeDtype...  6.47 us
    pallas_call x1, Pallas kernels, per_device(): pl.pallas_call(lambda *refs: ascent_kernel((lv0, lv1, lv2), *refs), out_s...  4.2 us
    dynamic_slice x2, local copies, waits for them, and re-layouts, per_device(): lax.dynamic_slice_in_dim(a, at, h, 0)  1.83 us
  transfers between devices with their start and end apart: 20, of which 11 were waited for; matrix products, arithmetic and copies ran while one was open for 0% of the time, Pallas kernels for 0%

profile of v5, /device:TPU:10, one launch (start us, length us, event | category | flops | bytes accessed | tf_op | source)
XLA Modules:
  0.0 71.3 jit_solution(8102301982742473749)
XLA Ops:
  0.0 0.9 %constant_dynamic-slice_fusion.1 = (f32[4,16,256]{2,1,0:T(8,128)S(1)}, f32[4,16,256]{2,1,0:T(8,128)S(1)}) fusion(f32[32,16,256]{2,1,0:T(8,128)} %refs_0_, s32[]{:T(128)S(6)} %select_n.137, s32[]{:T(128)S(6)} %select_n.136), kind=kLoop, calls=%fused_computation.38 | loop fusion | bytes 262152 | tf_op jit(solution)/shard_map/dynamic_slice | solution.py:520
  3.1 5.9 %collective-permute-start.3 = (f32[32,8,256]{2,1,0:T(8,128)S(1)}, f32[32,8,256]{2,1,0:T(8,128)S(1)}, u32[]{:S(2)}, u32[]{:S(2)}) collective-permute-start(f32[32,8,256]{2,1,0:T(8,128)S(1)} %get-tuple-element.68), channel_id=1, source_target_pairs={{0,32},{32,0},{64,96},{96,64},{128,160},{160,128},{192,224},{224,1... | collective-permute-start | bytes 786440 | tf_op jit(solution)/shard_map/ppermute | solution.py:494
  9.1 2.1 %collective-permute-start.4 = (f32[8,8,256]{2,1,0:T(8,128)S(1)}, f32[8,8,256]{2,1,0:T(8,128)S(1)}, u32[]{:S(2)}, u32[]{:S(2)}) collective-permute-start(f32[8,8,256]{2,1,0:T(8,128)S(1)} %broadcast_select_fusion.7), channel_id=1, source_target_pairs={{0,1},{32,33},{64,65},{96,97},{128,129},{160,161},{192,193},{224,2... | collective-permute-start | bytes 196616 | tf_op jit(solution)/shard_map/ppermute | solution.py:494
  11.2 2.3 %collective-permute-start.5 = (f32[8,8,256]{2,1,0:T(8,128)S(1)}, f32[8,8,256]{2,1,0:T(8,128)S(1)}, u32[]{:S(2)}, u32[]{:S(2)}) collective-permute-start(f32[8,8,256]{2,1,0:T(8,128)S(1)} %get-tuple-element.65), channel_id=1, source_target_pairs={{0,32},{32,0},{64,96},{96,64},{128,160},{160,128},{192,224},{224,1... | collective-permute-start | bytes 196616 | tf_op jit(solution)/shard_map/ppermute | solution.py:494
  13.5 5.8 %collective-permute-done.4.refs_6_ = f32[8,8,256]{2,1,0:T(8,128)S(1)} collective-permute-done((f32[8,8,256]{2,1,0:T(8,128)S(1)}, f32[8,8,256]{2,1,0:T(8,128)S(1)}, u32[]{:S(2)}, u32[]{:S(2)}) %collective-permute-start.4) | collective-permute-done | bytes 65568 | tf_op jit(solution)/shard_map/ppermute | solution.py:494
  19.3 4.5 %descent.3 = (f32[16,24,128]{2,1,0:T(8,128)S(1)}, f32[40,24,256]{2,1,0:T(8,128)S(1)}, f32[40,24,256]{2,1,0:T(8,128)S(1)}, f32[40,24,256]{2,1,0:T(8,128)S(1)}, f3...) custom-call(f32[32,16,256]{2,1,0:T(8,128)S(1)} %copy-done, ...), custom_call_target="tpu_custom_call" | custom-call | tf_op jit(solution)/shard_map/descent/pallas_call | solution.py:448
  23.9 1.4 %collective-permute-start.6 = (f32[6,24,128]{2,1,0:T(8,128)S(1)}, f32[6,24,128]{2,1,0:T(8,128)S(1)}, u32[]{:S(2)}, u32[]{:S(2)}) collective-permute-start(f32[6,24,128]{2,1,0:T(8,128)S(1)} %get-tuple-element.87), channel_id=1, source_target_pairs={{0,32},{1,33},{2,34},{3,35},{4,36},{5,37},{6,38},{7,39},{8,40},{9,... | collective-permute-start | bytes 221192 | tf_op jit(solution)/shard_map/ppermute | solution.py:494
  25.3 2.4 %collective-permute-done.7.refs_2_ = f32[6,24,128]{2,1,0:T(8,128)S(1)} collective-permute-done((f32[6,24,128]{2,1,0:T(8,128)S(1)}, f32[6,24,128]{2,1,0:T(8,128)S(1)}, u32[]{:S(2)}, u32[]{:S(2)}) %collective-permute-start.7) | collective-permute-done | bytes 73760 | tf_op jit(solution)/shard_map/ppermute | solution.py:494
  27.7 2.5 %collective-permute-start.9 = (f32[28,8,128]{2,1,0:T(8,128)S(1)}, f32[28,8,128]{2,1,0:T(8,128)S(1)}, u32[]{:S(2)}, u32[]{:S(2)}) collective-permute-start(f32[28,8,128]{2,1,0:T(8,128)S(1)} %get-tuple-element.80), channel_id=1, source_target_pairs={{0,32},{32,0},{64,96},{96,64},{128,160},{160,128},{192,224},{224,1... | collective-permute-start | bytes 344072 | tf_op jit(solution)/shard_map/ppermute | solution.py:494
  30.2 4.9 %collective-permute-done.9.refs_4_ = f32[28,8,128]{2,1,0:T(8,128)S(1)} collective-permute-done((f32[28,8,128]{2,1,0:T(8,128)S(1)}, f32[28,8,128]{2,1,0:T(8,128)S(1)}, u32[]{:S(2)}, u32[]{:S(2)}) %collective-permute-start.9) | collective-permute-done | bytes 114720 | tf_op jit(solution)/shard_map/ppermute | solution.py:494
  35.1 1.0 %descent.4 = (f32[8,16,128]{2,1,0:T(8,128)S(1)}, f32[28,24,128]{2,1,0:T(8,128)S(1)}, f32[28,24,128]{2,1,0:T(8,128)S(1)}, f32[28,24,128]{2,1,0:T(8,128)S(1)}, f32...) custom-call(f32[16,24,128]{2,1,0:T(8,128)S(1)} %get-tuple-element.43.refs_0_, ...), custom_call_target="tpu_custom_call" | custom-call | tf_op jit(solution)/shard_map/descent/pallas_call | solution.py:448
  36.2 1.4 %collective-permute-start.10 = (f32[8,16,128]{2,1,0:T(8,128)S(1)}, f32[8,16,128]{2,1,0:T(8,128)S(1)}, u32[]{:S(2)}, u32[]{:S(2)}) collective-permute-start(f32[8,16,128]{2,1,0:T(8,128)S(1)} %get-tuple-element.44.refs_0_), channel_id=1, source_target_pairs={{0,32},{1,33},{2,34},{3,35},{4,36},{5,37},{6,38},{7,39},{8,40},{9,... | collective-permute-start | bytes 196616 | tf_op jit(solution)/shard_map/ppermute | solution.py:494
  37.5 2.3 %collective-permute-done.11.refs_2_ = f32[8,16,128]{2,1,0:T(8,128)S(1)} collective-permute-done((f32[8,16,128]{2,1,0:T(8,128)S(1)}, f32[8,16,128]{2,1,0:T(8,128)S(1)}, u32[]{:S(2)}, u32[]{:S(2)}) %collective-permute-start.11) | collective-permute-done | bytes 65568 | tf_op jit(solution)/shard_map/ppermute | solution.py:494
  39.9 2.5 %collective-permute-start.13 = (f32[24,8,128]{2,1,0:T(8,128)S(1)}, f32[24,8,128]{2,1,0:T(8,128)S(1)}, u32[]{:S(2)}, u32[]{:S(2)}) collective-permute-start(f32[24,8,128]{2,1,0:T(8,128)S(1)} %get-tuple-element.82), channel_id=1, source_target_pairs={{0,32},{32,0},{64,96},{96,64},{128,160},{160,128},{192,224},{224,1... | collective-permute-start | bytes 294920 | tf_op jit(solution)/shard_map/ppermute | solution.py:494
  42.4 4.3 %collective-permute-done.13.refs_4_ = f32[24,8,128]{2,1,0:T(8,128)S(1)} collective-permute-done((f32[24,8,128]{2,1,0:T(8,128)S(1)}, f32[24,8,128]{2,1,0:T(8,128)S(1)}, u32[]{:S(2)}, u32[]{:S(2)}) %collective-permute-start.13) | collective-permute-done | bytes 98336 | tf_op jit(solution)/shard_map/ppermute | solution.py:494
  47.0 1.0 %descent.5 = (f32[3,8,128]{2,1,0:T(8,128)S(1)}, f32[24,24,128]{2,1,0:T(8,128)S(1)}, f32[24,24,128]{2,1,0:T(8,128)S(1)}, f32[24,24,128]{2,1,0:T(8,128)S(1)}, f32[...) custom-call(f32[8,16,128]{2,1,0:T(8,128)S(1)} %get-tuple-element.44.refs_0_, ...), custom_call_target="tpu_custom_call" | custom-call | tf_op jit(solution)/shard_map/descent/pallas_call | solution.py:448
  48.0 1.3 %collective-permute-start.15 = (f32[3,8,128]{2,1,0:T(8,128)S(1)}, f32[3,8,128]{2,1,0:T(8,128)S(1)}, u32[]{:S(2)}, u32[]{:S(2)}) collective-permute-start(f32[3,8,128]{2,1,0:T(8,128)S(1)} %get-tuple-element.45), channel_id=1, source_target_pairs={{0,32},{1,33},{2,34},{3,35},{4,36},{5,37},{6,38},{7,39},{8,40},{9,... | collective-permute-start | bytes 36872 | tf_op jit(solution)/shard_map/ppermute | solution.py:494
  49.5 2.4 %collective-permute-done.15 = f32[3,8,128]{2,1,0:T(8,128)S(1)} collective-permute-done((f32[3,8,128]{2,1,0:T(8,128)S(1)}, f32[3,8,128]{2,1,0:T(8,128)S(1)}, u32[]{:S(2)}, u32[]{:S(2)}) %collective-permute-start.15) | collective-permute-done | bytes 12320 | tf_op jit(solution)/shard_map/ppermute | solution.py:494
  51.8 1.3 %collective-permute-done.14 = f32[3,8,128]{2,1,0:T(8,128)S(1)} collective-permute-done((f32[3,8,128]{2,1,0:T(8,128)S(1)}, f32[3,8,128]{2,1,0:T(8,128)S(1)}, u32[]{:S(2)}, u32[]{:S(2)}) %collective-permute-start.14) | collective-permute-done | bytes 12320 | tf_op jit(solution)/shard_map/ppermute | solution.py:494
  53.1 1.4 %collective-permute-start.19 = (f32[3,24,128]{2,1,0:T(8,128)S(1)}, f32[3,24,128]{2,1,0:T(8,128)S(1)}, u32[]{:S(2)}, u32[]{:S(2)}) collective-permute-start(f32[3,24,128]{2,1,0:T(8,128)S(1)} %pad_maximum_fusion.10.refs_0_), channel_id=1, source_target_pairs={{0,3},{32,35},{64,67},{96,99},{128,131},{160,163},{192,195},{224,2... | collective-permute-start | bytes 110600 | tf_op jit(solution)/shard_map/ppermute | solution.py:494
  54.5 5.6 %collective-permute-start.18 = (f32[3,24,128]{2,1,0:T(8,128)S(1)}, f32[3,24,128]{2,1,0:T(8,128)S(1)}, u32[]{:S(2)}, u32[]{:S(2)}) collective-permute-start(f32[3,24,128]{2,1,0:T(8,128)S(1)} %pad_maximum_fusion.10.refs_0_), channel_id=1, source_target_pairs={{0,4},{32,36},{64,68},{96,100},{128,132},{160,164},{192,196},{224,... | collective-permute-start | bytes 110600 | tf_op jit(solution)/shard_map/ppermute | solution.py:494
  61.0 1.0 %collective-permute-done.19.refs_4_ = f32[3,24,128]{2,1,0:T(8,128)S(1)} collective-permute-done((f32[3,24,128]{2,1,0:T(8,128)S(1)}, f32[3,24,128]{2,1,0:T(8,128)S(1)}, u32[]{:S(2)}, u32[]{:S(2)}) %collective-permute-start.19) | collective-permute-done | bytes 36896 | tf_op jit(solution)/shard_map/ppermute | solution.py:494
  62.7 4.4 %collective-permute-done.17.refs_2_ = f32[3,24,128]{2,1,0:T(8,128)S(1)} collective-permute-done((f32[3,24,128]{2,1,0:T(8,128)S(1)}, f32[3,24,128]{2,1,0:T(8,128)S(1)}, u32[]{:S(2)}, u32[]{:S(2)}) %collective-permute-start.17) | collective-permute-done | bytes 36896 | tf_op jit(solution)/shard_map/ppermute | solution.py:494
  67.1 4.2 %ascent.1 = f32[32,16,256]{2,1,0:T(8,128)} custom-call(f32[3,24,128]{2,1,0:T(8,128)S(1)} %pad_maximum_fusion.10.refs_0_, f32[3,24,128]{2,1,0:T(8,128)S(1)} %collective-permute-done.16.refs_1_, f32[3,24,128]{2,1,0:T(8,128)S(1)} %collective-permute-done.17.refs_2_, f32[3,24,128]{2,1,0:T(8,128)S(1)} %collective-permute-done.18.refs_3_, ...), custom_call_target="tpu_custom_call" | custom-call | tf_op jit(solution)/shard_map/ascent/pallas_call | solution.py:563
  (52 shorter events, 4.4 us)
Async XLA Ops:
  0.0 2.6 %copy-start = (f32[32,16,256]{2,1,0:T(8,128)S(1)}, f32[32,16,256]{2,1,0:T(8,128)}, u32[]{:S(2)}) copy-start(f32[32,16,256]{2,1,0:T(8,128)} %refs_0_) | copy-start | bytes 1572868
  1.8 1.0 %copy-start.1 = (f32[32,16,256]{2,1,0:T(8,128)S(1)}, f32[32,16,256]{2,1,0:T(8,128)}, u32[]{:S(2)}) copy-start(f32[32,16,256]{2,1,0:T(8,128)} %refs_1_) | copy-start | bytes 1572868
  1.9 7.1 %collective-permute-start = (f32[8,16,256]{2,1,0:T(8,128)S(1)}, f32[8,16,256]{2,1,0:T(8,128)S(1)}, u32[]{:S(2)}, u32[]{:S(2)}) collective-permute-start(f32[8,16,256]{2,1,0:T(8,128)S(1)} %pad_maximum_fusion.2), channel_id=1, source_target_pairs={{0,32},{1,33},{2,34},{3,35},{4,36},{5,37},{6,38},{7,39},{8,40},{9,... | collective-permute-start | bytes 393224 | tf_op jit(solution)/shard_map/ppermute | solution.py:494
  2.0 7.0 %collective-permute-start.1 = (f32[8,16,256]{2,1,0:T(8,128)S(1)}, f32[8,16,256]{2,1,0:T(8,128)S(1)}, u32[]{:S(2)}, u32[]{:S(2)}) collective-permute-start(f32[8,16,256]{2,1,0:T(8,128)S(1)} %pad_maximum_fusion.3), channel_id=1, source_target_pairs={{0,1},{1,0},{2,3},{3,2},{4,5},{5,4},{6,7},{7,6},{8,9},{9,8},{10,11... | collective-permute-start | bytes 393224 | tf_op jit(solution)/shard_map/ppermute | solution.py:494
  3.1 16.2 %collective-permute-start.3 = (f32[32,8,256]{2,1,0:T(8,128)S(1)}, f32[32,8,256]{2,1,0:T(8,128)S(1)}, u32[]{:S(2)}, u32[]{:S(2)}) collective-permute-start(f32[32,8,256]{2,1,0:T(8,128)S(1)} %get-tuple-element.68), channel_id=1, source_target_pairs={{0,32},{32,0},{64,96},{96,64},{128,160},{160,128},{192,224},{224,1... | collective-permute-start | bytes 786440 | tf_op jit(solution)/shard_map/ppermute | solution.py:494
  9.0 10.3 %collective-permute-start.2 = (f32[32,8,256]{2,1,0:T(8,128)S(1)}, f32[32,8,256]{2,1,0:T(8,128)S(1)}, u32[]{:S(2)}, u32[]{:S(2)}) collective-permute-start(f32[32,8,256]{2,1,0:T(8,128)S(1)} %get-tuple-element.69), channel_id=1, source_target_pairs={{0,1},{32,33},{64,65},{96,97},{128,129},{160,161},{192,193},{224,2... | collective-permute-start | bytes 786440 | tf_op jit(solution)/shard_map/ppermute | solution.py:494
  9.1 10.2 %collective-permute-start.4 = (f32[8,8,256]{2,1,0:T(8,128)S(1)}, f32[8,8,256]{2,1,0:T(8,128)S(1)}, u32[]{:S(2)}, u32[]{:S(2)}) collective-permute-start(f32[8,8,256]{2,1,0:T(8,128)S(1)} %broadcast_select_fusion.7), channel_id=1, source_target_pairs={{0,1},{32,33},{64,65},{96,97},{128,129},{160,161},{192,193},{224,2... | collective-permute-start | bytes 196616 | tf_op jit(solution)/shard_map/ppermute | solution.py:494
  11.2 8.1 %collective-permute-start.5 = (f32[8,8,256]{2,1,0:T(8,128)S(1)}, f32[8,8,256]{2,1,0:T(8,128)S(1)}, u32[]{:S(2)}, u32[]{:S(2)}) collective-permute-start(f32[8,8,256]{2,1,0:T(8,128)S(1)} %get-tuple-element.65), channel_id=1, source_target_pairs={{0,32},{32,0},{64,96},{96,64},{128,160},{160,128},{192,224},{224,1... | collective-permute-start | bytes 196616 | tf_op jit(solution)/shard_map/ppermute | solution.py:494
  23.8 3.9 %collective-permute-start.7 = (f32[6,24,128]{2,1,0:T(8,128)S(1)}, f32[6,24,128]{2,1,0:T(8,128)S(1)}, u32[]{:S(2)}, u32[]{:S(2)}) collective-permute-start(f32[6,24,128]{2,1,0:T(8,128)S(1)} %get-tuple-element.86), channel_id=1, source_target_pairs={{0,1},{1,0},{2,3},{3,2},{4,5},{5,4},{6,7},{7,6},{8,9},{9,8},{10,11... | collective-permute-start | bytes 221192 | tf_op jit(solution)/shard_map/ppermute | solution.py:494
  23.9 3.8 %collective-permute-start.6 = (f32[6,24,128]{2,1,0:T(8,128)S(1)}, f32[6,24,128]{2,1,0:T(8,128)S(1)}, u32[]{:S(2)}, u32[]{:S(2)}) collective-permute-start(f32[6,24,128]{2,1,0:T(8,128)S(1)} %get-tuple-element.87), channel_id=1, source_target_pairs={{0,32},{1,33},{2,34},{3,35},{4,36},{5,37},{6,38},{7,39},{8,40},{9,... | collective-permute-start | bytes 221192 | tf_op jit(solution)/shard_map/ppermute | solution.py:494
  27.7 7.4 %collective-permute-start.9 = (f32[28,8,128]{2,1,0:T(8,128)S(1)}, f32[28,8,128]{2,1,0:T(8,128)S(1)}, u32[]{:S(2)}, u32[]{:S(2)}) collective-permute-start(f32[28,8,128]{2,1,0:T(8,128)S(1)} %get-tuple-element.80), channel_id=1, source_target_pairs={{0,32},{32,0},{64,96},{96,64},{128,160},{160,128},{192,224},{224,1... | collective-permute-start | bytes 344072 | tf_op jit(solution)/shard_map/ppermute | solution.py:494
  30.2 4.9 %collective-permute-start.8 = (f32[28,8,128]{2,1,0:T(8,128)S(1)}, f32[28,8,128]{2,1,0:T(8,128)S(1)}, u32[]{:S(2)}, u32[]{:S(2)}) collective-permute-start(f32[28,8,128]{2,1,0:T(8,128)S(1)} %get-tuple-element.81), channel_id=1, source_target_pairs={{0,1},{32,33},{64,65},{96,97},{128,129},{160,161},{192,193},{224,2... | collective-permute-start | bytes 344072 | tf_op jit(solution)/shard_map/ppermute | solution.py:494
  36.1 3.8 %collective-permute-start.11 = (f32[8,16,128]{2,1,0:T(8,128)S(1)}, f32[8,16,128]{2,1,0:T(8,128)S(1)}, u32[]{:S(2)}, u32[]{:S(2)}) collective-permute-start(f32[8,16,128]{2,1,0:T(8,128)S(1)} %get-tuple-element.44.refs_0_), channel_id=1, source_target_pairs={{0,1},{1,0},{2,3},{3,2},{4,5},{5,4},{6,7},{7,6},{8,9},{9,8},{10,11... | collective-permute-start | bytes 196616 | tf_op jit(solution)/shard_map/ppermute | solution.py:494
  36.2 3.7 %collective-permute-start.10 = (f32[8,16,128]{2,1,0:T(8,128)S(1)}, f32[8,16,128]{2,1,0:T(8,128)S(1)}, u32[]{:S(2)}, u32[]{:S(2)}) collective-permute-start(f32[8,16,128]{2,1,0:T(8,128)S(1)} %get-tuple-element.44.refs_0_), channel_id=1, source_target_pairs={{0,32},{1,33},{2,34},{3,35},{4,36},{5,37},{6,38},{7,39},{8,40},{9,... | collective-permute-start | bytes 196616 | tf_op jit(solution)/shard_map/ppermute | solution.py:494
  39.9 6.8 %collective-permute-start.13 = (f32[24,8,128]{2,1,0:T(8,128)S(1)}, f32[24,8,128]{2,1,0:T(8,128)S(1)}, u32[]{:S(2)}, u32[]{:S(2)}) collective-permute-start(f32[24,8,128]{2,1,0:T(8,128)S(1)} %get-tuple-element.82), channel_id=1, source_target_pairs={{0,32},{32,0},{64,96},{96,64},{128,160},{160,128},{192,224},{224,1... | collective-permute-start | bytes 294920 | tf_op jit(solution)/shard_map/ppermute | solution.py:494
  42.4 4.6 %collective-permute-start.12 = (f32[24,8,128]{2,1,0:T(8,128)S(1)}, f32[24,8,128]{2,1,0:T(8,128)S(1)}, u32[]{:S(2)}, u32[]{:S(2)}) collective-permute-start(f32[24,8,128]{2,1,0:T(8,128)S(1)} %get-tuple-element.83), channel_id=1, source_target_pairs={{0,1},{32,33},{64,65},{96,97},{128,129},{160,161},{192,193},{224,2... | collective-permute-start | bytes 294920 | tf_op jit(solution)/shard_map/ppermute | solution.py:494
  48.0 3.8 %collective-permute-start.15 = (f32[3,8,128]{2,1,0:T(8,128)S(1)}, f32[3,8,128]{2,1,0:T(8,128)S(1)}, u32[]{:S(2)}, u32[]{:S(2)}) collective-permute-start(f32[3,8,128]{2,1,0:T(8,128)S(1)} %get-tuple-element.45), channel_id=1, source_target_pairs={{0,32},{1,33},{2,34},{3,35},{4,36},{5,37},{6,38},{7,39},{8,40},{9,... | collective-permute-start | bytes 36872 | tf_op jit(solution)/shard_map/ppermute | solution.py:494
  49.4 3.7 %collective-permute-start.14 = (f32[3,8,128]{2,1,0:T(8,128)S(1)}, f32[3,8,128]{2,1,0:T(8,128)S(1)}, u32[]{:S(2)}, u32[]{:S(2)}) collective-permute-start(f32[3,8,128]{2,1,0:T(8,128)S(1)} %get-tuple-element.45), channel_id=1, source_target_pairs={{0,64},{1,65},{2,66},{3,67},{4,68},{5,69},{6,70},{7,71},{8,72},{9,... | collective-permute-start | bytes 36872 | tf_op jit(solution)/shard_map/ppermute | solution.py:494
  53.1 8.9 %collective-permute-start.19 = (f32[3,24,128]{2,1,0:T(8,128)S(1)}, f32[3,24,128]{2,1,0:T(8,128)S(1)}, u32[]{:S(2)}, u32[]{:S(2)}) collective-permute-start(f32[3,24,128]{2,1,0:T(8,128)S(1)} %pad_maximum_fusion.10.refs_0_), channel_id=1, source_target_pairs={{0,3},{32,35},{64,67},{96,99},{128,131},{160,163},{192,195},{224,2... | collective-permute-start | bytes 110600 | tf_op jit(solution)/shard_map/ppermute | solution.py:494
  54.5 8.2 %collective-permute-start.18 = (f32[3,24,128]{2,1,0:T(8,128)S(1)}, f32[3,24,128]{2,1,0:T(8,128)S(1)}, u32[]{:S(2)}, u32[]{:S(2)}) collective-permute-start(f32[3,24,128]{2,1,0:T(8,128)S(1)} %pad_maximum_fusion.10.refs_0_), channel_id=1, source_target_pairs={{0,4},{32,36},{64,68},{96,100},{128,132},{160,164},{192,196},{224,... | collective-permute-start | bytes 110600 | tf_op jit(solution)/shard_map/ppermute | solution.py:494
  60.1 7.0 %collective-permute-start.17 = (f32[3,24,128]{2,1,0:T(8,128)S(1)}, f32[3,24,128]{2,1,0:T(8,128)S(1)}, u32[]{:S(2)}, u32[]{:S(2)}) collective-permute-start(f32[3,24,128]{2,1,0:T(8,128)S(1)} %pad_maximum_fusion.10.refs_0_), channel_id=1, source_target_pairs={{0,1},{32,33},{64,65},{96,97},{128,129},{160,161},{192,193},{224,2... | collective-permute-start | bytes 110600 | tf_op jit(solution)/shard_map/ppermute | solution.py:494
  60.1 7.0 %collective-permute-start.16 = (f32[3,24,128]{2,1,0:T(8,128)S(1)}, f32[3,24,128]{2,1,0:T(8,128)S(1)}, u32[]{:S(2)}, u32[]{:S(2)}) collective-permute-start(f32[3,24,128]{2,1,0:T(8,128)S(1)} %pad_maximum_fusion.10.refs_0_), channel_id=1, source_target_pairs={{0,2},{32,34},{64,66},{96,98},{128,130},{160,162},{192,194},{224,2... | collective-permute-start | bytes 110600 | tf_op jit(solution)/shard_map/ppermute | solution.py:494

commit v6 on v5

--- a/solution.py
+++ b/solution.py
@@ -210,7 +210,7 @@
         pair[k] = mob[h + 2 * k] + mob[h + 2 * k + 1]
         return carry
 
-    lax.fori_loop(0, half, mobs, 0, unroll=8)
+    lax.fori_loop(0, half, mobs, 0, unroll=half)
     low[...] = 0.125 * dot(pair[...].reshape(half * W, lv.lanes), z)
     at = iota((8, 128), 0)
     beside = jnp.zeros((4, 128), F32)
@@ -267,7 +267,7 @@
         pair[k] = mob[h + 2 * k] + mob[h + 2 * k + 1]
         return carry
 
-    lax.fori_loop(0, half, mobs, 0, unroll=8)
+    lax.fori_loop(0, half, mobs, 0, unroll=half)
     low[...] = x + 0.125 * dot(pair[...].reshape(half * W, lv.lanes), pair_planes(lv.lanes, 64))
     for k in range(half):
         a = k * W

time: 71.4 us -> 71.2 us (level)
  no operation moved by 1% of the time
where the time goes in v6:
time: 71.2 us; the launch traced here: 71 us
  waiting for transfers between devices  29.6 us (42%)
  starting transfers between devices  28.2 us (40%)
  Pallas kernels  10.4 us (15%)
  local copies, waits for them, and re-layouts  2.21 us (3%)
    ppermute x20, waiting for transfers between devices, exchange(): got.append(lax.ppermute(out, ('px', 'py'), pairs))  29.6 us
    ppermute x20, starting transfers between devices, exchange(): got.append(lax.ppermute(out, ('px', 'py'), pairs))  28.2 us
    pallas_call x3, Pallas kernels, descend(): pl.pallas_call(lambda *refs: kernel(lv, *refs), out_shape=[jax.ShapeDtype...  6.19 us
    pallas_call x1, Pallas kernels, per_device(): pl.pallas_call(lambda *refs: ascent_kernel((lv0, lv1, lv2), *refs), out_s...  4.2 us
    dynamic_slice x2, local copies, waits for them, and re-layouts, per_device(): lax.dynamic_slice_in_dim(a, at, h, 0)  1.83 us
  transfers between devices with their start and end apart: 20, of which 11 were waited for; matrix products, arithmetic and copies ran while one was open for 0% of the time, Pallas kernels for 0%

profile of v6, /device:TPU:10, one launch (start us, length us, event | category | flops | bytes accessed | tf_op | source)
XLA Modules:
  0.0 71.0 jit_solution(15765376032259037453)
XLA Ops:
  0.0 0.9 %constant_dynamic-slice_fusion.1 = (f32[4,16,256]{2,1,0:T(8,128)S(1)}, f32[4,16,256]{2,1,0:T(8,128)S(1)}) fusion(f32[32,16,256]{2,1,0:T(8,128)} %refs_0_, s32[]{:T(128)S(6)} %select_n.137, s32[]{:T(128)S(6)} %select_n.136), kind=kLoop, calls=%fused_computation.38 | loop fusion | bytes 262152 | tf_op jit(solution)/shard_map/dynamic_slice | solution.py:520
  3.1 5.9 %collective-permute-start.3 = (f32[32,8,256]{2,1,0:T(8,128)S(1)}, f32[32,8,256]{2,1,0:T(8,128)S(1)}, u32[]{:S(2)}, u32[]{:S(2)}) collective-permute-start(f32[32,8,256]{2,1,0:T(8,128)S(1)} %get-tuple-element.68), channel_id=1, source_target_pairs={{0,32},{32,0},{64,96},{96,64},{128,160},{160,128},{192,224},{224,1... | collective-permute-start | bytes 786440 | tf_op jit(solution)/shard_map/ppermute | solution.py:494
  9.1 2.1 %collective-permute-start.4 = (f32[8,8,256]{2,1,0:T(8,128)S(1)}, f32[8,8,256]{2,1,0:T(8,128)S(1)}, u32[]{:S(2)}, u32[]{:S(2)}) collective-permute-start(f32[8,8,256]{2,1,0:T(8,128)S(1)} %broadcast_select_fusion.7), channel_id=1, source_target_pairs={{0,1},{32,33},{64,65},{96,97},{128,129},{160,161},{192,193},{224,2... | collective-permute-start | bytes 196616 | tf_op jit(solution)/shard_map/ppermute | solution.py:494
  11.2 2.3 %collective-permute-start.5 = (f32[8,8,256]{2,1,0:T(8,128)S(1)}, f32[8,8,256]{2,1,0:T(8,128)S(1)}, u32[]{:S(2)}, u32[]{:S(2)}) collective-permute-start(f32[8,8,256]{2,1,0:T(8,128)S(1)} %get-tuple-element.65), channel_id=1, source_target_pairs={{0,32},{32,0},{64,96},{96,64},{128,160},{160,128},{192,224},{224,1... | collective-permute-start | bytes 196616 | tf_op jit(solution)/shard_map/ppermute | solution.py:494
  13.5 5.8 %collective-permute-done.4.refs_6_ = f32[8,8,256]{2,1,0:T(8,128)S(1)} collective-permute-done((f32[8,8,256]{2,1,0:T(8,128)S(1)}, f32[8,8,256]{2,1,0:T(8,128)S(1)}, u32[]{:S(2)}, u32[]{:S(2)}) %collective-permute-start.4) | collective-permute-done | bytes 65568 | tf_op jit(solution)/shard_map/ppermute | solution.py:494
  19.3 4.2 %descent.3 = (f32[16,24,128]{2,1,0:T(8,128)S(1)}, f32[40,24,256]{2,1,0:T(8,128)S(1)}, f32[40,24,256]{2,1,0:T(8,128)S(1)}, f32[40,24,256]{2,1,0:T(8,128)S(1)}, f3...) custom-call(f32[32,16,256]{2,1,0:T(8,128)S(1)} %copy-done, ...), custom_call_target="tpu_custom_call" | custom-call | tf_op jit(solution)/shard_map/descent/pallas_call | solution.py:448
  23.6 1.4 %collective-permute-start.6 = (f32[6,24,128]{2,1,0:T(8,128)S(1)}, f32[6,24,128]{2,1,0:T(8,128)S(1)}, u32[]{:S(2)}, u32[]{:S(2)}) collective-permute-start(f32[6,24,128]{2,1,0:T(8,128)S(1)} %get-tuple-element.87), channel_id=1, source_target_pairs={{0,32},{1,33},{2,34},{3,35},{4,36},{5,37},{6,38},{7,39},{8,40},{9,... | collective-permute-start | bytes 221192 | tf_op jit(solution)/shard_map/ppermute | solution.py:494
  25.0 2.4 %collective-permute-done.7.refs_2_ = f32[6,24,128]{2,1,0:T(8,128)S(1)} collective-permute-done((f32[6,24,128]{2,1,0:T(8,128)S(1)}, f32[6,24,128]{2,1,0:T(8,128)S(1)}, u32[]{:S(2)}, u32[]{:S(2)}) %collective-permute-start.7) | collective-permute-done | bytes 73760 | tf_op jit(solution)/shard_map/ppermute | solution.py:494
  27.4 2.5 %collective-permute-start.9 = (f32[28,8,128]{2,1,0:T(8,128)S(1)}, f32[28,8,128]{2,1,0:T(8,128)S(1)}, u32[]{:S(2)}, u32[]{:S(2)}) collective-permute-start(f32[28,8,128]{2,1,0:T(8,128)S(1)} %get-tuple-element.80), channel_id=1, source_target_pairs={{0,32},{32,0},{64,96},{96,64},{128,160},{160,128},{192,224},{224,1... | collective-permute-start | bytes 344072 | tf_op jit(solution)/shard_map/ppermute | solution.py:494
  29.9 4.9 %collective-permute-done.9.refs_4_ = f32[28,8,128]{2,1,0:T(8,128)S(1)} collective-permute-done((f32[28,8,128]{2,1,0:T(8,128)S(1)}, f32[28,8,128]{2,1,0:T(8,128)S(1)}, u32[]{:S(2)}, u32[]{:S(2)}) %collective-permute-start.9) | collective-permute-done | bytes 114720 | tf_op jit(solution)/shard_map/ppermute | solution.py:494
  34.8 1.0 %descent.4 = (f32[8,16,128]{2,1,0:T(8,128)S(1)}, f32[28,24,128]{2,1,0:T(8,128)S(1)}, f32[28,24,128]{2,1,0:T(8,128)S(1)}, f32[28,24,128]{2,1,0:T(8,128)S(1)}, f32...) custom-call(f32[16,24,128]{2,1,0:T(8,128)S(1)} %get-tuple-element.43.refs_0_, ...), custom_call_target="tpu_custom_call" | custom-call | tf_op jit(solution)/shard_map/descent/pallas_call | solution.py:448
  35.9 1.4 %collective-permute-start.10 = (f32[8,16,128]{2,1,0:T(8,128)S(1)}, f32[8,16,128]{2,1,0:T(8,128)S(1)}, u32[]{:S(2)}, u32[]{:S(2)}) collective-permute-start(f32[8,16,128]{2,1,0:T(8,128)S(1)} %get-tuple-element.44.refs_0_), channel_id=1, source_target_pairs={{0,32},{1,33},{2,34},{3,35},{4,36},{5,37},{6,38},{7,39},{8,40},{9,... | collective-permute-start | bytes 196616 | tf_op jit(solution)/shard_map/ppermute | solution.py:494
  37.3 2.3 %collective-permute-done.11.refs_2_ = f32[8,16,128]{2,1,0:T(8,128)S(1)} collective-permute-done((f32[8,16,128]{2,1,0:T(8,128)S(1)}, f32[8,16,128]{2,1,0:T(8,128)S(1)}, u32[]{:S(2)}, u32[]{:S(2)}) %collective-permute-start.11) | collective-permute-done | bytes 65568 | tf_op jit(solution)/shard_map/ppermute | solution.py:494
  39.7 2.5 %collective-permute-start.13 = (f32[24,8,128]{2,1,0:T(8,128)S(1)}, f32[24,8,128]{2,1,0:T(8,128)S(1)}, u32[]{:S(2)}, u32[]{:S(2)}) collective-permute-start(f32[24,8,128]{2,1,0:T(8,128)S(1)} %get-tuple-element.82), channel_id=1, source_target_pairs={{0,32},{32,0},{64,96},{96,64},{128,160},{160,128},{192,224},{224,1... | collective-permute-start | bytes 294920 | tf_op jit(solution)/shard_map/ppermute | solution.py:494
  42.1 4.3 %collective-permute-done.13.refs_4_ = f32[24,8,128]{2,1,0:T(8,128)S(1)} collective-permute-done((f32[24,8,128]{2,1,0:T(8,128)S(1)}, f32[24,8,128]{2,1,0:T(8,128)S(1)}, u32[]{:S(2)}, u32[]{:S(2)}) %collective-permute-start.13) | collective-permute-done | bytes 98336 | tf_op jit(solution)/shard_map/ppermute | solution.py:494
  46.8 1.0 %descent.5 = (f32[3,8,128]{2,1,0:T(8,128)S(1)}, f32[24,24,128]{2,1,0:T(8,128)S(1)}, f32[24,24,128]{2,1,0:T(8,128)S(1)}, f32[24,24,128]{2,1,0:T(8,128)S(1)}, f32[...) custom-call(f32[8,16,128]{2,1,0:T(8,128)S(1)} %get-tuple-element.44.refs_0_, ...), custom_call_target="tpu_custom_call" | custom-call | tf_op jit(solution)/shard_map/descent/pallas_call | solution.py:448
  47.8 1.3 %collective-permute-start.15 = (f32[3,8,128]{2,1,0:T(8,128)S(1)}, f32[3,8,128]{2,1,0:T(8,128)S(1)}, u32[]{:S(2)}, u32[]{:S(2)}) collective-permute-start(f32[3,8,128]{2,1,0:T(8,128)S(1)} %get-tuple-element.45), channel_id=1, source_target_pairs={{0,32},{1,33},{2,34},{3,35},{4,36},{5,37},{6,38},{7,39},{8,40},{9,... | collective-permute-start | bytes 36872 | tf_op jit(solution)/shard_map/ppermute | solution.py:494
  49.2 2.4 %collective-permute-done.15 = f32[3,8,128]{2,1,0:T(8,128)S(1)} collective-permute-done((f32[3,8,128]{2,1,0:T(8,128)S(1)}, f32[3,8,128]{2,1,0:T(8,128)S(1)}, u32[]{:S(2)}, u32[]{:S(2)}) %collective-permute-start.15) | collective-permute-done | bytes 12320 | tf_op jit(solution)/shard_map/ppermute | solution.py:494
  51.5 1.3 %collective-permute-done.14 = f32[3,8,128]{2,1,0:T(8,128)S(1)} collective-permute-done((f32[3,8,128]{2,1,0:T(8,128)S(1)}, f32[3,8,128]{2,1,0:T(8,128)S(1)}, u32[]{:S(2)}, u32[]{:S(2)}) %collective-permute-start.14) | collective-permute-done | bytes 12320 | tf_op jit(solution)/shard_map/ppermute | solution.py:494
  52.9 1.4 %collective-permute-start.19 = (f32[3,24,128]{2,1,0:T(8,128)S(1)}, f32[3,24,128]{2,1,0:T(8,128)S(1)}, u32[]{:S(2)}, u32[]{:S(2)}) collective-permute-start(f32[3,24,128]{2,1,0:T(8,128)S(1)} %pad_maximum_fusion.10.refs_0_), channel_id=1, source_target_pairs={{0,3},{32,35},{64,67},{96,99},{128,131},{160,163},{192,195},{224,2... | collective-permute-start | bytes 110600 | tf_op jit(solution)/shard_map/ppermute | solution.py:494
  54.2 5.6 %collective-permute-start.18 = (f32[3,24,128]{2,1,0:T(8,128)S(1)}, f32[3,24,128]{2,1,0:T(8,128)S(1)}, u32[]{:S(2)}, u32[]{:S(2)}) collective-permute-start(f32[3,24,128]{2,1,0:T(8,128)S(1)} %pad_maximum_fusion.10.refs_0_), channel_id=1, source_target_pairs={{0,4},{32,36},{64,68},{96,100},{128,132},{160,164},{192,196},{224,... | collective-permute-start | bytes 110600 | tf_op jit(solution)/shard_map/ppermute | solution.py:494
  60.7 1.0 %collective-permute-done.19.refs_4_ = f32[3,24,128]{2,1,0:T(8,128)S(1)} collective-permute-done((f32[3,24,128]{2,1,0:T(8,128)S(1)}, f32[3,24,128]{2,1,0:T(8,128)S(1)}, u32[]{:S(2)}, u32[]{:S(2)}) %collective-permute-start.19) | collective-permute-done | bytes 36896 | tf_op jit(solution)/shard_map/ppermute | solution.py:494
  62.4 4.4 %collective-permute-done.17.refs_2_ = f32[3,24,128]{2,1,0:T(8,128)S(1)} collective-permute-done((f32[3,24,128]{2,1,0:T(8,128)S(1)}, f32[3,24,128]{2,1,0:T(8,128)S(1)}, u32[]{:S(2)}, u32[]{:S(2)}) %collective-permute-start.17) | collective-permute-done | bytes 36896 | tf_op jit(solution)/shard_map/ppermute | solution.py:494
  66.8 4.2 %ascent.1 = f32[32,16,256]{2,1,0:T(8,128)} custom-call(f32[3,24,128]{2,1,0:T(8,128)S(1)} %pad_maximum_fusion.10.refs_0_, f32[3,24,128]{2,1,0:T(8,128)S(1)} %collective-permute-done.16.refs_1_, f32[3,24,128]{2,1,0:T(8,128)S(1)} %collective-permute-done.17.refs_2_, f32[3,24,128]{2,1,0:T(8,128)S(1)} %collective-permute-done.18.refs_3_, ...), custom_call_target="tpu_custom_call" | custom-call | tf_op jit(solution)/shard_map/ascent/pallas_call | solution.py:563
  (52 shorter events, 4.4 us)
Async XLA Ops:
  0.0 2.6 %copy-start = (f32[32,16,256]{2,1,0:T(8,128)S(1)}, f32[32,16,256]{2,1,0:T(8,128)}, u32[]{:S(2)}) copy-start(f32[32,16,256]{2,1,0:T(8,128)} %refs_0_) | copy-start | bytes 1572868
  1.8 1.0 %copy-start.1 = (f32[32,16,256]{2,1,0:T(8,128)S(1)}, f32[32,16,256]{2,1,0:T(8,128)}, u32[]{:S(2)}) copy-start(f32[32,16,256]{2,1,0:T(8,128)} %refs_1_) | copy-start | bytes 1572868
  1.9 7.1 %collective-permute-start = (f32[8,16,256]{2,1,0:T(8,128)S(1)}, f32[8,16,256]{2,1,0:T(8,128)S(1)}, u32[]{:S(2)}, u32[]{:S(2)}) collective-permute-start(f32[8,16,256]{2,1,0:T(8,128)S(1)} %pad_maximum_fusion.2), channel_id=1, source_target_pairs={{0,32},{1,33},{2,34},{3,35},{4,36},{5,37},{6,38},{7,39},{8,40},{9,... | collective-permute-start | bytes 393224 | tf_op jit(solution)/shard_map/ppermute | solution.py:494
  2.0 7.0 %collective-permute-start.1 = (f32[8,16,256]{2,1,0:T(8,128)S(1)}, f32[8,16,256]{2,1,0:T(8,128)S(1)}, u32[]{:S(2)}, u32[]{:S(2)}) collective-permute-start(f32[8,16,256]{2,1,0:T(8,128)S(1)} %pad_maximum_fusion.3), channel_id=1, source_target_pairs={{0,1},{1,0},{2,3},{3,2},{4,5},{5,4},{6,7},{7,6},{8,9},{9,8},{10,11... | collective-permute-start | bytes 393224 | tf_op jit(solution)/shard_map/ppermute | solution.py:494
  3.1 16.2 %collective-permute-start.3 = (f32[32,8,256]{2,1,0:T(8,128)S(1)}, f32[32,8,256]{2,1,0:T(8,128)S(1)}, u32[]{:S(2)}, u32[]{:S(2)}) collective-permute-start(f32[32,8,256]{2,1,0:T(8,128)S(1)} %get-tuple-element.68), channel_id=1, source_target_pairs={{0,32},{32,0},{64,96},{96,64},{128,160},{160,128},{192,224},{224,1... | collective-permute-start | bytes 786440 | tf_op jit(solution)/shard_map/ppermute | solution.py:494
  9.0 10.3 %collective-permute-start.2 = (f32[32,8,256]{2,1,0:T(8,128)S(1)}, f32[32,8,256]{2,1,0:T(8,128)S(1)}, u32[]{:S(2)}, u32[]{:S(2)}) collective-permute-start(f32[32,8,256]{2,1,0:T(8,128)S(1)} %get-tuple-element.69), channel_id=1, source_target_pairs={{0,1},{32,33},{64,65},{96,97},{128,129},{160,161},{192,193},{224,2... | collective-permute-start | bytes 786440 | tf_op jit(solution)/shard_map/ppermute | solution.py:494
  9.1 10.2 %collective-permute-start.4 = (f32[8,8,256]{2,1,0:T(8,128)S(1)}, f32[8,8,256]{2,1,0:T(8,128)S(1)}, u32[]{:S(2)}, u32[]{:S(2)}) collective-permute-start(f32[8,8,256]{2,1,0:T(8,128)S(1)} %broadcast_select_fusion.7), channel_id=1, source_target_pairs={{0,1},{32,33},{64,65},{96,97},{128,129},{160,161},{192,193},{224,2... | collective-permute-start | bytes 196616 | tf_op jit(solution)/shard_map/ppermute | solution.py:494
  11.2 8.1 %collective-permute-start.5 = (f32[8,8,256]{2,1,0:T(8,128)S(1)}, f32[8,8,256]{2,1,0:T(8,128)S(1)}, u32[]{:S(2)}, u32[]{:S(2)}) collective-permute-start(f32[8,8,256]{2,1,0:T(8,128)S(1)} %get-tuple-element.65), channel_id=1, source_target_pairs={{0,32},{32,0},{64,96},{96,64},{128,160},{160,128},{192,224},{224,1... | collective-permute-start | bytes 196616 | tf_op jit(solution)/shard_map/ppermute | solution.py:494
  23.5 3.9 %collective-permute-start.7 = (f32[6,24,128]{2,1,0:T(8,128)S(1)}, f32[6,24,128]{2,1,0:T(8,128)S(1)}, u32[]{:S(2)}, u32[]{:S(2)}) collective-permute-start(f32[6,24,128]{2,1,0:T(8,128)S(1)} %get-tuple-element.86), channel_id=1, source_target_pairs={{0,1},{1,0},{2,3},{3,2},{4,5},{5,4},{6,7},{7,6},{8,9},{9,8},{10,11... | collective-permute-start | bytes 221192 | tf_op jit(solution)/shard_map/ppermute | solution.py:494
  23.6 3.8 %collective-permute-start.6 = (f32[6,24,128]{2,1,0:T(8,128)S(1)}, f32[6,24,128]{2,1,0:T(8,128)S(1)}, u32[]{:S(2)}, u32[]{:S(2)}) collective-permute-start(f32[6,24,128]{2,1,0:T(8,128)S(1)} %get-tuple-element.87), channel_id=1, source_target_pairs={{0,32},{1,33},{2,34},{3,35},{4,36},{5,37},{6,38},{7,39},{8,40},{9,... | collective-permute-start | bytes 221192 | tf_op jit(solution)/shard_map/ppermute | solution.py:494
  27.4 7.4 %collective-permute-start.9 = (f32[28,8,128]{2,1,0:T(8,128)S(1)}, f32[28,8,128]{2,1,0:T(8,128)S(1)}, u32[]{:S(2)}, u32[]{:S(2)}) collective-permute-start(f32[28,8,128]{2,1,0:T(8,128)S(1)} %get-tuple-element.80), channel_id=1, source_target_pairs={{0,32},{32,0},{64,96},{96,64},{128,160},{160,128},{192,224},{224,1... | collective-permute-start | bytes 344072 | tf_op jit(solution)/shard_map/ppermute | solution.py:494
  29.9 4.9 %collective-permute-start.8 = (f32[28,8,128]{2,1,0:T(8,128)S(1)}, f32[28,8,128]{2,1,0:T(8,128)S(1)}, u32[]{:S(2)}, u32[]{:S(2)}) collective-permute-start(f32[28,8,128]{2,1,0:T(8,128)S(1)} %get-tuple-element.81), channel_id=1, source_target_pairs={{0,1},{32,33},{64,65},{96,97},{128,129},{160,161},{192,193},{224,2... | collective-permute-start | bytes 344072 | tf_op jit(solution)/shard_map/ppermute | solution.py:494
  35.8 3.8 %collective-permute-start.11 = (f32[8,16,128]{2,1,0:T(8,128)S(1)}, f32[8,16,128]{2,1,0:T(8,128)S(1)}, u32[]{:S(2)}, u32[]{:S(2)}) collective-permute-start(f32[8,16,128]{2,1,0:T(8,128)S(1)} %get-tuple-element.44.refs_0_), channel_id=1, source_target_pairs={{0,1},{1,0},{2,3},{3,2},{4,5},{5,4},{6,7},{7,6},{8,9},{9,8},{10,11... | collective-permute-start | bytes 196616 | tf_op jit(solution)/shard_map/ppermute | solution.py:494
  35.9 3.7 %collective-permute-start.10 = (f32[8,16,128]{2,1,0:T(8,128)S(1)}, f32[8,16,128]{2,1,0:T(8,128)S(1)}, u32[]{:S(2)}, u32[]{:S(2)}) collective-permute-start(f32[8,16,128]{2,1,0:T(8,128)S(1)} %get-tuple-element.44.refs_0_), channel_id=1, source_target_pairs={{0,32},{1,33},{2,34},{3,35},{4,36},{5,37},{6,38},{7,39},{8,40},{9,... | collective-permute-start | bytes 196616 | tf_op jit(solution)/shard_map/ppermute | solution.py:494
  39.7 6.8 %collective-permute-start.13 = (f32[24,8,128]{2,1,0:T(8,128)S(1)}, f32[24,8,128]{2,1,0:T(8,128)S(1)}, u32[]{:S(2)}, u32[]{:S(2)}) collective-permute-start(f32[24,8,128]{2,1,0:T(8,128)S(1)} %get-tuple-element.82), channel_id=1, source_target_pairs={{0,32},{32,0},{64,96},{96,64},{128,160},{160,128},{192,224},{224,1... | collective-permute-start | bytes 294920 | tf_op jit(solution)/shard_map/ppermute | solution.py:494
  42.1 4.6 %collective-permute-start.12 = (f32[24,8,128]{2,1,0:T(8,128)S(1)}, f32[24,8,128]{2,1,0:T(8,128)S(1)}, u32[]{:S(2)}, u32[]{:S(2)}) collective-permute-start(f32[24,8,128]{2,1,0:T(8,128)S(1)} %get-tuple-element.83), channel_id=1, source_target_pairs={{0,1},{32,33},{64,65},{96,97},{128,129},{160,161},{192,193},{224,2... | collective-permute-start | bytes 294920 | tf_op jit(solution)/shard_map/ppermute | solution.py:494
  47.8 3.8 %collective-permute-start.15 = (f32[3,8,128]{2,1,0:T(8,128)S(1)}, f32[3,8,128]{2,1,0:T(8,128)S(1)}, u32[]{:S(2)}, u32[]{:S(2)}) collective-permute-start(f32[3,8,128]{2,1,0:T(8,128)S(1)} %get-tuple-element.45), channel_id=1, source_target_pairs={{0,32},{1,33},{2,34},{3,35},{4,36},{5,37},{6,38},{7,39},{8,40},{9,... | collective-permute-start | bytes 36872 | tf_op jit(solution)/shard_map/ppermute | solution.py:494
  49.1 3.7 %collective-permute-start.14 = (f32[3,8,128]{2,1,0:T(8,128)S(1)}, f32[3,8,128]{2,1,0:T(8,128)S(1)}, u32[]{:S(2)}, u32[]{:S(2)}) collective-permute-start(f32[3,8,128]{2,1,0:T(8,128)S(1)} %get-tuple-element.45), channel_id=1, source_target_pairs={{0,64},{1,65},{2,66},{3,67},{4,68},{5,69},{6,70},{7,71},{8,72},{9,... | collective-permute-start | bytes 36872 | tf_op jit(solution)/shard_map/ppermute | solution.py:494
  52.9 8.9 %collective-permute-start.19 = (f32[3,24,128]{2,1,0:T(8,128)S(1)}, f32[3,24,128]{2,1,0:T(8,128)S(1)}, u32[]{:S(2)}, u32[]{:S(2)}) collective-permute-start(f32[3,24,128]{2,1,0:T(8,128)S(1)} %pad_maximum_fusion.10.refs_0_), channel_id=1, source_target_pairs={{0,3},{32,35},{64,67},{96,99},{128,131},{160,163},{192,195},{224,2... | collective-permute-start | bytes 110600 | tf_op jit(solution)/shard_map/ppermute | solution.py:494
  54.2 8.2 %collective-permute-start.18 = (f32[3,24,128]{2,1,0:T(8,128)S(1)}, f32[3,24,128]{2,1,0:T(8,128)S(1)}, u32[]{:S(2)}, u32[]{:S(2)}) collective-permute-start(f32[3,24,128]{2,1,0:T(8,128)S(1)} %pad_maximum_fusion.10.refs_0_), channel_id=1, source_target_pairs={{0,4},{32,36},{64,68},{96,100},{128,132},{160,164},{192,196},{224,... | collective-permute-start | bytes 110600 | tf_op jit(solution)/shard_map/ppermute | solution.py:494
  59.8 7.0 %collective-permute-start.17 = (f32[3,24,128]{2,1,0:T(8,128)S(1)}, f32[3,24,128]{2,1,0:T(8,128)S(1)}, u32[]{:S(2)}, u32[]{:S(2)}) collective-permute-start(f32[3,24,128]{2,1,0:T(8,128)S(1)} %pad_maximum_fusion.10.refs_0_), channel_id=1, source_target_pairs={{0,1},{32,33},{64,65},{96,97},{128,129},{160,161},{192,193},{224,2... | collective-permute-start | bytes 110600 | tf_op jit(solution)/shard_map/ppermute | solution.py:494
  59.8 7.0 %collective-permute-start.16 = (f32[3,24,128]{2,1,0:T(8,128)S(1)}, f32[3,24,128]{2,1,0:T(8,128)S(1)}, u32[]{:S(2)}, u32[]{:S(2)}) collective-permute-start(f32[3,24,128]{2,1,0:T(8,128)S(1)} %pad_maximum_fusion.10.refs_0_), channel_id=1, source_target_pairs={{0,2},{32,34},{64,66},{96,98},{128,130},{160,162},{192,194},{224,2... | collective-permute-start | bytes 110600 | tf_op jit(solution)/shard_map/ppermute | solution.py:494
